TPU v7x, 32 devices: a whole 2x2x4 slice. The times are simulated.
32 devices in a mesh: pipe: 4 (over z), dp: 4 (over x, core), expert: 2 (over y).
Axes of the slice: x: 2, y: 2, z: 4, core: 2. Of those that a mesh axis runs over, the one named last changes fastest.
Arguments:
- block_input: bfloat16 [4, 1024, 3072], P('pipe', ('dp', 'expert')), may hold values from -6 to 6
- output_grad: bfloat16 [4, 1024, 3072], P('pipe', ('dp', 'expert')), may hold values from -6 to 6
- expert_ids: int32 [4, 1024, 6], P('pipe', ('dp', 'expert')), may hold values from 0 to 159, all different within a row
- gate_weights: float32 [4, 1024, 6], P('pipe', ('dp', 'expert')), may hold values from 0.25 to 2
- gate_proj: bfloat16 [4, 2, 3072, 1024], P('pipe', 'expert', None, 'dp'), may hold values from -0.109375 to 0.109375
- up_proj: bfloat16 [4, 2, 3072, 1024], P('pipe', 'expert', None, 'dp'), may hold values from -0.109375 to 0.109375
- down_proj: bfloat16 [4, 2, 1024, 3072], P('pipe', 'expert', 'dp'), may hold values from -0.1875 to 0.1875
Outputs:
- received_grad: bfloat16 [4, 1024, 3072], P('pipe', ('dp', 'expert'))
- gate_weight_grad: float32 [4, 1024, 6], P('pipe', ('dp', 'expert'))
- gate_proj_grad: bfloat16 [4, 2, 3072, 1024], P('pipe', 'expert', None, 'dp')
- up_proj_grad: bfloat16 [4, 2, 3072, 1024], P('pipe', 'expert', None, 'dp')
- down_proj_grad: bfloat16 [4, 2, 1024, 3072], P('pipe', 'expert', 'dp')
Inputs may be any that keep to these rules, and one draw needn't show every extreme that they name: `expert_ids`: each token names 6 different experts.
All inputs are finite; a program needn't handle non-finite values.
Results may differ from a plain program's by a relative error of at most 0.006.
Values may be sent and summed in bfloat16 or wider, within the bound.
No kernel may reach another device: no remote copies, remote signals or barrier semaphores. Data moves between devices by JAX's collectives and lax.ppermute only.
A program may use at most 128 MiB of HBM per device.

v0:
```python
import jax
import jax.numpy as jnp
from jax import lax
from jax.sharding import PartitionSpec as P


def shifted(value, axis, steps):
    count = lax.axis_size(axis)
    pairs = [(source, (source + steps) % count) for source in range(count)]
    return lax.ppermute(value, axis, pairs)


def slot_tables(chosen_ids, experts, capacity):
    tok_count, chosen = chosen_ids.shape
    flat_ids = chosen_ids.reshape(-1)
    columns = jnp.arange(experts, dtype=jnp.int32)
    onehot = (flat_ids[:, None] == columns[None, :]).astype(jnp.int32)
    earlier = jnp.cumsum(onehot, axis=0) - onehot
    slot_rank = jnp.sum(earlier * onehot, axis=1)
    kept_pair = (flat_ids < experts) & (slot_rank < capacity)
    slot_index = jnp.where(kept_pair, flat_ids * capacity + slot_rank, experts * capacity)
    slot_rows = jnp.arange(experts * capacity, dtype=jnp.int32)
    placed = slot_index[None, :] == slot_rows[:, None]
    pair_index = jnp.arange(tok_count * chosen, dtype=jnp.int32)
    source_pair = jnp.sum(jnp.where(placed, pair_index[None, :], 0), axis=1)
    filled = jnp.any(placed, axis=1)
    return (slot_index, source_pair, filled)


def shards(block_input, output_grad, expert_ids, gate_weights, gate_proj, up_proj, down_proj):
    acts_local = block_input[0]
    grad_local = output_grad[0]
    chosen_ids = expert_ids[0]
    route_weight = gate_weights[0]
    tok_count, chosen = chosen_ids.shape
    width = acts_local.shape[1]
    local_count = gate_proj.shape[1]
    dp_count = lax.axis_size("dp")
    expert_count = lax.axis_size("expert")
    experts = local_count * expert_count
    capacity = tok_count // 16
    slot_index, source_pair, filled = slot_tables(chosen_ids, experts, capacity)
    source_token = source_pair // chosen
    slot_weight = route_weight.reshape(-1)[source_pair]
    send_acts = jnp.where(filled[:, None], acts_local[source_token], jnp.zeros((), jnp.bfloat16))
    scaled = slot_weight[:, None] * grad_local[source_token].astype(jnp.float32)
    send_grad = jnp.where(filled[:, None], scaled, 0.0).astype(jnp.bfloat16)
    send_acts = send_acts.reshape(experts, capacity, width)
    send_grad = send_grad.reshape(experts, capacity, width)
    acts_copies = jnp.broadcast_to(send_acts[None], (dp_count,) + send_acts.shape).reshape(
        dp_count * experts, capacity, width
    )
    grad_copies = jnp.broadcast_to(send_grad[None], (dp_count,) + send_grad.shape).reshape(
        dp_count * experts, capacity, width
    )
    recv_acts, recv_grad = (
        lax.all_to_all(acts_copies, ("dp", "expert"), split_axis=0, concat_axis=1, tiled=True),
        lax.all_to_all(grad_copies, ("dp", "expert"), split_axis=0, concat_axis=1, tiled=True),
    )
    gate_local = gate_proj[0]
    upper_local = up_proj[0]
    lower_local = down_proj[0]
    gate_pre = jnp.einsum("erd,edh->erh", recv_acts, gate_local, preferred_element_type=jnp.float32)
    up_value = jnp.einsum(
        "erd,edh->erh", recv_acts, upper_local, preferred_element_type=jnp.float32
    )
    grad_hidden = jnp.einsum(
        "erd,ehd->erh", recv_grad, lower_local, preferred_element_type=jnp.float32
    )
    sigma_gate = jax.nn.sigmoid(gate_pre)
    swish = gate_pre * sigma_gate
    hidden = swish * up_value
    scores = jnp.sum(hidden * grad_hidden, axis=2)
    lower_grad = jnp.einsum(
        "erh,erd->ehd", hidden.astype(jnp.bfloat16), recv_grad, preferred_element_type=jnp.float32
    ).astype(jnp.bfloat16)
    delta_gate = (
        grad_hidden * up_value * sigma_gate * (1.0 + gate_pre * (1.0 - sigma_gate))
    ).astype(jnp.bfloat16)
    delta_up = (grad_hidden * swish).astype(jnp.bfloat16)
    gate_grad = jnp.einsum(
        "erd,erh->edh", recv_acts, delta_gate, preferred_element_type=jnp.float32
    ).astype(jnp.bfloat16)
    upper_grad = jnp.einsum(
        "erd,erh->edh", recv_acts, delta_up, preferred_element_type=jnp.float32
    ).astype(jnp.bfloat16)
    partial_value = jnp.einsum(
        "erh,edh->erd", delta_gate, gate_local, preferred_element_type=jnp.float32
    ) + jnp.einsum("erh,edh->erd", delta_up, upper_local, preferred_element_type=jnp.float32)
    back_rows, back_scores = (
        lax.all_to_all(partial_value, ("dp", "expert"), split_axis=1, concat_axis=0, tiled=True),
        lax.all_to_all(scores, ("dp", "expert"), split_axis=1, concat_axis=0, tiled=True),
    )
    slot_grad = jnp.sum(back_rows.reshape(dp_count, experts * capacity, width), axis=0).astype(
        jnp.bfloat16
    )
    slot_scores = jnp.sum(back_scores.reshape(dp_count, experts * capacity), axis=0)
    token_rows = jnp.arange(tok_count, dtype=jnp.int32)
    token_map = ((source_token[:, None] == token_rows[None, :]) & filled[:, None]).astype(
        jnp.bfloat16
    )
    input_grad = jnp.einsum(
        "st,sd->td", token_map, slot_grad, preferred_element_type=jnp.float32
    ).astype(jnp.bfloat16)
    padded_scores = jnp.concatenate([slot_scores, jnp.zeros((1,), jnp.float32)])
    weight_grad = (padded_scores[slot_index] / route_weight.reshape(-1)).reshape(tok_count, chosen)
    received = shifted(input_grad, "pipe", -1)
    return (received[None], weight_grad[None], gate_grad[None], upper_grad[None], lower_grad[None])


def solution(mesh):
    in_specs = (
        P("pipe", ("dp", "expert"), None),
        P("pipe", ("dp", "expert"), None),
        P("pipe", ("dp", "expert"), None),
        P("pipe", ("dp", "expert"), None),
        P("pipe", "expert", None, "dp"),
        P("pipe", "expert", None, "dp"),
        P("pipe", "expert", "dp", None),
    )
    out_specs = (
        P("pipe", ("dp", "expert"), None),
        P("pipe", ("dp", "expert"), None),
        P("pipe", "expert", None, "dp"),
        P("pipe", "expert", None, "dp"),
        P("pipe", "expert", "dp", None),
    )
    return jax.shard_map(shards, mesh=mesh, in_specs=in_specs, out_specs=out_specs, check_vma=False)
```

profile of v0, /device:TPU:0, one launch (start us, length us, event | category | flops | bytes accessed | tf_op | source)
XLA Modules:
  0.0 79.5 jit_solution(6049653979190262560)
XLA Ops:
  0.7 0.9 %copy.28 = s32[1,128,6]{2,1,0:T(8,128)S(1)} copy(s32[1,128,6]{1,0,2:T(1,128)} %param.9) | data formatting | bytes 6144 | tf_op args[2]
  3.3 1.9 %gather_fusion.2 = bf16[16,3072]{1,0:T(8,128)(2,1)S(1)} fusion(bf16[128,3072]{1,0:T(8,128)(2,1)} %bitcast.109, s32[1024]{0:T(1024)S(1)} %get-tuple-element.53), kind=kCustom, calls=%fused_computation.2 | custom fusion | bytes 196672 | tf_op jit(solution)/shard_map/gather | solution.py:45
  6.1 5.2 %all-to-all-start.1 = ((bf16[8,8,3072]{2,1,0:T(8,128)(2,1)}), bf16[8,8,3072]{2,1,0:T(8,128)(2,1)S(1)}, u32[]{:S(2)}, u32[]{:S(2)}) async-start(bf16[8,8,3072]{2,1,0:T(8,128)(2,1)} %bitcast.11), calls=%async_computation.1 | async-start | bytes 786432 | tf_op jit(solution)/shard_map/all_to_all | solution.py:57
  14.0 4.7 %all-to-all-done.1 = bf16[8,8,3072]{2,1,0:T(8,128)(2,1)S(1)} async-done(((bf16[8,8,3072]{2,1,0:T(8,128)(2,1)}), bf16[8,8,3072]{2,1,0:T(8,128)(2,1)S(1)}, u32[]{:S(2)}, u32[]{:S(2)}) %all-to-all-start.1) | async-done | bytes 393248 | tf_op jit(solution)/shard_map/all_to_all | solution.py:57
  18.7 1.7 %broadcast_in_dim.84 = bf16[4,2,8,3072]{3,2,1,0:T(8,128)(2,1)} broadcast(bf16[2,8,3072]{2,1,0:T(8,128)(2,1)} %fusion.20), dimensions={1,2,3} | broadcast | bytes 491520 | tf_op jit(solution)/shard_map/broadcast_in_dim | solution.py:53
  20.4 4.1 %all-to-all-start = ((bf16[8,8,3072]{2,1,0:T(8,128)(2,1)}), bf16[8,8,3072]{2,1,0:T(8,128)(2,1)}, u32[]{:S(2)}, u32[]{:S(2)}) async-start(bf16[8,8,3072]{2,1,0:T(8,128)(2,1)} %bitcast.108), calls=%async_computation | async-start | bytes 786432 | tf_op jit(solution)/shard_map/all_to_all | solution.py:58
  24.5 1.0 %fusion.6 = f32[64,256]{1,0:T(8,128)} fusion(bf16[1,1,3072,256]{3,2,1,0:T(8,128)(2,1)S(1)} %copy-done, bf16[8,8,3072]{2,1,0:T(8,128)(2,1)S(1)} %all-to-all-done.1), kind=kOutput, calls=%fused_computation.14 | convolution fusion | flops 100663296 | bytes 2031616 | tf_op jit(solution)/shard_map/erd,edh->erh/dot_general | solution.py:63
  25.5 1.0 %fusion.9 = f32[64,256]{1,0:T(8,128)} fusion(bf16[1,1,3072,256]{3,2,1,0:T(8,128)(2,1)S(1)} %copy-done.1, bf16[8,8,3072]{2,1,0:T(8,128)(2,1)S(1)} %all-to-all-done.1), kind=kOutput, calls=%fused_computation.17 | convolution fusion | flops 100663296 | bytes 2031616 | tf_op jit(solution)/shard_map/erd,edh->erh/dot_general | solution.py:64
  26.5 5.4 %all-to-all-done = bf16[8,8,3072]{2,1,0:T(8,128)(2,1)} async-done(((bf16[8,8,3072]{2,1,0:T(8,128)(2,1)}), bf16[8,8,3072]{2,1,0:T(8,128)(2,1)}, u32[]{:S(2)}, u32[]{:S(2)}) %all-to-all-start) | async-done | bytes 393248 | tf_op jit(solution)/shard_map/all_to_all | solution.py:58
  31.9 2.7 %multiply_reduce_fusion = (f32[64]{0:T(128)}, bf16[64,256]{1,0:T(8,128)(2,1)S(1)}, bf16[64,256]{1,0:T(8,128)(2,1)S(1)}) fusion(f32[64,256]{1,0:T(8,128)} %fusion.9, f32[64,256]{1,0:T(8,128)} %fusion.6, bf16[1,1,256,3072]{3,2,1,0:T(8,128)(2,1)} %param.13, bf16[8,8,3072]{2,1,0:T(8,128)(2,1)} %all-to-all-done), kind=kOutput, calls=%fused_computation.32 | convolution fusion | flops 100925376 | bytes 2162944 | tf_op jit(solution)/shard_map/erd,ehd->erh/dot_general | solution.py:67
  35.9 1.7 %copy.31 = f32[1,64,3072]{2,0,1:T(1,128)} copy(f32[1,64,3072]{2,1,0:T(8,128)S(1)} %fusion.3) | data formatting | bytes 1572864 | tf_op jit(solution)/shard_map/add | solution.py:87
  37.6 3.7 %all-to-all-start.2 = ((f32[1,64,3072]{2,0,1:T(1,128)}), f32[1,64,3072]{2,0,1:T(1,128)S(1)}, u32[]{:S(2)}, u32[]{:S(2)}) async-start(f32[1,64,3072]{2,0,1:T(1,128)} %copy.31), calls=%async_computation.2 | async-start | bytes 1572864 | tf_op jit(solution)/shard_map/all_to_all | solution.py:91
  42.8 1.7 %fusion.1 = bf16[1,1,3072,256]{3,2,1,0:T(8,128)(2,1)} fusion(bf16[64,256]{1,0:T(8,128)(2,1)S(1)} %copy-done.8, bf16[8,8,3072]{2,1,0:T(8,128)(2,1)S(1)} %all-to-all-done.1), kind=kOutput, calls=%fused_computation.7 | convolution fusion | flops 101449728 | bytes 1998848 | tf_op jit(solution)/shard_map/erd,erh->edh/dot_general | solution.py:84
  44.6 2.7 %fusion.2 = bf16[1,1,256,3072]{3,2,1,0:T(8,128)(2,1)} fusion(bf16[8,8,3072]{2,1,0:T(8,128)(2,1)} %all-to-all-done, f32[64,256]{1,0:T(8,128)S(1)} %copy-done.4, f32[64,256]{1,0:T(8,128)S(1)} %copy-done.3), kind=kOutput, calls=%fused_computation.8 | convolution fusion | flops 101548032 | bytes 2097152 | tf_op jit(solution)/shard_map/erh,erd->ehd/dot_general | solution.py:74
  47.3 5.6 %all-to-all-done.2 = f32[1,64,3072]{2,0,1:T(1,128)S(1)} async-done(((f32[1,64,3072]{2,0,1:T(1,128)}), f32[1,64,3072]{2,0,1:T(1,128)S(1)}, u32[]{:S(2)}, u32[]{:S(2)}) %all-to-all-start.2) | async-done | bytes 786464 | tf_op jit(solution)/shard_map/all_to_all | solution.py:91
  52.9 3.3 %all-to-all-start.3 = ((f32[1,8,8]{2,0,1:T(1,128)}), f32[1,8,8]{2,0,1:T(1,128)S(1)}, u32[]{:S(2)}, u32[]{:S(2)}) async-start(f32[1,8,8]{2,0,1:T(1,128)} %bitcast.17), calls=%async_computation.3 | async-start | bytes 8192 | tf_op jit(solution)/shard_map/all_to_all | solution.py:92
  56.4 1.2 %convolution_convert_fusion.3 = bf16[128,3072]{1,0:T(8,128)(2,1)S(1)} fusion(bf16[16,3072]{1,0:T(8,128)(2,1)S(1)} %reduce_sum.52, s32[16]{0:T(128)} %and_select_fusion.2, pred[16]{0:T(512)(128)(4,1)} %copy-done.11), kind=kOutput, calls=%fused_computation.9 | convolution fusion | flops 12980224 | bytes 884816 | tf_op jit(solution)/shard_map/st,sd->td/dot_general | solution.py:102
  57.6 3.7 %collective-permute-start = (bf16[128,3072]{1,0:T(8,128)(2,1)S(1)}, bf16[128,3072]{1,0:T(8,128)(2,1)S(1)}, u32[]{:S(2)}, u32[]{:S(2)}) collective-permute-start(bf16[128,3072]{1,0:T(8,128)(2,1)S(1)} %convolution_convert_fusion.3), channel_id=1, source_target_pairs={{0,24},{8,0},{16,8},{24,16},{1,25},{9,1},{17,9},{25,17},{2,26},{10... | collective-permute-start | bytes 2359304 | tf_op jit(solution)/shard_map/ppermute | solution.py:10
  61.2 2.5 %fusion = bf16[1,1,3072,256]{3,2,1,0:T(8,128)(2,1)} fusion(bf16[64,256]{1,0:T(8,128)(2,1)} %copy-done.6, bf16[8,8,3072]{2,1,0:T(8,128)(2,1)S(1)} %all-to-all-done.1), kind=kOutput, calls=%fused_computation.6 | convolution fusion | flops 101449728 | bytes 1998848 | tf_op jit(solution)/shard_map/erd,erh->edh/dot_general | solution.py:81
  65.7 4.4 %fusion.34 = (f32[768]{0:T(1024)S(1)}, s32[768,1]{0,1:T(1,128)S(1)}) fusion(f32[]{:T(128)} %bitcast.27, f32[]{:T(128)} %bitcast.28, f32[]{:T(128)} %bitcast.29, f32[]{:T(128)} %bitcast.30, f32[]{:T(128)} %bitcast.31, f32[]{:T(128)} %bitcast.33, f32[]{:T(128)} %bitcast.32, s32[768,1]{0,1:T(1,128)S(1)} %mul.82, pred[768,1]{0,1:T(4,128)(4,1)S(1)} %lt.81, ...), kind=kLoop, calls=%fused_computation.76 | loop fusion | flops 14592 | bytes 13084 | tf_op jit(solution)/shard_map/gather | solution.py:106
  70.2 5.6 %select_select_fusion = f32[768]{0:T(1024)S(1)} fusion(pred[768]{0:T(1024)(128)(4,1)S(1)} %get-tuple-element.29, pred[768]{0:T(1024)(128)(4,1)S(1)} %get-tuple-element.28, pred[768]{0:T(1024)(128)(4,1)S(1)} %get-tuple-element.27, pred[768]{0:T(1024)(128)(4,1)S(1)} %get-tuple-element.26, pred[768]{0:T(1024)(128)(4,1)S(1)} %get-tuple-element.25, ...), kind=kLoop, calls=%fused_computation.72 | loop fusion | flops 7680 | bytes 13860 | tf_op jit(solution)/shard_map/gather | solution.py:106
  76.0 0.9 %div.29 = f32[1,128,6]{2,1,0:T(8,128)S(1)} divide(f32[1,128,6]{2,1,0:T(8,128)S(1)} %gather.21, f32[1,128,6]{2,1,0:T(8,128)} %copy-done.5) | non-fusion elementwise | flops 768 | bytes 9216 | tf_op jit(solution)/shard_map/div | solution.py:106
  77.5 1.0 %collective-permute-done = bf16[128,3072]{1,0:T(8,128)(2,1)S(1)} collective-permute-done((bf16[128,3072]{1,0:T(8,128)(2,1)S(1)}, bf16[128,3072]{1,0:T(8,128)(2,1)S(1)}, u32[]{:S(2)}, u32[]{:S(2)}) %collective-permute-start) | collective-permute-done | bytes 786464 | tf_op jit(solution)/shard_map/ppermute | solution.py:10
  78.6 0.9 %copy.41 = bf16[1,128,3072]{2,1,0:T(8,128)(2,1)} copy(bf16[1,128,3072]{2,1,0:T(8,128)(2,1)S(1)} %bitcast.111) | data formatting | bytes 1572864
  (73 shorter events, 11.0 us)
Async XLA Ops:
  0.6 23.9 %copy-start = (bf16[1,1,3072,256]{3,2,1,0:T(8,128)(2,1)S(1)}, bf16[1,1,3072,256]{3,2,1,0:T(8,128)(2,1)}, u32[]{:S(2)}) copy-start(bf16[1,1,3072,256]{3,2,1,0:T(8,128)(2,1)} %param.11) | copy-start | bytes 4718596
  0.6 10.7 %copy-start.9 = (s32[1,128,6]{1,0,2:T(1,128)S(1)}, s32[1,128,6]{1,0,2:T(1,128)}, u32[]{:S(2)}) copy-start(s32[1,128,6]{1,0,2:T(1,128)} %param.9) | copy-start | bytes 9220
  0.7 11.0 %copy-start.10 = (f32[1,128,6]{1,0,2:T(1,128)S(1)}, f32[1,128,6]{1,0,2:T(1,128)}, u32[]{:S(2)}) copy-start(f32[1,128,6]{1,0,2:T(1,128)} %param.10) | copy-start | bytes 9220
  2.8 9.8 %copy-start.2 = (bf16[1,128,3072]{2,1,0:T(8,128)(2,1)S(1)}, bf16[1,128,3072]{2,1,0:T(8,128)(2,1)}, u32[]{:S(2)}) copy-start(bf16[1,128,3072]{2,1,0:T(8,128)(2,1)} %param.8) | copy-start | bytes 2359300
  3.1 9.5 %copy-start.11 = (pred[16]{0:T(512)(128)(4,1)}, pred[16]{0:T(512)(128)(4,1)S(1)}, u32[]{:S(2)}) copy-start(pred[16]{0:T(512)(128)(4,1)S(1)} %fusion.23) | copy-start | bytes 52
  3.2 9.4 %copy-start.13 = (s32[16]{0:T(128)}, s32[16]{0:T(128)S(1)}, u32[]{:S(2)}) copy-start(s32[16]{0:T(128)S(1)} %select_reduce_fusion) | copy-start | bytes 196
  6.1 12.6 %all-to-all-start.1 = ((bf16[8,8,3072]{2,1,0:T(8,128)(2,1)}), bf16[8,8,3072]{2,1,0:T(8,128)(2,1)S(1)}, u32[]{:S(2)}, u32[]{:S(2)}) async-start(bf16[8,8,3072]{2,1,0:T(8,128)(2,1)} %bitcast.11), calls=%async_computation.1 | async-start | bytes 786432 | tf_op jit(solution)/shard_map/all_to_all | solution.py:57
  11.8 1.5 %copy-start.5 = (f32[1,128,6]{2,1,0:T(8,128)}, f32[1,128,6]{2,1,0:T(8,128)S(1)}, u32[]{:S(2)}) copy-start(f32[1,128,6]{2,1,0:T(8,128)S(1)} %copy.30) | copy-start | bytes 9220
  14.0 11.5 %copy-start.1 = (bf16[1,1,3072,256]{3,2,1,0:T(8,128)(2,1)S(1)}, bf16[1,1,3072,256]{3,2,1,0:T(8,128)(2,1)}, u32[]{:S(2)}) copy-start(bf16[1,1,3072,256]{3,2,1,0:T(8,128)(2,1)} %param.12) | copy-start | bytes 4718596
  20.4 11.5 %all-to-all-start = ((bf16[8,8,3072]{2,1,0:T(8,128)(2,1)}), bf16[8,8,3072]{2,1,0:T(8,128)(2,1)}, u32[]{:S(2)}, u32[]{:S(2)}) async-start(bf16[8,8,3072]{2,1,0:T(8,128)(2,1)} %bitcast.108), calls=%async_computation | async-start | bytes 786432 | tf_op jit(solution)/shard_map/all_to_all | solution.py:58
  34.6 0.6 copy-start.6
  34.6 0.6 copy-start.7
  35.9 5.7 %copy-start.14 = (s32[16]{0:T(128)S(1)}, s32[16]{0:T(128)}, u32[]{:S(2)}) copy-start(s32[16]{0:T(128)} %copy-done.13) | copy-start | bytes 196
  35.9 6.3 %copy-start.12 = (f32[64]{0:T(128)S(1)}, f32[64]{0:T(128)}, u32[]{:S(2)}) copy-start(f32[64]{0:T(128)} %get-tuple-element.32) | copy-start | bytes 772
  35.9 7.0 %copy-start.8 = (bf16[64,256]{1,0:T(8,128)(2,1)S(1)}, bf16[64,256]{1,0:T(8,128)(2,1)}, u32[]{:S(2)}) copy-start(bf16[64,256]{1,0:T(8,128)(2,1)} %copy-done.7) | copy-start | bytes 98308
  37.6 7.0 %copy-start.3 = (f32[64,256]{1,0:T(8,128)S(1)}, f32[64,256]{1,0:T(8,128)}, u32[]{:S(2)}) copy-start(f32[64,256]{1,0:T(8,128)} %fusion.6) | copy-start | bytes 196612
  37.6 7.0 %copy-start.4 = (f32[64,256]{1,0:T(8,128)S(1)}, f32[64,256]{1,0:T(8,128)}, u32[]{:S(2)}) copy-start(f32[64,256]{1,0:T(8,128)} %fusion.9) | copy-start | bytes 196612
  37.6 15.3 %all-to-all-start.2 = ((f32[1,64,3072]{2,0,1:T(1,128)}), f32[1,64,3072]{2,0,1:T(1,128)S(1)}, u32[]{:S(2)}, u32[]{:S(2)}) async-start(f32[1,64,3072]{2,0,1:T(1,128)} %copy.31), calls=%async_computation.2 | async-start | bytes 1572864 | tf_op jit(solution)/shard_map/all_to_all | solution.py:91
  52.9 10.8 %all-to-all-start.3 = ((f32[1,8,8]{2,0,1:T(1,128)}), f32[1,8,8]{2,0,1:T(1,128)S(1)}, u32[]{:S(2)}, u32[]{:S(2)}) async-start(f32[1,8,8]{2,0,1:T(1,128)} %bitcast.17), calls=%async_computation.3 | async-start | bytes 8192 | tf_op jit(solution)/shard_map/all_to_all | solution.py:92
  57.6 21.0 %collective-permute-start = (bf16[128,3072]{1,0:T(8,128)(2,1)S(1)}, bf16[128,3072]{1,0:T(8,128)(2,1)S(1)}, u32[]{:S(2)}, u32[]{:S(2)}) collective-permute-start(bf16[128,3072]{1,0:T(8,128)(2,1)S(1)} %convolution_convert_fusion.3), channel_id=1, source_target_pairs={{0,24},{8,0},{16,8},{24,16},{1,25},{9,1},{17,9},{25,17},{2,26},{10... | collective-permute-start | bytes 2359304 | tf_op jit(solution)/shard_map/ppermute | solution.py:10
where the time goes:
time: 80.3 us; the launch traced here: 79.5 us
  starting transfers between devices  19.9 us (25%)
  waiting for transfers between devices  16.7 us (21%)
  other arithmetic  14.3 us (18%)
  matrix products  14.1 us (18%)
  local copies, waits for them, and re-layouts  13.5 us (17%)
  between operations  0.92 us (1%)
    gather x3, other arithmetic, shards(): padded_scores[slot_index] / route_weight.reshape(-1)  10.2 us
    all_to_all x1, waiting for transfers between devices, shards(): lax.all_to_all(partial_value, ('dp', 'expert'), split_axis=1, concat_axis...  5.58 us
    all_to_all x1, waiting for transfers between devices, shards(): lax.all_to_all(grad_copies, ('dp', 'expert'), split_axis=0, concat_axis=1...  5.38 us
    all_to_all x1, starting transfers between devices, shards(): lax.all_to_all(acts_copies, ('dp', 'expert'), split_axis=0, concat_axis=1...  5.2 us
    all_to_all x1, waiting for transfers between devices, shards(): lax.all_to_all(acts_copies, ('dp', 'expert'), split_axis=0, concat_axis=1...  4.73 us
    all_to_all x1, starting transfers between devices, shards(): lax.all_to_all(grad_copies, ('dp', 'expert'), split_axis=0, concat_axis=1...  4.1 us
    all_to_all x1, starting transfers between devices, shards(): lax.all_to_all(partial_value, ('dp', 'expert'), split_axis=1, concat_axis...  3.68 us
    ppermute x1, starting transfers between devices, shifted(): return lax.ppermute(value, axis, pairs)  3.66 us
  transfers between devices with their start and end apart: 5, of which 4 were waited for; matrix products, arithmetic and copies ran while one was open for 35% of the time, Pallas kernels for 0%

commit v1 on v0

--- a/solution.py
+++ b/solution.py
@@ -1,7 +1,354 @@
+import functools
+
 import jax
 import jax.numpy as jnp
 from jax import lax
+from jax.experimental import pallas as pl
+from jax.experimental.pallas import tpu as pltpu
 from jax.sharding import PartitionSpec as P
+
+PAIRWISE_MAX = 8
+LANES = 128
+VMEM = pl.BlockSpec(memory_space=pltpu.VMEM)
+ANY = pl.BlockSpec(memory_space=pl.ANY)
+
+
+def shape_of(shape, dtype):
+    return jax.ShapeDtypeStruct(shape, dtype)
+
+
+def cost(flops, bytes_moved):
+    return pl.CostEstimate(flops=flops, bytes_accessed=bytes_moved, transcendentals=0)
+
+
+def power_of_two(number):
+    return number > 0 and number & (number - 1) == 0
+
+
+def swap(value, offset):
+    count = lax.axis_size("dp") * lax.axis_size("expert")
+    return lax.ppermute(value, ("dp", "expert"), [(i, i ^ offset) for i in range(count)])
+
+
+def swap_back(value, offset):
+    sections = lax.axis_size("pipe")
+    count = lax.axis_size("dp") * lax.axis_size("expert")
+    pairs = [
+        (s * count + i, ((s - 1) % sections) * count + (i ^ offset))
+        for s in range(sections)
+        for i in range(count)
+    ]
+    return lax.ppermute(value, ("pipe", "dp", "expert"), pairs)
+
+
+def pick_kernel(capacity, groups, own_ref, ids_ref, weight_ref, acts_ref, grad_ref, *refs):
+    outs = refs[:groups]
+    select_ref, acts_buf, grad_buf, sems = refs[groups:]
+    acts_copy = pltpu.make_async_copy(acts_ref, acts_buf, sems.at[0])
+    grad_copy = pltpu.make_async_copy(grad_ref, grad_buf, sems.at[1])
+    acts_copy.start()
+    grad_copy.start()
+    chosen, _, tokens = ids_ref.shape
+    rows = groups * capacity
+    row = lax.broadcasted_iota(jnp.int32, (rows, tokens), 0)
+    row_expert = (row // capacity) ^ own_ref[0]
+    taken = jnp.zeros((rows, tokens), jnp.float32)
+    scale = jnp.zeros((rows, tokens), jnp.float32)
+    for k in range(chosen):
+        same = ids_ref[k] == row_expert
+        taken = jnp.where(same, 1.0, taken)
+        scale = jnp.where(same, weight_ref[k], scale)
+    before = lax.broadcasted_iota(jnp.int32, (tokens, tokens), 0)
+    after = lax.broadcasted_iota(jnp.int32, (tokens, tokens), 1)
+    earlier = jnp.where(before < after, 1.0, 0.0).astype(jnp.bfloat16)
+    rank = jnp.dot(taken.astype(jnp.bfloat16), earlier, preferred_element_type=jnp.float32)
+    slot = (row % capacity).astype(jnp.float32)
+    select = jnp.where(rank == slot, taken, 0.0)
+    row_scale = jnp.sum(select * scale, axis=1, keepdims=True)
+    select = select.astype(jnp.bfloat16)
+    select_ref[...] = select
+    acts_copy.wait()
+    acts_rows = jnp.dot(select, acts_buf[...], preferred_element_type=jnp.float32)
+    grad_copy.wait()
+    grad_rows = jnp.dot(select, grad_buf[...], preferred_element_type=jnp.float32) * row_scale
+    for j in range(groups):
+        part = slice(j * capacity, (j + 1) * capacity)
+        outs[j][...] = jnp.concatenate([acts_rows[part], grad_rows[part]], axis=0).astype(jnp.bfloat16)
+
+
+def pick_rows(own, ids, weights, acts, grads, groups, capacity):
+    tokens, width = acts.shape
+    group = shape_of((2 * capacity, width), jnp.bfloat16)
+    return pl.pallas_call(
+        functools.partial(pick_kernel, capacity, groups),
+        out_shape=[group] * groups + [shape_of((groups * capacity, tokens), jnp.bfloat16)],
+        in_specs=[pl.BlockSpec(memory_space=pltpu.SMEM), VMEM, VMEM, ANY, ANY],
+        out_specs=[VMEM] * (groups + 1),
+        scratch_shapes=[
+            pltpu.VMEM((tokens, width), jnp.bfloat16),
+            pltpu.VMEM((tokens, width), jnp.bfloat16),
+            pltpu.SemaphoreType.DMA((2,)),
+        ],
+        cost_estimate=cost(4 * groups * capacity * tokens * width, 4 * tokens * width),
+        compiler_params=pltpu.CompilerParams(vmem_limit_bytes=16 * 2**20),
+        name="pick_rows",
+    )(own, ids, weights, acts, grads)
+
+
+def split_rows(value, capacity):
+    pieces = value.shape[0] // (2 * capacity)
+    upper = [value[2 * p * capacity : (2 * p + 1) * capacity] for p in range(pieces)]
+    lower = [value[(2 * p + 1) * capacity : (2 * p + 2) * capacity] for p in range(pieces)]
+    return jnp.concatenate(upper, axis=0), jnp.concatenate(lower, axis=0)
+
+
+def weave(value, capacity, upper):
+    blank = jnp.zeros((capacity, value.shape[1]), value.dtype)
+    parts = []
+    for p in range(value.shape[0] // capacity):
+        part = value[p * capacity : (p + 1) * capacity]
+        parts += [part, blank] if upper else [blank, part]
+    return jnp.concatenate(parts, axis=0)
+
+
+def hidden_kernel(capacity, pieces, *refs):
+    piece_refs = refs[:pieces]
+    gate_ref, upper_ref, lower_ref = refs[pieces : pieces + 3]
+    keep_ref, send_ref, score_ref, delta_ref, hidden_ref = refs[pieces + 3 :]
+    rows = jnp.concatenate([ref[...] for ref in piece_refs], axis=0)
+    across = (((1,), (1,)), ((), ()))
+    gate_pre, _ = split_rows(jnp.dot(rows, gate_ref[...], preferred_element_type=jnp.float32), capacity)
+    up_value, _ = split_rows(jnp.dot(rows, upper_ref[...], preferred_element_type=jnp.float32), capacity)
+    _, grad_hidden = split_rows(
+        lax.dot_general(rows, lower_ref[...], across, preferred_element_type=jnp.float32), capacity
+    )
+    sigma_gate = jax.nn.sigmoid(gate_pre)
+    swish = gate_pre * sigma_gate
+    hidden = swish * up_value
+    scores = jnp.sum(hidden * grad_hidden, axis=1, keepdims=True)
+    delta_gate = grad_hidden * up_value * sigma_gate * (1.0 + gate_pre * (1.0 - sigma_gate))
+    delta_up = grad_hidden * swish
+    partial_rows = lax.dot_general(
+        delta_gate.astype(jnp.bfloat16), gate_ref[...], across, preferred_element_type=jnp.float32
+    ) + lax.dot_general(
+        delta_up.astype(jnp.bfloat16), upper_ref[...], across, preferred_element_type=jnp.float32
+    )
+    half, width = keep_ref.shape
+    units = gate_ref.shape[1]
+    keep_ref[...] = partial_rows[:half]
+    send_ref[:, :width] = partial_rows[half:].astype(jnp.bfloat16)
+    score_ref[...] = jnp.broadcast_to(scores[:half], (half, LANES))
+    rest = scores[half:]
+    high = rest.astype(jnp.bfloat16).astype(jnp.float32)
+    middle = (rest - high).astype(jnp.bfloat16).astype(jnp.float32)
+    low = rest - high - middle
+    lane = lax.broadcasted_iota(jnp.int32, (half, LANES), 1)
+    parts = jnp.where(lane == 0, high, jnp.where(lane == 1, middle, jnp.where(lane == 2, low, 0.0)))
+    send_ref[:, width:] = parts.astype(jnp.bfloat16)
+    delta_ref[:, :units] = weave(delta_gate, capacity, True).astype(jnp.bfloat16)
+    delta_ref[:, units:] = weave(delta_up, capacity, True).astype(jnp.bfloat16)
+    hidden_ref[...] = weave(hidden, capacity, False).astype(jnp.bfloat16)
+
+
+def hidden_pass(pieces, gate, upper, lower, capacity):
+    width, units = gate.shape
+    count = len(pieces)
+    half = count * capacity // 2
+    rows = 2 * count * capacity
+    return pl.pallas_call(
+        functools.partial(hidden_kernel, capacity, count),
+        out_shape=[
+            shape_of((half, width), jnp.float32),
+            shape_of((half, width + LANES), jnp.bfloat16),
+            shape_of((half, LANES), jnp.float32),
+            shape_of((rows, 2 * units), jnp.bfloat16),
+            shape_of((rows, units), jnp.bfloat16),
+        ],
+        in_specs=[VMEM] * (count + 3),
+        out_specs=[VMEM] * 5,
+        cost_estimate=cost(10 * rows * width * units, 6 * width * units),
+        compiler_params=pltpu.CompilerParams(vmem_limit_bytes=24 * 2**20),
+        name="hidden_pass",
+    )(*pieces, gate, upper, lower)
+
+
+def join_kernel(capacity, groups, keep_ref, score_ref, recv_ref, *out_refs):
+    width = keep_ref.shape[1]
+    for j in range(groups):
+        part = slice(j * capacity, (j + 1) * capacity)
+        other = recv_ref[part, :width].astype(jnp.float32)
+        out_refs[j][...] = (keep_ref[part] + other).astype(jnp.bfloat16)
+    extra = recv_ref[:, width:].astype(jnp.float32)
+    out_refs[groups][...] = score_ref[...] + jnp.sum(extra, axis=1, keepdims=True)
+
+
+def join_cores(keep, scores, recv, groups, capacity):
+    half, width = keep.shape
+    return pl.pallas_call(
+        functools.partial(join_kernel, capacity, groups),
+        out_shape=[shape_of((capacity, width), jnp.bfloat16)] * groups + [shape_of((half, LANES), jnp.float32)],
+        in_specs=[VMEM] * 3,
+        out_specs=[VMEM] * (groups + 1),
+        cost_estimate=cost(2 * half * width, 8 * half * width),
+        compiler_params=pltpu.CompilerParams(vmem_limit_bytes=8 * 2**20),
+        name="join_cores",
+    )(keep, scores, recv)
+
+
+def weights_kernel(pieces, step, *refs):
+    piece_refs = refs[:pieces]
+    delta_ref, hidden_ref, gate_out, upper_out, lower_out = refs[pieces:]
+    start = pl.multiple_of(pl.program_id(0) * step, step)
+    rows = jnp.concatenate([ref[:, pl.ds(start, step)] for ref in piece_refs], axis=0)
+    down = (((0,), (0,)), ((), ()))
+    both = lax.dot_general(rows, delta_ref[...], down, preferred_element_type=jnp.float32)
+    units = gate_out.shape[1]
+    gate_out[...] = both[:, :units].astype(jnp.bfloat16)
+    upper_out[...] = both[:, units:].astype(jnp.bfloat16)
+    lower_out[...] = lax.dot_general(
+        hidden_ref[...], rows, down, preferred_element_type=jnp.float32
+    ).astype(jnp.bfloat16)
+
+
+def weight_grads(pieces, delta, hidden, step):
+    width = pieces[0].shape[1]
+    rows, units = hidden.shape
+    count = len(pieces)
+
+    def whole(array):
+        return pl.BlockSpec(array.shape, lambda i: (0, 0))
+
+    return pl.pallas_call(
+        functools.partial(weights_kernel, count, step),
+        grid=(width // step,),
+        out_shape=[
+            shape_of((width, units), jnp.bfloat16),
+            shape_of((width, units), jnp.bfloat16),
+            shape_of((units, width), jnp.bfloat16),
+        ],
+        in_specs=[whole(array) for array in (*pieces, delta, hidden)],
+        out_specs=[
+            pl.BlockSpec((step, units), lambda i: (i, 0)),
+            pl.BlockSpec((step, units), lambda i: (i, 0)),
+            pl.BlockSpec((units, step), lambda i: (0, i)),
+        ],
+        cost_estimate=cost(6 * rows * width * units, 6 * width * units),
+        compiler_params=pltpu.CompilerParams(vmem_limit_bytes=24 * 2**20),
+        name="weight_grads",
+    )(*pieces, delta, hidden)
+
+
+def score_kernel(capacity, groups, own_ref, ids_ref, weight_ref, select_ref, *refs):
+    out_ref = refs[-1]
+    chosen, _, tokens = ids_ref.shape
+    sums = []
+    for j in range(groups):
+        part = slice(j * capacity, (j + 1) * capacity)
+        picked = select_ref[part].astype(jnp.float32) * refs[j][:, :1]
+        sums.append(jnp.sum(picked, axis=0, keepdims=True))
+    for k in range(chosen):
+        value = jnp.zeros((1, tokens), jnp.float32)
+        for j in range(groups):
+            value = jnp.where(ids_ref[k] == (own_ref[0] ^ j), sums[j], value)
+        out_ref[k] = value / weight_ref[k]
+
+
+def score_grads(own, ids, weights, select, scores, capacity):
+    groups = len(scores)
+    return pl.pallas_call(
+        functools.partial(score_kernel, capacity, groups),
+        out_shape=shape_of(weights.shape, jnp.float32),
+        in_specs=[pl.BlockSpec(memory_space=pltpu.SMEM)] + [VMEM] * (3 + groups),
+        out_specs=VMEM,
+        cost_estimate=cost(1000, 1000),
+        compiler_params=pltpu.CompilerParams(vmem_limit_bytes=4 * 2**20),
+        name="score_grads",
+    )(own, ids, weights, select, *scores)
+
+
+def spread_kernel(groups, terms, select_ref, *refs):
+    out_ref = refs[-1]
+    sums = []
+    for j in range(groups):
+        total = refs[j * terms][...].astype(jnp.float32)
+        for term in range(1, terms):
+            total = total + refs[j * terms + term][...].astype(jnp.float32)
+        sums.append(total)
+    slot_grad = jnp.concatenate(sums, axis=0).astype(jnp.bfloat16)
+    out_ref[...] = lax.dot_general(
+        select_ref[...], slot_grad, (((0,), (0,)), ((), ())), preferred_element_type=jnp.float32
+    ).astype(jnp.bfloat16)
+
+
+def spread_rows(select, groups, step):
+    tokens = select.shape[1]
+    capacity, width = groups[0][0].shape
+    terms = len(groups[0])
+    flat = [array for group in groups for array in group]
+    return pl.pallas_call(
+        functools.partial(spread_kernel, len(groups), terms),
+        grid=(width // step,),
+        out_shape=shape_of((tokens, width), jnp.bfloat16),
+        in_specs=[pl.BlockSpec(select.shape, lambda i: (0, 0))]
+        + [pl.BlockSpec((capacity, step), lambda i: (0, i)) for _ in flat],
+        out_specs=pl.BlockSpec((tokens, step), lambda i: (0, i)),
+        cost_estimate=cost(2 * select.shape[0] * tokens * width, 2 * tokens * width),
+        compiler_params=pltpu.CompilerParams(vmem_limit_bytes=16 * 2**20),
+        name="spread_rows",
+    )(select, *flat)
+
+
+def pairwise_shards(block_input, output_grad, expert_ids, gate_weights, gate_proj, up_proj, down_proj):
+    tokens = block_input.shape[1]
+    width = block_input.shape[2]
+    capacity = tokens // 16
+    groups = lax.axis_size("expert")
+    partner = groups
+    count = lax.axis_size("dp") * groups
+    plane = [offset for offset in range(count) if not offset & partner]
+    own = lax.axis_index("expert").astype(jnp.int32).reshape(1)
+    ids = jnp.transpose(expert_ids, (2, 0, 1))
+    weights = jnp.transpose(gate_weights, (2, 0, 1))
+    *sends, select = pick_rows(own, ids, weights, block_input[0], output_grad[0], groups, capacity)
+    select_next = swap_back(select, 0)
+    mine = {0: sends[0]}
+    for offset in sorted(plane[1:], reverse=True):
+        mine[offset] = swap(sends[offset % groups], offset)
+    theirs = {offset: swap(mine[offset], partner) for offset in plane}
+    pieces = [mine[offset] for offset in plane] + [theirs[offset] for offset in plane]
+    keep, send, scores, delta, hidden = hidden_pass(
+        pieces, gate_proj[0, 0], up_proj[0, 0], down_proj[0, 0], capacity
+    )
+    recv = swap(send, partner)
+    *joined, scores = join_cores(keep, scores, recv, len(plane), capacity)
+    back = {offset: swap_back(joined[i], offset) for i, offset in enumerate(plane)}
+    gate_grad, upper_grad, lower_grad = weight_grads(pieces, delta, hidden, 512)
+    score_rows = {offset: scores[i * capacity : (i + 1) * capacity, :] for i, offset in enumerate(plane)}
+    bit = count // 2
+    while bit > partner:
+        low = [offset for offset in score_rows if not offset & bit]
+        moved = swap(jnp.concatenate([score_rows[offset | bit][:, :1] for offset in low]), bit)
+        score_rows = {
+            offset: score_rows[offset][:, :1] + moved[i * capacity : (i + 1) * capacity]
+            for i, offset in enumerate(low)
+        }
+        bit //= 2
+    score_list = [
+        score_rows[j][:, :1] if j == 0 else swap(score_rows[j][:, :1], j) for j in range(groups)
+    ]
+    weight_grad = score_grads(own, ids, weights, select, score_list, capacity)
+    received = spread_rows(
+        select_next,
+        [[back[offset] for offset in plane if offset % groups == j] for j in range(groups)],
+        width // 2,
+    )
+    return (
+        received[None],
+        jnp.transpose(weight_grad, (1, 2, 0)),
+        gate_grad[None, None],
+        upper_grad[None, None],
+        lower_grad[None, None],
+    )
 
 
 def shifted(value, axis, steps):
@@ -27,7 +374,7 @@
     return (slot_index, source_pair, filled)
 
 
-def shards(block_input, output_grad, expert_ids, gate_weights, gate_proj, up_proj, down_proj):
+def general_shards(block_input, output_grad, expert_ids, gate_weights, gate_proj, up_proj, down_proj):
     acts_local = block_input[0]
     grad_local = output_grad[0]
     chosen_ids = expert_ids[0]
@@ -125,4 +472,16 @@
         P("pipe", "expert", None, "dp"),
         P("pipe", "expert", "dp", None),
     )
+    dp_count, expert_count = mesh.shape["dp"], mesh.shape["expert"]
+
+    def shards(*arrays):
+        pairwise = (
+            dp_count * expert_count <= PAIRWISE_MAX
+            and dp_count > 1
+            and power_of_two(dp_count)
+            and power_of_two(expert_count)
+            and arrays[4].shape[1] == 1
+        )
+        return (pairwise_shards if pairwise else general_shards)(*arrays)
+
     return jax.shard_map(shards, mesh=mesh, in_specs=in_specs, out_specs=out_specs, check_vma=False)

time: 80.3 us -> 43.4 us (0.54)
  other arithmetic: 14.3 us -> 0.01 us
  matrix products: 14.1 us -> 0 us
  Pallas kernels: 0 us -> 9.63 us
  waiting for transfers between devices: 16.7 us -> 9.49 us
  local copies, waits for them, and re-layouts: 13.5 us -> 6.58 us
  starting transfers between devices: 19.9 us -> 16.7 us
    all_to_all x4 -> x0, starting transfers between devices: 16.3 us -> none  [the longest x1 5.2 us: shards(): lax.all_to_all(acts_copies, ('dp', 'expert'), split_axis=0, concat_axis=1...]
    all_to_all x4 -> x0, waiting for transfers between devices: 15.7 us -> none  [the longest x1 5.58 us: shards(): lax.all_to_all(partial_value, ('dp', 'expert'), split_axis=1, concat_axis...]
    dot_general x9 -> x0, matrix products: 14.1 us -> none  [the longest x1 2.75 us: shards(): jnp.einsum('erh,erd->ehd', hidden.astype(jnp.bfloat16), recv_grad, prefer...]
    ppermute x1 -> x15, starting transfers between devices: 3.66 us -> 16.7 us  [the longest x5 10.1 us: swap_back(): return lax.ppermute(value, ('pipe', 'dp', 'expert'), pairs)]
    gather x4 -> x0, other arithmetic: 10.2 us -> none  [the longest x3 10.2 us: shards(): padded_scores[slot_index] / route_weight.reshape(-1)]
    pallas_call x0 -> x6, Pallas kernels: none -> 9.63 us  [the longest x1 4.01 us: weight_grads(): pl.pallas_call(functools.partial(weights_kernel, count, step), grid=(widt...]
    ppermute x1 -> x15, waiting for transfers between devices: 1.05 us -> 9.49 us  [the longest x10 9.47 us: swap(): lax.ppermute(value, ('dp', 'expert'), [(i, i ^ offset) for i in range(cou...]
    gather x5 -> x0, local copies, waits for them, and re-layouts: 4.03 us -> none  [the longest x1 1.94 us: shards(): acts_local[source_token]]
  transfers between devices with their start and end apart: 5 -> 15, of which waited for: 4 -> 5; matrix products, arithmetic and copies ran while one was open for 35% -> 0% of each run, Pallas kernels for 0% -> 11%
where the time goes in v1:
time: 43.4 us; the launch traced here: 43.2 us
  starting transfers between devices  16.7 us (38%)
  Pallas kernels  9.63 us (22%)
  waiting for transfers between devices  9.49 us (22%)
  local copies, waits for them, and re-layouts  6.58 us (15%)
  between operations  0.74 us (2%)
    ppermute x5, starting transfers between devices, swap_back(): return lax.ppermute(value, ('pipe', 'dp', 'expert'), pairs)  10.1 us
    ppermute x10, waiting for transfers between devices, swap(): lax.ppermute(value, ('dp', 'expert'), [(i, i ^ offset) for i in range(cou...  9.47 us
    unnamed x18, local copies, waits for them, and re-layouts  6.58 us
    ppermute x10, starting transfers between devices, swap(): lax.ppermute(value, ('dp', 'expert'), [(i, i ^ offset) for i in range(cou...  6.57 us
    pallas_call x1, Pallas kernels, weight_grads(): pl.pallas_call(functools.partial(weights_kernel, count, step), grid=(widt...  4.01 us
    pallas_call x1, Pallas kernels, hidden_pass(): pl.pallas_call(functools.partial(hidden_kernel, capacity, count), out_sha...  2.73 us
    pallas_call x1, Pallas kernels, spread_rows(): pl.pallas_call(functools.partial(spread_kernel, len(groups), terms), grid...  1.34 us
  transfers between devices with their start and end apart: 15, of which 5 were waited for; matrix products, arithmetic and copies ran while one was open for 0% of the time, Pallas kernels for 11%

profile of v1, /device:TPU:0, one launch (start us, length us, event | category | flops | bytes accessed | tf_op | source)
XLA Modules:
  0.0 43.2 jit_solution(11253403239141938636)
XLA Ops:
  0.7 1.2 %copy-done.3 = bf16[1,128,3072]{2,1,0:T(8,128)(2,1)S(1)} copy-done((bf16[1,128,3072]{2,1,0:T(8,128)(2,1)S(1)}, bf16[1,128,3072]{2,1,0:T(8,128)(2,1)}, u32[]{:S(2)}) %copy-start.3) | copy-done | bytes 786456
  1.9 1.1 %copy-done.4 = bf16[1,128,3072]{2,1,0:T(8,128)(2,1)S(1)} copy-done((bf16[1,128,3072]{2,1,0:T(8,128)(2,1)S(1)}, bf16[1,128,3072]{2,1,0:T(8,128)(2,1)}, u32[]{:S(2)}) %copy-start.4) | copy-done | bytes 786456
  3.0 0.7 %copy-done.5 = s32[1,128,6]{1,0,2:T(1,128)S(1)} copy-done((s32[1,128,6]{1,0,2:T(1,128)S(1)}, s32[1,128,6]{1,0,2:T(1,128)}, u32[]{:S(2)}) %copy-start.5) | copy-done | bytes 3096
  3.7 0.7 %copy-done.7 = f32[1,128,6]{1,0,2:T(1,128)S(1)} copy-done((f32[1,128,6]{1,0,2:T(1,128)S(1)}, f32[1,128,6]{1,0,2:T(1,128)}, u32[]{:S(2)}) %copy-start.7) | copy-done | bytes 3096
  4.4 0.8 %pick_rows.1 = (bf16[16,3072]{1,0:T(8,128)(2,1)S(1)}, bf16[16,3072]{1,0:T(8,128)(2,1)S(1)}, bf16[16,128]{1,0:T(8,128)(2,1)S(1)}) custom-call(s32[1]{0:T(128)} %bitcast.own_ref, s32[6,1,128]{2,1,0:T(1,128)S(1)} %bitcast.18, f32[6,1,128]{2,1,0:T(1,128)S(1)} %bitcast.20, bf16[128,3072]{1,0:T(8,128)(2,1)S(1)} %bitcast.16, bf16[128,3072]{1,0:T(8,128)(2,1)S(1)} %bitcast.17), custom_call_target="tpu_custom_call" | custom-call | flops 25165824 | bytes 1572864 | tf_op jit(solution)/shard_map/pick_rows/pallas_call | solution.py:82
  5.2 3.0 %collective-permute-start.2 = (bf16[16,3072]{1,0:T(8,128)(2,1)S(1)}, bf16[16,3072]{1,0:T(8,128)(2,1)S(1)}, u32[]{:S(2)}, u32[]{:S(2)}) collective-permute-start(bf16[16,3072]{1,0:T(8,128)(2,1)S(1)} %get-tuple-element.22.refs_0_), channel_id=1, source_target_pairs={{0,4},{1,5},{2,6},{3,7},{4,0},{5,1},{6,2},{7,3},{8,12},{9,13},{10,... | collective-permute-start | bytes 294920 | tf_op jit(solution)/shard_map/ppermute | solution.py:30
  8.2 1.5 %collective-permute-start.1 = (bf16[16,3072]{1,0:T(8,128)(2,1)S(1)}, bf16[16,3072]{1,0:T(8,128)(2,1)S(1)}, u32[]{:S(2)}, u32[]{:S(2)}) collective-permute-start(bf16[16,3072]{1,0:T(8,128)(2,1)S(1)} %get-tuple-element.23), channel_id=1, source_target_pairs={{0,1},{1,0},{2,3},{3,2},{4,5},{5,4},{6,7},{7,6},{8,9},{9,8},{10,11... | collective-permute-start | bytes 294920 | tf_op jit(solution)/shard_map/ppermute | solution.py:30
  9.8 1.5 %collective-permute-done.2.refs_2_ = bf16[16,3072]{1,0:T(8,128)(2,1)S(1)} collective-permute-done((bf16[16,3072]{1,0:T(8,128)(2,1)S(1)}, bf16[16,3072]{1,0:T(8,128)(2,1)S(1)}, u32[]{:S(2)}, u32[]{:S(2)}) %collective-permute-start.2) | collective-permute-done | bytes 98336 | tf_op jit(solution)/shard_map/ppermute | solution.py:30
  11.3 2.6 %collective-permute-done.1.refs_1_ = bf16[16,3072]{1,0:T(8,128)(2,1)S(1)} collective-permute-done((bf16[16,3072]{1,0:T(8,128)(2,1)S(1)}, bf16[16,3072]{1,0:T(8,128)(2,1)S(1)}, u32[]{:S(2)}, u32[]{:S(2)}) %collective-permute-start.1) | collective-permute-done | bytes 98336 | tf_op jit(solution)/shard_map/ppermute | solution.py:30
  13.9 1.4 %collective-permute-done.3.refs_3_ = bf16[16,3072]{1,0:T(8,128)(2,1)S(1)} collective-permute-done((bf16[16,3072]{1,0:T(8,128)(2,1)S(1)}, bf16[16,3072]{1,0:T(8,128)(2,1)S(1)}, u32[]{:S(2)}, u32[]{:S(2)}) %collective-permute-start.3) | collective-permute-done | bytes 98336 | tf_op jit(solution)/shard_map/ppermute | solution.py:30
  15.3 1.3 %collective-permute-done.7.refs_7_ = bf16[16,3072]{1,0:T(8,128)(2,1)S(1)} collective-permute-done((bf16[16,3072]{1,0:T(8,128)(2,1)S(1)}, bf16[16,3072]{1,0:T(8,128)(2,1)S(1)}, u32[]{:S(2)}, u32[]{:S(2)}) %collective-permute-start.7) | collective-permute-done | bytes 98336 | tf_op jit(solution)/shard_map/ppermute | solution.py:30
  16.6 1.4 %copy-done.1 = bf16[1,1,3072,256]{3,2,1,0:T(8,128)(2,1)S(1)} copy-done((bf16[1,1,3072,256]{3,2,1,0:T(8,128)(2,1)S(1)}, bf16[1,1,3072,256]{3,2,1,0:T(8,128)(2,1)}, u32[]{:S(2)}) %copy-start.1) | copy-done | bytes 1572888
  18.0 1.4 %copy-done.2 = bf16[1,1,256,3072]{3,2,1,0:T(8,128)(2,1)S(1)} copy-done((bf16[1,1,256,3072]{3,2,1,0:T(8,128)(2,1)S(1)}, bf16[1,1,256,3072]{3,2,1,0:T(8,128)(2,1)}, u32[]{:S(2)}) %copy-start.2) | copy-done | bytes 1572888
  19.4 2.7 %hidden_pass.1 = (f32[32,3072]{1,0:T(8,128)S(1)}, bf16[32,3200]{1,0:T(8,128)(2,1)S(1)}, f32[32,128]{1,0:T(8,128)S(1)}, bf16[128,512]{1,0:T(8,128)(2,1)S(1)}, bf16[128,256]{1,0:T(8,128)(2,1)S(1)}) custom-call(bf16[16,3072]{1,0:T(8,128)(2,1)S(1)} %get-tuple-element.22.refs_0_, bf16[16,3072]{1,0:T(8,128)(2,1)S(1)} %collective-permute-done.1.refs_1_, ...), custom_call_target="tpu_custom_call" | custom-call | flops 1006632960 | bytes 4718592 | tf_op jit(solution)/shard_map/hidden_pass/pallas_call | solution.py:158
  22.4 3.6 %collective-permute-start = (bf16[16,128]{1,0:T(8,128)(2,1)S(1)}, bf16[16,128]{1,0:T(8,128)(2,1)S(1)}, u32[]{:S(2)}, u32[]{:S(2)}) collective-permute-start(bf16[16,128]{1,0:T(8,128)(2,1)S(1)} %get-tuple-element.21.select_ref), channel_id=1, source_target_pairs={{0,24},{1,25},{2,26},{3,27},{4,28},{5,29},{6,30},{7,31},{8,0},{9,1... | collective-permute-start | bytes 12296 | tf_op jit(solution)/shard_map/ppermute | solution.py:41
  26.7 2.1 %collective-permute-start.10 = (bf16[8,3072]{1,0:T(8,128)(2,1)S(1)}, bf16[8,3072]{1,0:T(8,128)(2,1)S(1)}, u32[]{:S(2)}, u32[]{:S(2)}) collective-permute-start(bf16[8,3072]{1,0:T(8,128)(2,1)S(1)} %get-tuple-element.28), channel_id=1, source_target_pairs={{0,28},{1,29},{2,30},{3,31},{4,24},{5,25},{6,26},{7,27},{8,4},{9,5... | collective-permute-start | bytes 147464 | tf_op jit(solution)/shard_map/ppermute | solution.py:41
  28.9 0.9 %collective-permute-start.11 = (bf16[8,3072]{1,0:T(8,128)(2,1)S(1)}, bf16[8,3072]{1,0:T(8,128)(2,1)S(1)}, u32[]{:S(2)}, u32[]{:S(2)}) collective-permute-start(bf16[8,3072]{1,0:T(8,128)(2,1)S(1)} %get-tuple-element.29), channel_id=1, source_target_pairs={{0,25},{1,24},{2,27},{3,26},{4,29},{5,28},{6,31},{7,30},{8,1},{9,0... | collective-permute-start | bytes 147464 | tf_op jit(solution)/shard_map/ppermute | solution.py:41
  29.8 0.9 %collective-permute-start.12 = (bf16[8,3072]{1,0:T(8,128)(2,1)S(1)}, bf16[8,3072]{1,0:T(8,128)(2,1)S(1)}, u32[]{:S(2)}, u32[]{:S(2)}) collective-permute-start(bf16[8,3072]{1,0:T(8,128)(2,1)S(1)} %get-tuple-element.30), channel_id=1, source_target_pairs={{0,29},{1,28},{2,31},{3,30},{4,25},{5,24},{6,27},{7,26},{8,5},{9,4... | collective-permute-start | bytes 147464 | tf_op jit(solution)/shard_map/ppermute | solution.py:41
  30.7 1.1 %collective-permute-start.14 = (f32[8,1]{1,0:T(8,128)S(1)}, f32[8,1]{1,0:T(8,128)S(1)}, u32[]{:S(2)}, u32[]{:S(2)}) collective-permute-start(f32[8,1]{1,0:T(8,128)S(1)} %get-tuple-element.37), channel_id=1, source_target_pairs={{0,1},{1,0},{2,3},{3,2},{4,5},{5,4},{6,7},{7,6},{8,9},{9,8},{10,11... | collective-permute-start | bytes 104 | tf_op jit(solution)/shard_map/ppermute | solution.py:30
  31.9 2.7 %collective-permute-done.14.refs_1_ = f32[8,1]{1,0:T(8,128)S(1)} collective-permute-done((f32[8,1]{1,0:T(8,128)S(1)}, f32[8,1]{1,0:T(8,128)S(1)}, u32[]{:S(2)}, u32[]{:S(2)}) %collective-permute-start.14) | collective-permute-done | bytes 64 | tf_op jit(solution)/shard_map/ppermute | solution.py:30
  34.6 2.5 %collective-permute-start.9 = (bf16[8,3072]{1,0:T(8,128)(2,1)S(1)}, bf16[8,3072]{1,0:T(8,128)(2,1)S(1)}, u32[]{:S(2)}, u32[]{:S(2)}) collective-permute-start(bf16[8,3072]{1,0:T(8,128)(2,1)S(1)} %get-tuple-element.27), channel_id=1, source_target_pairs={{0,24},{1,25},{2,26},{3,27},{4,28},{5,29},{6,30},{7,31},{8,0},{9,1... | collective-permute-start | bytes 147464 | tf_op jit(solution)/shard_map/ppermute | solution.py:41
  37.1 4.0 %weight_grads.1 = (bf16[3072,256]{1,0:T(8,128)(2,1)}, bf16[3072,256]{1,0:T(8,128)(2,1)}, bf16[256,3072]{1,0:T(8,128)(2,1)}) custom-call(bf16[16,3072]{1,0:T(8,128)(2,1)S(1)} %get-tuple-element.22.refs_0_, bf16[16,3072]{1,0:T(8,128)(2,1)S(1)} %collective-permute-done.1.refs_1_, bf16[16,3072]{1,0:T(8,128)(2,1)S(1)} %collective-permute-done.2.refs_2_, ...), custom_call_target="tpu_custom_call" | custom-call | flops 603979776 | bytes 4718592 | tf_op jit(solution)/shard_map/weight_grads/pallas_call | solution.py:221
  41.1 0.7 %score_grads.1 = f32[6,1,128]{2,1,0:T(1,128)} custom-call(s32[1]{0:T(128)} %bitcast.own_ref, s32[6,1,128]{2,1,0:T(1,128)S(1)} %bitcast.19, f32[6,1,128]{2,1,0:T(1,128)S(1)} %bitcast.21, bf16[16,128]{1,0:T(8,128)(2,1)S(1)} %get-tuple-element.21.select_ref, f32[8,1]{1,0:T(8,128)S(1)} %get-tuple-element.38.refs_0_, f32[8,1]{1,0:T(8,128)S(1)} %collective-permute-done.14.refs_1_), custom_call_target="tpu_custom_call" | custom-call | flops 1000 | bytes 1000 | tf_op jit(solution)/shard_map/score_grads/pallas_call | solution.py:258
  41.8 1.3 %spread_rows.1 = bf16[128,3072]{1,0:T(8,128)(2,1)} custom-call(bf16[16,128]{1,0:T(8,128)(2,1)S(1)} %collective-permute-done.select_ref, bf16[8,3072]{1,0:T(8,128)(2,1)S(1)} %collective-permute-done.9.refs_0_, bf16[8,3072]{1,0:T(8,128)(2,1)S(1)} %collective-permute-done.10.refs_1_, bf16[8,3072]{1,0:T(8,128)(2,1)S(1)} %collective-permute-done.11.refs_2_, ...), custom_call_target="tpu_custom_call" | custom-call | flops 12582912 | bytes 786432 | tf_op jit(solution)/shard_map/spread_rows/pallas_call | solution.py:288
  (32 shorter events, 1.1 us)
Async XLA Ops:
  0.6 15.9 %copy-start = (bf16[1,1,3072,256]{3,2,1,0:T(8,128)(2,1)S(1)}, bf16[1,1,3072,256]{3,2,1,0:T(8,128)(2,1)}, u32[]{:S(2)}) copy-start(bf16[1,1,3072,256]{3,2,1,0:T(8,128)(2,1)} %param.11) | copy-start | bytes 4718596
  0.6 1.3 %copy-start.3 = (bf16[1,128,3072]{2,1,0:T(8,128)(2,1)S(1)}, bf16[1,128,3072]{2,1,0:T(8,128)(2,1)}, u32[]{:S(2)}) copy-start(bf16[1,128,3072]{2,1,0:T(8,128)(2,1)} %param.7) | copy-start | bytes 2359300
  1.9 1.1 %copy-start.4 = (bf16[1,128,3072]{2,1,0:T(8,128)(2,1)S(1)}, bf16[1,128,3072]{2,1,0:T(8,128)(2,1)}, u32[]{:S(2)}) copy-start(bf16[1,128,3072]{2,1,0:T(8,128)(2,1)} %param.8) | copy-start | bytes 2359300
  3.0 0.7 %copy-start.5 = (s32[1,128,6]{1,0,2:T(1,128)S(1)}, s32[1,128,6]{1,0,2:T(1,128)}, u32[]{:S(2)}) copy-start(s32[1,128,6]{1,0,2:T(1,128)} %param.9) | copy-start | bytes 9220
  3.7 0.7 %copy-start.7 = (f32[1,128,6]{1,0,2:T(1,128)S(1)}, f32[1,128,6]{1,0,2:T(1,128)}, u32[]{:S(2)}) copy-start(f32[1,128,6]{1,0,2:T(1,128)} %param.10) | copy-start | bytes 9220
  5.2 6.1 %collective-permute-start.2 = (bf16[16,3072]{1,0:T(8,128)(2,1)S(1)}, bf16[16,3072]{1,0:T(8,128)(2,1)S(1)}, u32[]{:S(2)}, u32[]{:S(2)}) collective-permute-start(bf16[16,3072]{1,0:T(8,128)(2,1)S(1)} %get-tuple-element.22.refs_0_), channel_id=1, source_target_pairs={{0,4},{1,5},{2,6},{3,7},{4,0},{5,1},{6,2},{7,3},{8,12},{9,13},{10,... | collective-permute-start | bytes 294920 | tf_op jit(solution)/shard_map/ppermute | solution.py:30
  8.2 5.7 %collective-permute-start.1 = (bf16[16,3072]{1,0:T(8,128)(2,1)S(1)}, bf16[16,3072]{1,0:T(8,128)(2,1)S(1)}, u32[]{:S(2)}, u32[]{:S(2)}) collective-permute-start(bf16[16,3072]{1,0:T(8,128)(2,1)S(1)} %get-tuple-element.23), channel_id=1, source_target_pairs={{0,1},{1,0},{2,3},{3,2},{4,5},{5,4},{6,7},{7,6},{8,9},{9,8},{10,11... | collective-permute-start | bytes 294920 | tf_op jit(solution)/shard_map/ppermute | solution.py:30
  9.7 5.5 %collective-permute-start.3 = (bf16[16,3072]{1,0:T(8,128)(2,1)S(1)}, bf16[16,3072]{1,0:T(8,128)(2,1)S(1)}, u32[]{:S(2)}, u32[]{:S(2)}) collective-permute-start(bf16[16,3072]{1,0:T(8,128)(2,1)S(1)} %get-tuple-element.23), channel_id=1, source_target_pairs={{0,5},{1,4},{2,7},{3,6},{4,1},{5,0},{6,3},{7,2},{8,13},{9,12},{10,... | collective-permute-start | bytes 294920 | tf_op jit(solution)/shard_map/ppermute | solution.py:30
  9.8 5.5 %collective-permute-start.4 = (bf16[16,3072]{1,0:T(8,128)(2,1)S(1)}, bf16[16,3072]{1,0:T(8,128)(2,1)S(1)}, u32[]{:S(2)}, u32[]{:S(2)}) collective-permute-start(bf16[16,3072]{1,0:T(8,128)(2,1)S(1)} %get-tuple-element.22.refs_0_), channel_id=1, source_target_pairs={{0,2},{1,3},{2,0},{3,1},{4,6},{5,7},{6,4},{7,5},{8,10},{9,11},{10,... | collective-permute-start | bytes 294920 | tf_op jit(solution)/shard_map/ppermute | solution.py:30
  11.3 4.0 %collective-permute-start.6 = (bf16[16,3072]{1,0:T(8,128)(2,1)S(1)}, bf16[16,3072]{1,0:T(8,128)(2,1)S(1)}, u32[]{:S(2)}, u32[]{:S(2)}) collective-permute-start(bf16[16,3072]{1,0:T(8,128)(2,1)S(1)} %collective-permute-done.2.refs_2_), channel_id=1, source_target_pairs={{0,2},{1,3},{2,0},{3,1},{4,6},{5,7},{6,4},{7,5},{8,10},{9,11},{10,... | collective-permute-start | bytes 294920 | tf_op jit(solution)/shard_map/ppermute | solution.py:30
  13.9 1.4 %collective-permute-start.5 = (bf16[16,3072]{1,0:T(8,128)(2,1)S(1)}, bf16[16,3072]{1,0:T(8,128)(2,1)S(1)}, u32[]{:S(2)}, u32[]{:S(2)}) collective-permute-start(bf16[16,3072]{1,0:T(8,128)(2,1)S(1)} %collective-permute-done.1.refs_1_), channel_id=1, source_target_pairs={{0,2},{1,3},{2,0},{3,1},{4,6},{5,7},{6,4},{7,5},{8,10},{9,11},{10,... | collective-permute-start | bytes 294920 | tf_op jit(solution)/shard_map/ppermute | solution.py:30
  15.3 1.3 %collective-permute-start.7 = (bf16[16,3072]{1,0:T(8,128)(2,1)S(1)}, bf16[16,3072]{1,0:T(8,128)(2,1)S(1)}, u32[]{:S(2)}, u32[]{:S(2)}) collective-permute-start(bf16[16,3072]{1,0:T(8,128)(2,1)S(1)} %collective-permute-done.3.refs_3_), channel_id=1, source_target_pairs={{0,2},{1,3},{2,0},{3,1},{4,6},{5,7},{6,4},{7,5},{8,10},{9,11},{10,... | collective-permute-start | bytes 294920 | tf_op jit(solution)/shard_map/ppermute | solution.py:30
  16.6 1.4 %copy-start.1 = (bf16[1,1,3072,256]{3,2,1,0:T(8,128)(2,1)S(1)}, bf16[1,1,3072,256]{3,2,1,0:T(8,128)(2,1)}, u32[]{:S(2)}) copy-start(bf16[1,1,3072,256]{3,2,1,0:T(8,128)(2,1)} %param.12) | copy-start | bytes 4718596
  18.0 1.4 %copy-start.2 = (bf16[1,1,256,3072]{3,2,1,0:T(8,128)(2,1)S(1)}, bf16[1,1,256,3072]{3,2,1,0:T(8,128)(2,1)}, u32[]{:S(2)}) copy-start(bf16[1,1,256,3072]{3,2,1,0:T(8,128)(2,1)} %param.13) | copy-start | bytes 4718596
  22.1 19.0 %copy-start.6 = (s32[1,128,6]{1,0,2:T(1,128)S(1)}, s32[1,128,6]{1,0,2:T(1,128)}, u32[]{:S(2)}) copy-start(s32[1,128,6]{1,0,2:T(1,128)} %param.9) | copy-start | bytes 9220
  22.1 19.0 %copy-start.8 = (f32[1,128,6]{1,0,2:T(1,128)S(1)}, f32[1,128,6]{1,0,2:T(1,128)}, u32[]{:S(2)}) copy-start(f32[1,128,6]{1,0,2:T(1,128)} %param.10) | copy-start | bytes 9220
  22.1 3.8 %collective-permute-start.8 = (bf16[32,3200]{1,0:T(8,128)(2,1)S(1)}, bf16[32,3200]{1,0:T(8,128)(2,1)S(1)}, u32[]{:S(2)}, u32[]{:S(2)}) collective-permute-start(bf16[32,3200]{1,0:T(8,128)(2,1)S(1)} %get-tuple-element.26), channel_id=1, source_target_pairs={{0,2},{1,3},{2,0},{3,1},{4,6},{5,7},{6,4},{7,5},{8,10},{9,11},{10,... | collective-permute-start | bytes 614408 | tf_op jit(solution)/shard_map/ppermute | solution.py:30
  22.4 19.4 %collective-permute-start = (bf16[16,128]{1,0:T(8,128)(2,1)S(1)}, bf16[16,128]{1,0:T(8,128)(2,1)S(1)}, u32[]{:S(2)}, u32[]{:S(2)}) collective-permute-start(bf16[16,128]{1,0:T(8,128)(2,1)S(1)} %get-tuple-element.21.select_ref), channel_id=1, source_target_pairs={{0,24},{1,25},{2,26},{3,27},{4,28},{5,29},{6,30},{7,31},{8,0},{9,1... | collective-permute-start | bytes 12296 | tf_op jit(solution)/shard_map/ppermute | solution.py:41
  26.1 4.6 %collective-permute-start.13 = (f32[16,1]{1,0:T(8,128)S(1)}, f32[16,1]{1,0:T(8,128)S(1)}, u32[]{:S(2)}, u32[]{:S(2)}) collective-permute-start(f32[16,1]{1,0:T(8,128)S(1)} %concatenate.3), channel_id=1, source_target_pairs={{0,4},{1,5},{2,6},{3,7},{4,0},{5,1},{6,2},{7,3},{8,12},{9,13},{10,... | collective-permute-start | bytes 200 | tf_op jit(solution)/shard_map/ppermute | solution.py:30
  26.7 15.0 %collective-permute-start.10 = (bf16[8,3072]{1,0:T(8,128)(2,1)S(1)}, bf16[8,3072]{1,0:T(8,128)(2,1)S(1)}, u32[]{:S(2)}, u32[]{:S(2)}) collective-permute-start(bf16[8,3072]{1,0:T(8,128)(2,1)S(1)} %get-tuple-element.28), channel_id=1, source_target_pairs={{0,28},{1,29},{2,30},{3,31},{4,24},{5,25},{6,26},{7,27},{8,4},{9,5... | collective-permute-start | bytes 147464 | tf_op jit(solution)/shard_map/ppermute | solution.py:41
  28.9 12.9 %collective-permute-start.11 = (bf16[8,3072]{1,0:T(8,128)(2,1)S(1)}, bf16[8,3072]{1,0:T(8,128)(2,1)S(1)}, u32[]{:S(2)}, u32[]{:S(2)}) collective-permute-start(bf16[8,3072]{1,0:T(8,128)(2,1)S(1)} %get-tuple-element.29), channel_id=1, source_target_pairs={{0,25},{1,24},{2,27},{3,26},{4,29},{5,28},{6,31},{7,30},{8,1},{9,0... | collective-permute-start | bytes 147464 | tf_op jit(solution)/shard_map/ppermute | solution.py:41
  29.8 12.0 %collective-permute-start.12 = (bf16[8,3072]{1,0:T(8,128)(2,1)S(1)}, bf16[8,3072]{1,0:T(8,128)(2,1)S(1)}, u32[]{:S(2)}, u32[]{:S(2)}) collective-permute-start(bf16[8,3072]{1,0:T(8,128)(2,1)S(1)} %get-tuple-element.30), channel_id=1, source_target_pairs={{0,29},{1,28},{2,31},{3,30},{4,25},{5,24},{6,27},{7,26},{8,5},{9,4... | collective-permute-start | bytes 147464 | tf_op jit(solution)/shard_map/ppermute | solution.py:41
  30.7 3.8 %collective-permute-start.14 = (f32[8,1]{1,0:T(8,128)S(1)}, f32[8,1]{1,0:T(8,128)S(1)}, u32[]{:S(2)}, u32[]{:S(2)}) collective-permute-start(f32[8,1]{1,0:T(8,128)S(1)} %get-tuple-element.37), channel_id=1, source_target_pairs={{0,1},{1,0},{2,3},{3,2},{4,5},{5,4},{6,7},{7,6},{8,9},{9,8},{10,11... | collective-permute-start | bytes 104 | tf_op jit(solution)/shard_map/ppermute | solution.py:30
  34.6 7.2 %collective-permute-start.9 = (bf16[8,3072]{1,0:T(8,128)(2,1)S(1)}, bf16[8,3072]{1,0:T(8,128)(2,1)S(1)}, u32[]{:S(2)}, u32[]{:S(2)}) collective-permute-start(bf16[8,3072]{1,0:T(8,128)(2,1)S(1)} %get-tuple-element.27), channel_id=1, source_target_pairs={{0,24},{1,25},{2,26},{3,27},{4,28},{5,29},{6,30},{7,31},{8,0},{9,1... | collective-permute-start | bytes 147464 | tf_op jit(solution)/shard_map/ppermute | solution.py:41

commit v2 on v1

--- a/solution.py
+++ b/solution.py
@@ -7,10 +7,11 @@
 from jax.experimental.pallas import tpu as pltpu
 from jax.sharding import PartitionSpec as P
 
+
 PAIRWISE_MAX = 8
 LANES = 128
 VMEM = pl.BlockSpec(memory_space=pltpu.VMEM)
-ANY = pl.BlockSpec(memory_space=pl.ANY)
+HBM = pl.BlockSpec(memory_space=pltpu.HBM)
 
 
 def shape_of(shape, dtype):
@@ -30,76 +31,110 @@
     return lax.ppermute(value, ("dp", "expert"), [(i, i ^ offset) for i in range(count)])
 
 
-def swap_back(value, offset):
+def send_back(value, across):
     sections = lax.axis_size("pipe")
-    count = lax.axis_size("dp") * lax.axis_size("expert")
-    pairs = [
-        (s * count + i, ((s - 1) % sections) * count + (i ^ offset))
-        for s in range(sections)
-        for i in range(count)
+    chips = lax.axis_size("dp") // 2
+    pairs = []
+    for s in range(sections):
+        for x in range(chips):
+            for core in range(2):
+                for expert in range(2):
+                    source = (s * chips + x) * 4 + 2 * core + expert
+                    target = (((s - 1) % sections) * chips + (x ^ across)) * 4 + 2 * expert + core
+                    pairs.append((source, target))
+    return lax.ppermute(value, ("pipe", "dp", "expert"), pairs)
+
+
+def pick_kernel(capacity, own_ref, ids_hbm, weight_hbm, acts_hbm, grad_hbm, *refs):
+    outs = refs[:2]
+    select_ref, ids_ref, weight_ref, acts_ref, grad_ref, sems = refs[2:]
+    copies = [
+        pltpu.make_async_copy(source, target, sems.at[i])
+        for i, (source, target) in enumerate(
+            [(ids_hbm, ids_ref), (weight_hbm, weight_ref), (acts_hbm, acts_ref), (grad_hbm, grad_ref)]
+        )
     ]
-    return lax.ppermute(value, ("pipe", "dp", "expert"), pairs)
-
-
-def pick_kernel(capacity, groups, own_ref, ids_ref, weight_ref, acts_ref, grad_ref, *refs):
-    outs = refs[:groups]
-    select_ref, acts_buf, grad_buf, sems = refs[groups:]
-    acts_copy = pltpu.make_async_copy(acts_ref, acts_buf, sems.at[0])
-    grad_copy = pltpu.make_async_copy(grad_ref, grad_buf, sems.at[1])
-    acts_copy.start()
-    grad_copy.start()
+    for copy in copies:
+        copy.start()
     chosen, _, tokens = ids_ref.shape
-    rows = groups * capacity
+    width = acts_ref.shape[1]
+    rows = 2 * capacity
     row = lax.broadcasted_iota(jnp.int32, (rows, tokens), 0)
     row_expert = (row // capacity) ^ own_ref[0]
+    before = lax.broadcasted_iota(jnp.int32, (tokens, tokens), 0)
+    after = lax.broadcasted_iota(jnp.int32, (tokens, tokens), 1)
+    earlier = jnp.where(before < after, 1.0, 0.0).astype(jnp.bfloat16)
+    slot = (row % capacity).astype(jnp.float32)
+    token = lax.broadcasted_iota(jnp.int32, (rows, tokens), 1).astype(jnp.float32)
+    lane = lax.broadcasted_iota(jnp.int32, (rows, LANES), 1)
     taken = jnp.zeros((rows, tokens), jnp.float32)
     scale = jnp.zeros((rows, tokens), jnp.float32)
+    copies[0].wait()
+    copies[1].wait()
     for k in range(chosen):
         same = ids_ref[k] == row_expert
         taken = jnp.where(same, 1.0, taken)
         scale = jnp.where(same, weight_ref[k], scale)
-    before = lax.broadcasted_iota(jnp.int32, (tokens, tokens), 0)
-    after = lax.broadcasted_iota(jnp.int32, (tokens, tokens), 1)
-    earlier = jnp.where(before < after, 1.0, 0.0).astype(jnp.bfloat16)
     rank = jnp.dot(taken.astype(jnp.bfloat16), earlier, preferred_element_type=jnp.float32)
-    slot = (row % capacity).astype(jnp.float32)
     select = jnp.where(rank == slot, taken, 0.0)
     row_scale = jnp.sum(select * scale, axis=1, keepdims=True)
+    number = jnp.sum(select * (token + 1.0), axis=1, keepdims=True)
+    high = jnp.floor(number / 256.0)
+    marks = jnp.where(lane == 0, high, jnp.where(lane == 1, number - 256.0 * high, 0.0))
     select = select.astype(jnp.bfloat16)
     select_ref[...] = select
-    acts_copy.wait()
-    acts_rows = jnp.dot(select, acts_buf[...], preferred_element_type=jnp.float32)
-    grad_copy.wait()
-    grad_rows = jnp.dot(select, grad_buf[...], preferred_element_type=jnp.float32) * row_scale
-    for j in range(groups):
+    copies[2].wait()
+    acts_rows = jnp.dot(select, acts_ref[...], preferred_element_type=jnp.float32)
+    copies[3].wait()
+    grad_rows = jnp.dot(select, grad_ref[...], preferred_element_type=jnp.float32) * row_scale
+    for j in range(2):
         part = slice(j * capacity, (j + 1) * capacity)
-        outs[j][...] = jnp.concatenate([acts_rows[part], grad_rows[part]], axis=0).astype(jnp.bfloat16)
-
-
-def pick_rows(own, ids, weights, acts, grads, groups, capacity):
+        outs[j][:, :width] = jnp.concatenate([acts_rows[part], grad_rows[part]], axis=0).astype(jnp.bfloat16)
+        outs[j][:, width:] = jnp.concatenate([marks[part]] * 2, axis=0).astype(jnp.bfloat16)
+
+
+def pick_rows(own, ids, weights, acts, grads, capacity):
     tokens, width = acts.shape
-    group = shape_of((2 * capacity, width), jnp.bfloat16)
-    return pl.pallas_call(
-        functools.partial(pick_kernel, capacity, groups),
-        out_shape=[group] * groups + [shape_of((groups * capacity, tokens), jnp.bfloat16)],
-        in_specs=[pl.BlockSpec(memory_space=pltpu.SMEM), VMEM, VMEM, ANY, ANY],
-        out_specs=[VMEM] * (groups + 1),
+    group = shape_of((2 * capacity, width + LANES), jnp.bfloat16)
+    return pl.pallas_call(
+        functools.partial(pick_kernel, capacity),
+        out_shape=[group, group, shape_of((2 * capacity, tokens), jnp.bfloat16)],
+        in_specs=[pl.BlockSpec(memory_space=pltpu.SMEM)] + [HBM] * 4,
+        out_specs=[VMEM] * 3,
         scratch_shapes=[
+            pltpu.VMEM(ids.shape, jnp.int32),
+            pltpu.VMEM(weights.shape, jnp.float32),
             pltpu.VMEM((tokens, width), jnp.bfloat16),
             pltpu.VMEM((tokens, width), jnp.bfloat16),
-            pltpu.SemaphoreType.DMA((2,)),
+            pltpu.SemaphoreType.DMA((4,)),
         ],
-        cost_estimate=cost(4 * groups * capacity * tokens * width, 4 * tokens * width),
+        cost_estimate=cost(8 * capacity * tokens * width, 4 * tokens * width),
         compiler_params=pltpu.CompilerParams(vmem_limit_bytes=16 * 2**20),
         name="pick_rows",
     )(own, ids, weights, acts, grads)
 
 
-def split_rows(value, capacity):
-    pieces = value.shape[0] // (2 * capacity)
-    upper = [value[2 * p * capacity : (2 * p + 1) * capacity] for p in range(pieces)]
-    lower = [value[(2 * p + 1) * capacity : (2 * p + 2) * capacity] for p in range(pieces)]
-    return jnp.concatenate(upper, axis=0), jnp.concatenate(lower, axis=0)
+def load_kernel(gate_hbm, upper_hbm, gate_ref, upper_ref, sems):
+    gate_copy = pltpu.make_async_copy(gate_hbm, gate_ref, sems.at[0])
+    upper_copy = pltpu.make_async_copy(upper_hbm.at[: upper_ref.shape[0]], upper_ref, sems.at[1])
+    gate_copy.start()
+    upper_copy.start()
+    gate_copy.wait()
+    upper_copy.wait()
+
+
+def load_weights(gate, upper):
+    width, units = gate.shape
+    return pl.pallas_call(
+        load_kernel,
+        out_shape=[shape_of((width, units), gate.dtype), shape_of((width // 2, units), upper.dtype)],
+        in_specs=[HBM] * 2,
+        out_specs=[VMEM] * 2,
+        scratch_shapes=[pltpu.SemaphoreType.DMA((2,))],
+        cost_estimate=cost(0, 3 * width * units),
+        compiler_params=pltpu.CompilerParams(vmem_limit_bytes=24 * 2**20),
+        name="load_weights",
+    )(gate, upper)
 
 
 def weave(value, capacity, upper):
@@ -111,32 +146,70 @@
     return jnp.concatenate(parts, axis=0)
 
 
-def hidden_kernel(capacity, pieces, *refs):
+def hidden_kernel(capacity, offsets, swapped_ref, *refs):
+    pieces = len(offsets)
     piece_refs = refs[:pieces]
-    gate_ref, upper_ref, lower_ref = refs[pieces : pieces + 3]
-    keep_ref, send_ref, score_ref, delta_ref, hidden_ref = refs[pieces + 3 :]
-    rows = jnp.concatenate([ref[...] for ref in piece_refs], axis=0)
+    gate_ref, head_ref, upper_hbm, lower_hbm = refs[pieces : pieces + 4]
+    keep_ref, send_ref, score_ref, delta_ref, hidden_ref, tail_ref, lower_ref, sems = refs[pieces + 4 :]
+    width, units = gate_ref.shape
+    middle_row = head_ref.shape[0]
+    tail_copy = pltpu.make_async_copy(upper_hbm.at[middle_row:], tail_ref, sems.at[0])
+    lower_copy = pltpu.make_async_copy(lower_hbm, lower_ref, sems.at[1])
+    tail_copy.start()
+    lower_copy.start()
+    half = keep_ref.shape[0]
     across = (((1,), (1,)), ((), ()))
-    gate_pre, _ = split_rows(jnp.dot(rows, gate_ref[...], preferred_element_type=jnp.float32), capacity)
-    up_value, _ = split_rows(jnp.dot(rows, upper_ref[...], preferred_element_type=jnp.float32), capacity)
-    _, grad_hidden = split_rows(
-        lax.dot_general(rows, lower_ref[...], across, preferred_element_type=jnp.float32), capacity
-    )
+
+    def rows(start, stop):
+        return jnp.concatenate([ref[:, start:stop] for ref in piece_refs], axis=0)
+
+    def upper_rows(value):
+        return jnp.concatenate(
+            [value[2 * p * capacity : (2 * p + 1) * capacity] for p in range(pieces)], axis=0
+        )
+
+    def lower_rows(value):
+        return jnp.concatenate(
+            [value[(2 * p + 1) * capacity : (2 * p + 2) * capacity] for p in range(pieces)], axis=0
+        )
+
+    def order(value, wanted):
+        lists = [
+            jnp.concatenate(
+                [value[offsets.index(o) * capacity : (offsets.index(o) + 1) * capacity] for o in chosen], axis=0
+            )
+            for chosen in wanted
+        ]
+        return jnp.where(swapped_ref[0] == 1, lists[1], lists[0])
+
+    chips = [4 * x for x in range(pieces // 4)]
+    kept = ([x | c for x in chips for c in (0, 2)], [x | c | 1 for x in chips for c in (2, 0)])
+    sent = ([x | c | 1 for x in chips for c in (0, 2)], [x | c for x in chips for c in (2, 0)])
+    gate_pre = upper_rows(jnp.dot(rows(0, width), gate_ref[...], preferred_element_type=jnp.float32))
+    up_value = jnp.dot(rows(0, middle_row), head_ref[...], preferred_element_type=jnp.float32)
+    tail_copy.wait()
+    up_value = upper_rows(
+        up_value + jnp.dot(rows(middle_row, width), tail_ref[...], preferred_element_type=jnp.float32)
+    )
+    lower_copy.wait()
+    grad_hidden = lower_rows(lax.dot_general(rows(0, width), lower_ref[...], across, preferred_element_type=jnp.float32))
     sigma_gate = jax.nn.sigmoid(gate_pre)
     swish = gate_pre * sigma_gate
     hidden = swish * up_value
     scores = jnp.sum(hidden * grad_hidden, axis=1, keepdims=True)
     delta_gate = grad_hidden * up_value * sigma_gate * (1.0 + gate_pre * (1.0 - sigma_gate))
     delta_up = grad_hidden * swish
-    partial_rows = lax.dot_general(
-        delta_gate.astype(jnp.bfloat16), gate_ref[...], across, preferred_element_type=jnp.float32
-    ) + lax.dot_general(
-        delta_up.astype(jnp.bfloat16), upper_ref[...], across, preferred_element_type=jnp.float32
-    )
-    half, width = keep_ref.shape
-    units = gate_ref.shape[1]
-    keep_ref[...] = partial_rows[:half]
-    send_ref[:, :width] = partial_rows[half:].astype(jnp.bfloat16)
+
+    marks = jnp.concatenate([ref[:, width:].astype(jnp.float32)[:capacity] for ref in piece_refs], axis=0)
+    gate_rows = jnp.concatenate([order(delta_gate, kept), order(delta_gate, sent)]).astype(jnp.bfloat16)
+    upper_part = jnp.concatenate([order(delta_up, kept), order(delta_up, sent)]).astype(jnp.bfloat16)
+    for part, ref in ((slice(0, middle_row), head_ref), (slice(middle_row, width), tail_ref)):
+        partial_rows = lax.dot_general(
+            gate_rows, gate_ref[part], across, preferred_element_type=jnp.float32
+        ) + lax.dot_general(upper_part, ref[...], across, preferred_element_type=jnp.float32)
+        keep_ref[:, part] = partial_rows[:half]
+        send_ref[:, part] = partial_rows[half:].astype(jnp.bfloat16)
+    keep_ref[:, width:] = order(marks, kept)
     score_ref[...] = jnp.broadcast_to(scores[:half], (half, LANES))
     rest = scores[half:]
     high = rest.astype(jnp.bfloat16).astype(jnp.float32)
@@ -150,46 +223,53 @@
     hidden_ref[...] = weave(hidden, capacity, False).astype(jnp.bfloat16)
 
 
-def hidden_pass(pieces, gate, upper, lower, capacity):
+def hidden_pass(swapped, pieces, offsets, gate, head, upper, lower, capacity):
     width, units = gate.shape
     count = len(pieces)
     half = count * capacity // 2
     rows = 2 * count * capacity
     return pl.pallas_call(
-        functools.partial(hidden_kernel, capacity, count),
+        functools.partial(hidden_kernel, capacity, offsets),
         out_shape=[
-            shape_of((half, width), jnp.float32),
+            shape_of((half, width + LANES), jnp.float32),
             shape_of((half, width + LANES), jnp.bfloat16),
             shape_of((half, LANES), jnp.float32),
             shape_of((rows, 2 * units), jnp.bfloat16),
             shape_of((rows, units), jnp.bfloat16),
         ],
-        in_specs=[VMEM] * (count + 3),
+        in_specs=[pl.BlockSpec(memory_space=pltpu.SMEM)] + [VMEM] * (count + 2) + [HBM] * 2,
         out_specs=[VMEM] * 5,
+        scratch_shapes=[
+            pltpu.VMEM((width - head.shape[0], units), jnp.bfloat16),
+            pltpu.VMEM((units, width), jnp.bfloat16),
+            pltpu.SemaphoreType.DMA((2,)),
+        ],
         cost_estimate=cost(10 * rows * width * units, 6 * width * units),
         compiler_params=pltpu.CompilerParams(vmem_limit_bytes=24 * 2**20),
         name="hidden_pass",
-    )(*pieces, gate, upper, lower)
-
-
-def join_kernel(capacity, groups, keep_ref, score_ref, recv_ref, *out_refs):
-    width = keep_ref.shape[1]
-    for j in range(groups):
-        part = slice(j * capacity, (j + 1) * capacity)
+    )(swapped, *pieces, gate, head, upper, lower)
+
+
+def join_kernel(width, messages, keep_ref, score_ref, recv_ref, *out_refs):
+    for j in range(messages):
+        rows = out_refs[j].shape[0]
+        part = slice(j * rows, (j + 1) * rows)
         other = recv_ref[part, :width].astype(jnp.float32)
-        out_refs[j][...] = (keep_ref[part] + other).astype(jnp.bfloat16)
+        out_refs[j][:, :width] = (keep_ref[part, :width] + other).astype(jnp.bfloat16)
+        out_refs[j][:, width:] = keep_ref[part, width:].astype(jnp.bfloat16)
     extra = recv_ref[:, width:].astype(jnp.float32)
-    out_refs[groups][...] = score_ref[...] + jnp.sum(extra, axis=1, keepdims=True)
-
-
-def join_cores(keep, scores, recv, groups, capacity):
-    half, width = keep.shape
-    return pl.pallas_call(
-        functools.partial(join_kernel, capacity, groups),
-        out_shape=[shape_of((capacity, width), jnp.bfloat16)] * groups + [shape_of((half, LANES), jnp.float32)],
+    out_refs[messages][...] = score_ref[...] + jnp.sum(extra, axis=1, keepdims=True)
+
+
+def join_cores(keep, scores, recv, messages):
+    half, wide = keep.shape
+    return pl.pallas_call(
+        functools.partial(join_kernel, wide - LANES, messages),
+        out_shape=[shape_of((half // messages, wide), jnp.bfloat16)] * messages
+        + [shape_of((half, LANES), jnp.float32)],
         in_specs=[VMEM] * 3,
-        out_specs=[VMEM] * (groups + 1),
-        cost_estimate=cost(2 * half * width, 8 * half * width),
+        out_specs=[VMEM] * (messages + 1),
+        cost_estimate=cost(2 * half * wide, 8 * half * wide),
         compiler_params=pltpu.CompilerParams(vmem_limit_bytes=8 * 2**20),
         name="join_cores",
     )(keep, scores, recv)
@@ -211,7 +291,7 @@
 
 
 def weight_grads(pieces, delta, hidden, step):
-    width = pieces[0].shape[1]
+    width = pieces[0].shape[1] - LANES
     rows, units = hidden.shape
     count = len(pieces)
 
@@ -238,27 +318,26 @@
     )(*pieces, delta, hidden)
 
 
-def score_kernel(capacity, groups, own_ref, ids_ref, weight_ref, select_ref, *refs):
+def score_kernel(capacity, own_ref, ids_ref, weight_ref, select_ref, *refs):
     out_ref = refs[-1]
     chosen, _, tokens = ids_ref.shape
     sums = []
-    for j in range(groups):
+    for j in range(2):
         part = slice(j * capacity, (j + 1) * capacity)
         picked = select_ref[part].astype(jnp.float32) * refs[j][:, :1]
         sums.append(jnp.sum(picked, axis=0, keepdims=True))
     for k in range(chosen):
         value = jnp.zeros((1, tokens), jnp.float32)
-        for j in range(groups):
+        for j in range(2):
             value = jnp.where(ids_ref[k] == (own_ref[0] ^ j), sums[j], value)
         out_ref[k] = value / weight_ref[k]
 
 
 def score_grads(own, ids, weights, select, scores, capacity):
-    groups = len(scores)
-    return pl.pallas_call(
-        functools.partial(score_kernel, capacity, groups),
+    return pl.pallas_call(
+        functools.partial(score_kernel, capacity),
         out_shape=shape_of(weights.shape, jnp.float32),
-        in_specs=[pl.BlockSpec(memory_space=pltpu.SMEM)] + [VMEM] * (3 + groups),
+        in_specs=[pl.BlockSpec(memory_space=pltpu.SMEM)] + [VMEM] * 5,
         out_specs=VMEM,
         cost_estimate=cost(1000, 1000),
         compiler_params=pltpu.CompilerParams(vmem_limit_bytes=4 * 2**20),
@@ -266,82 +345,113 @@
     )(own, ids, weights, select, *scores)
 
 
-def spread_kernel(groups, terms, select_ref, *refs):
-    out_ref = refs[-1]
-    sums = []
-    for j in range(groups):
-        total = refs[j * terms][...].astype(jnp.float32)
-        for term in range(1, terms):
-            total = total + refs[j * terms + term][...].astype(jnp.float32)
-        sums.append(total)
-    slot_grad = jnp.concatenate(sums, axis=0).astype(jnp.bfloat16)
+def total_kernel(messages, *refs):
+    own_ref, other_ref = refs[messages:]
+    capacity, wide = own_ref.shape
+    width = wide - LANES
+    total = refs[0][:, :width].astype(jnp.float32)
+    for ref in refs[1:messages]:
+        total = total + ref[:, :width].astype(jnp.float32)
+    marks = refs[0][:, width:].astype(jnp.float32)
+    own_ref[:, :width] = total[:capacity].astype(jnp.bfloat16)
+    own_ref[:, width:] = marks[:capacity].astype(jnp.bfloat16)
+    other_ref[:, :width] = total[capacity:].astype(jnp.bfloat16)
+    other_ref[:, width:] = marks[capacity:].astype(jnp.bfloat16)
+
+
+def total_rows(arrays):
+    rows, wide = arrays[0].shape
+    return pl.pallas_call(
+        functools.partial(total_kernel, len(arrays)),
+        out_shape=[shape_of((rows // 2, wide), jnp.bfloat16)] * 2,
+        in_specs=[VMEM] * len(arrays),
+        out_specs=[VMEM] * 2,
+        cost_estimate=cost(rows * wide, 4 * rows * wide),
+        compiler_params=pltpu.CompilerParams(vmem_limit_bytes=4 * 2**20),
+        name="total_rows",
+    )(*arrays)
+
+
+def spread_kernel(step, own_ref, other_ref, out_ref):
+    tokens = out_ref.shape[0]
+    capacity, wide = own_ref.shape
+    width = wide - LANES
+    start = pl.multiple_of(pl.program_id(0) * step, step)
+    marks = jnp.concatenate([ref[:, width:].astype(jnp.float32) for ref in (own_ref, other_ref)], axis=0)
+    lane = lax.broadcasted_iota(jnp.int32, marks.shape, 1)
+    number = jnp.sum(jnp.where(lane == 0, marks * 256.0, jnp.where(lane == 1, marks, 0.0)), axis=1, keepdims=True)
+    token = lax.broadcasted_iota(jnp.int32, (2 * capacity, tokens), 1).astype(jnp.float32)
+    select = jnp.where(token + 1.0 == number, 1.0, 0.0).astype(jnp.bfloat16)
+    rows = jnp.concatenate(
+        [ref[:, pl.ds(start, step)].astype(jnp.float32) for ref in (own_ref, other_ref)], axis=0
+    ).astype(jnp.bfloat16)
     out_ref[...] = lax.dot_general(
-        select_ref[...], slot_grad, (((0,), (0,)), ((), ())), preferred_element_type=jnp.float32
-    ).astype(jnp.bfloat16)
-
-
-def spread_rows(select, groups, step):
-    tokens = select.shape[1]
-    capacity, width = groups[0][0].shape
-    terms = len(groups[0])
-    flat = [array for group in groups for array in group]
-    return pl.pallas_call(
-        functools.partial(spread_kernel, len(groups), terms),
+        select, rows, (((0,), (0,)), ((), ())), preferred_element_type=jnp.float32
+    ).astype(jnp.bfloat16)
+
+
+def spread_rows(own_rows, other_rows, tokens, step):
+    capacity, wide = own_rows.shape
+    width = wide - LANES
+    whole = pl.BlockSpec(own_rows.shape, lambda i: (0, 0))
+    return pl.pallas_call(
+        functools.partial(spread_kernel, step),
         grid=(width // step,),
         out_shape=shape_of((tokens, width), jnp.bfloat16),
-        in_specs=[pl.BlockSpec(select.shape, lambda i: (0, 0))]
-        + [pl.BlockSpec((capacity, step), lambda i: (0, i)) for _ in flat],
+        in_specs=[whole, whole],
         out_specs=pl.BlockSpec((tokens, step), lambda i: (0, i)),
-        cost_estimate=cost(2 * select.shape[0] * tokens * width, 2 * tokens * width),
+        cost_estimate=cost(4 * capacity * tokens * width, 2 * tokens * width),
         compiler_params=pltpu.CompilerParams(vmem_limit_bytes=16 * 2**20),
         name="spread_rows",
-    )(select, *flat)
+    )(own_rows, other_rows)
 
 
 def pairwise_shards(block_input, output_grad, expert_ids, gate_weights, gate_proj, up_proj, down_proj):
     tokens = block_input.shape[1]
     width = block_input.shape[2]
     capacity = tokens // 16
-    groups = lax.axis_size("expert")
-    partner = groups
-    count = lax.axis_size("dp") * groups
-    plane = [offset for offset in range(count) if not offset & partner]
-    own = lax.axis_index("expert").astype(jnp.int32).reshape(1)
+    count = 2 * lax.axis_size("dp")
+    plane = [offset for offset in range(count) if not offset & 2]
+    offsets = plane + [offset | 2 for offset in plane]
+    expert_index = lax.axis_index("expert").astype(jnp.int32)
+    core_index = lax.axis_index("dp").astype(jnp.int32) & 1
+    own = expert_index.reshape(1)
+    swapped = (expert_index ^ core_index).reshape(1)
     ids = jnp.transpose(expert_ids, (2, 0, 1))
     weights = jnp.transpose(gate_weights, (2, 0, 1))
-    *sends, select = pick_rows(own, ids, weights, block_input[0], output_grad[0], groups, capacity)
-    select_next = swap_back(select, 0)
+    stay = functools.partial(pltpu.with_memory_space_constraint, memory_space=pltpu.HBM)
+    *sends, select = pick_rows(
+        own, stay(ids), stay(weights), stay(block_input[0]), stay(output_grad[0]), capacity
+    )
+    upper, lower = stay(up_proj[0, 0]), stay(down_proj[0, 0])
+    gate, head = load_weights(stay(gate_proj[0, 0]), upper)
     mine = {0: sends[0]}
     for offset in sorted(plane[1:], reverse=True):
-        mine[offset] = swap(sends[offset % groups], offset)
-    theirs = {offset: swap(mine[offset], partner) for offset in plane}
+        mine[offset] = swap(sends[offset % 2], offset)
+    theirs = {offset: swap(mine[offset], 2) for offset in plane}
     pieces = [mine[offset] for offset in plane] + [theirs[offset] for offset in plane]
     keep, send, scores, delta, hidden = hidden_pass(
-        pieces, gate_proj[0, 0], up_proj[0, 0], down_proj[0, 0], capacity
-    )
-    recv = swap(send, partner)
-    *joined, scores = join_cores(keep, scores, recv, len(plane), capacity)
-    back = {offset: swap_back(joined[i], offset) for i, offset in enumerate(plane)}
-    gate_grad, upper_grad, lower_grad = weight_grads(pieces, delta, hidden, 512)
-    score_rows = {offset: scores[i * capacity : (i + 1) * capacity, :] for i, offset in enumerate(plane)}
+        swapped, pieces, offsets, gate, head, upper, lower, capacity
+    )
+    recv = swap(send, 2)
+    chips = count // 4
+    *joined, scores = join_cores(keep, scores, recv, chips)
+    messages = [send_back(joined[x], x) for x in range(chips)]
+    gate_grad, upper_grad, lower_grad = weight_grads(pieces, delta, hidden, width // 2)
+    score_rows = {offset: scores[i * capacity : (i + 1) * capacity, :1] for i, offset in enumerate(plane)}
     bit = count // 2
-    while bit > partner:
+    while bit > 2:
         low = [offset for offset in score_rows if not offset & bit]
-        moved = swap(jnp.concatenate([score_rows[offset | bit][:, :1] for offset in low]), bit)
+        moved = swap(jnp.concatenate([score_rows[offset | bit] for offset in low]), bit)
         score_rows = {
-            offset: score_rows[offset][:, :1] + moved[i * capacity : (i + 1) * capacity]
+            offset: score_rows[offset] + moved[i * capacity : (i + 1) * capacity]
             for i, offset in enumerate(low)
         }
         bit //= 2
-    score_list = [
-        score_rows[j][:, :1] if j == 0 else swap(score_rows[j][:, :1], j) for j in range(groups)
-    ]
+    score_list = [score_rows[0], swap(score_rows[1], 1)]
     weight_grad = score_grads(own, ids, weights, select, score_list, capacity)
-    received = spread_rows(
-        select_next,
-        [[back[offset] for offset in plane if offset % groups == j] for j in range(groups)],
-        width // 2,
-    )
+    own_rows, other_rows = total_rows(messages)
+    received = spread_rows(own_rows, swap(other_rows, 2), tokens, width // 2)
     return (
         received[None],
         jnp.transpose(weight_grad, (1, 2, 0)),
@@ -476,10 +586,10 @@
 
     def shards(*arrays):
         pairwise = (
-            dp_count * expert_count <= PAIRWISE_MAX
+            expert_count == 2
+            and dp_count * expert_count <= PAIRWISE_MAX
             and dp_count > 1
             and power_of_two(dp_count)
-            and power_of_two(expert_count)
             and arrays[4].shape[1] == 1
         )
         return (pairwise_shards if pairwise else general_shards)(*arrays)

time: 43.4 us -> 36.7 us (0.85)
  local copies, waits for them, and re-layouts: 6.58 us -> 0.01 us
  starting transfers between devices: 16.7 us -> 13.1 us
  Pallas kernels: 9.63 us -> 12.5 us
  waiting for transfers between devices: 9.49 us -> 10.1 us
    unnamed x18 -> x4, local copies, waits for them, and re-layouts: 6.58 us -> 0.01 us
    ppermute x5 -> x2, starting transfers between devices: 10.1 us -> 4.22 us  [send_back(): return lax.ppermute(value, ('pipe', 'dp', 'expert'), pairs)]
    pallas_call x5 -> x7, Pallas kernels: 5.63 us -> 9.66 us  [the longest x1 4.08 us: hidden_pass(): pl.pallas_call(functools.partial(hidden_kernel, capacity, offsets), out_s...]
    ppermute x10 -> x11, starting transfers between devices: 6.57 us -> 8.93 us  [swap(): lax.ppermute(value, ('dp', 'expert'), [(i, i ^ offset) for i in range(cou...]
    ppermute x5 -> x2, waiting for transfers between devices: 0.01 us -> 1.61 us  [send_back(): return lax.ppermute(value, ('pipe', 'dp', 'expert'), pairs)]
    pallas_call x1, Pallas kernels: 4.01 us -> 2.83 us  [weight_grads(): pl.pallas_call(functools.partial(weights_kernel, count, step), grid=(widt...]
    ppermute x10 -> x11, waiting for transfers between devices: 9.47 us -> 8.53 us  [swap(): lax.ppermute(value, ('dp', 'expert'), [(i, i ^ offset) for i in range(cou...]
  transfers between devices with their start and end apart: 15 -> 13, of which waited for: 5 -> 7; matrix products, arithmetic and copies ran while one was open for 0% -> 0% of each run, Pallas kernels for 11% -> 14%
where the time goes in v2:
time: 36.7 us; the launch traced here: 36.5 us
  starting transfers between devices  13.1 us (36%)
  Pallas kernels  12.5 us (34%)
  waiting for transfers between devices  10.1 us (28%)
  between operations  0.73 us (2%)
    ppermute x11, starting transfers between devices, swap(): lax.ppermute(value, ('dp', 'expert'), [(i, i ^ offset) for i in range(cou...  8.93 us
    ppermute x11, waiting for transfers between devices, swap(): lax.ppermute(value, ('dp', 'expert'), [(i, i ^ offset) for i in range(cou...  8.53 us
    ppermute x2, starting transfers between devices, send_back(): return lax.ppermute(value, ('pipe', 'dp', 'expert'), pairs)  4.22 us
    pallas_call x1, Pallas kernels, hidden_pass(): pl.pallas_call(functools.partial(hidden_kernel, capacity, offsets), out_s...  4.08 us
    pallas_call x1, Pallas kernels, weight_grads(): pl.pallas_call(functools.partial(weights_kernel, count, step), grid=(widt...  2.83 us
    pallas_call x1, Pallas kernels, pick_rows(): pl.pallas_call(functools.partial(pick_kernel, capacity), out_shape=[group...  1.66 us
    pallas_call x1, Pallas kernels, load_weights(): pl.pallas_call(load_kernel, out_shape=[shape_of((width, units), gate.dtyp...  1.62 us
    ppermute x2, waiting for transfers between devices, send_back(): return lax.ppermute(value, ('pipe', 'dp', 'expert'), pairs)  1.61 us
  transfers between devices with their start and end apart: 13, of which 7 were waited for; matrix products, arithmetic and copies ran while one was open for 0% of the time, Pallas kernels for 14%

profile of v2, /device:TPU:0, one launch (start us, length us, event | category | flops | bytes accessed | tf_op | source)
XLA Modules:
  0.0 36.5 jit_solution(14984837892062147508)
XLA Ops:
  0.6 1.7 %pick_rows.1 = (bf16[16,3200]{1,0:T(8,128)(2,1)S(1)}, bf16[16,3200]{1,0:T(8,128)(2,1)S(1)}, bf16[16,128]{1,0:T(8,128)(2,1)S(1)}) custom-call(s32[1]{0:T(128)} %bitcast.1.own_ref, s32[6,1,128]{2,1,0:T(1,128)} %bitcast.14, f32[6,1,128]{2,1,0:T(1,128)} %bitcast.16, bf16[128,3072]{1,0:T(8,128)(2,1)} %bitcast.22, bf16[128,3072]{1,0:T(8,128)(2,1)} %bitcast.23), custom_call_target="tpu_custom_call" | custom-call | flops 25165824 | bytes 1572864 | tf_op jit(solution)/shard_map/pick_rows/pallas_call | solution.py:99
  2.3 3.0 %collective-permute-start.1 = (bf16[16,3200]{1,0:T(8,128)(2,1)S(1)}, bf16[16,3200]{1,0:T(8,128)(2,1)S(1)}, u32[]{:S(2)}, u32[]{:S(2)}) collective-permute-start(bf16[16,3200]{1,0:T(8,128)(2,1)S(1)} %get-tuple-element.23.refs_0_), channel_id=1, source_target_pairs={{0,4},{1,5},{2,6},{3,7},{4,0},{5,1},{6,2},{7,3},{8,12},{9,13},{10,... | collective-permute-start | bytes 307208 | tf_op jit(solution)/shard_map/ppermute | solution.py:31
  5.3 1.5 %collective-permute-start = (bf16[16,3200]{1,0:T(8,128)(2,1)S(1)}, bf16[16,3200]{1,0:T(8,128)(2,1)S(1)}, u32[]{:S(2)}, u32[]{:S(2)}) collective-permute-start(bf16[16,3200]{1,0:T(8,128)(2,1)S(1)} %get-tuple-element.24), channel_id=1, source_target_pairs={{0,1},{1,0},{2,3},{3,2},{4,5},{5,4},{6,7},{7,6},{8,9},{9,8},{10,11... | collective-permute-start | bytes 307208 | tf_op jit(solution)/shard_map/ppermute | solution.py:31
  6.9 0.0 collective-permute-start.2
  6.9 1.6 %collective-permute-done.1.refs_2_ = bf16[16,3200]{1,0:T(8,128)(2,1)S(1)} collective-permute-done((bf16[16,3200]{1,0:T(8,128)(2,1)S(1)}, bf16[16,3200]{1,0:T(8,128)(2,1)S(1)}, u32[]{:S(2)}, u32[]{:S(2)}) %collective-permute-start.1) | collective-permute-done | bytes 102432 | tf_op jit(solution)/shard_map/ppermute | solution.py:31
  8.5 2.6 %collective-permute-done.refs_1_ = bf16[16,3200]{1,0:T(8,128)(2,1)S(1)} collective-permute-done((bf16[16,3200]{1,0:T(8,128)(2,1)S(1)}, bf16[16,3200]{1,0:T(8,128)(2,1)S(1)}, u32[]{:S(2)}, u32[]{:S(2)}) %collective-permute-start) | collective-permute-done | bytes 102432 | tf_op jit(solution)/shard_map/ppermute | solution.py:31
  11.1 1.3 %collective-permute-done.2.refs_3_ = bf16[16,3200]{1,0:T(8,128)(2,1)S(1)} collective-permute-done((bf16[16,3200]{1,0:T(8,128)(2,1)S(1)}, bf16[16,3200]{1,0:T(8,128)(2,1)S(1)}, u32[]{:S(2)}, u32[]{:S(2)}) %collective-permute-start.2) | collective-permute-done | bytes 102432 | tf_op jit(solution)/shard_map/ppermute | solution.py:31
  12.4 1.6 %load_weights.1 = (bf16[3072,256]{1,0:T(8,128)(2,1)S(1)}, bf16[1536,256]{1,0:T(8,128)(2,1)S(1)}) custom-call(bf16[3072,256]{1,0:T(8,128)(2,1)} %bitcast.20, bf16[3072,256]{1,0:T(8,128)(2,1)} %bitcast.18), custom_call_target="tpu_custom_call" | custom-call | bytes 2359296 | tf_op jit(solution)/shard_map/load_weights/pallas_call | solution.py:128
  14.1 4.1 %hidden_pass.1 = (f32[32,3200]{1,0:T(8,128)S(1)}, bf16[32,3200]{1,0:T(8,128)(2,1)S(1)}, f32[32,128]{1,0:T(8,128)S(1)}, bf16[128,512]{1,0:T(8,128)(2,1)S(1)}, bf16[128,256]{1,0:T(8,128)(2,1)S(1)}) custom-call(s32[1]{0:T(128)} %bitcast.swapped_ref, bf16[16,3200]{1,0:T(8,128)(2,1)S(1)} %get-tuple-element.23.refs_0_, ...), custom_call_target="tpu_custom_call" | custom-call | flops 1006632960 | bytes 4718592 | tf_op jit(solution)/shard_map/hidden_pass/pallas_call | solution.py:231
  18.2 0.0 copy-start
  18.2 0.6 %collective-permute-start.7 = (bf16[32,3200]{1,0:T(8,128)(2,1)S(1)}, bf16[32,3200]{1,0:T(8,128)(2,1)S(1)}, u32[]{:S(2)}, u32[]{:S(2)}) collective-permute-start(bf16[32,3200]{1,0:T(8,128)(2,1)S(1)} %get-tuple-element.29), channel_id=1, source_target_pairs={{0,2},{1,3},{2,0},{3,1},{4,6},{5,7},{6,4},{7,5},{8,10},{9,11},{10,... | collective-permute-start | bytes 614408 | tf_op jit(solution)/shard_map/ppermute | solution.py:31
  18.8 1.1 %collective-permute-done.7.recv_ref = bf16[32,3200]{1,0:T(8,128)(2,1)S(1)} collective-permute-done((bf16[32,3200]{1,0:T(8,128)(2,1)S(1)}, bf16[32,3200]{1,0:T(8,128)(2,1)S(1)}, u32[]{:S(2)}, u32[]{:S(2)}) %collective-permute-start.7) | collective-permute-done | bytes 204832 | tf_op jit(solution)/shard_map/ppermute | solution.py:31
  19.9 0.1 join_cores.1
  20.0 3.6 %collective-permute-start.8 = (bf16[16,3200]{1,0:T(8,128)(2,1)S(1)}, bf16[16,3200]{1,0:T(8,128)(2,1)S(1)}, u32[]{:S(2)}, u32[]{:S(2)}) collective-permute-start(bf16[16,3200]{1,0:T(8,128)(2,1)S(1)} %get-tuple-element.30), channel_id=1, source_target_pairs={{0,24},{1,26},{2,25},{3,27},{4,28},{5,30},{6,29},{7,31},{8,0},{9,2... | collective-permute-start | bytes 307208 | tf_op jit(solution)/shard_map/ppermute | solution.py:45
  23.6 0.6 %collective-permute-start.9 = (bf16[16,3200]{1,0:T(8,128)(2,1)S(1)}, bf16[16,3200]{1,0:T(8,128)(2,1)S(1)}, u32[]{:S(2)}, u32[]{:S(2)}) collective-permute-start(bf16[16,3200]{1,0:T(8,128)(2,1)S(1)} %get-tuple-element.31), channel_id=1, source_target_pairs={{0,28},{1,30},{2,29},{3,31},{4,24},{5,26},{6,25},{7,27},{8,4},{9,6... | collective-permute-start | bytes 307208 | tf_op jit(solution)/shard_map/ppermute | solution.py:45
  24.2 2.8 %weight_grads.1 = (bf16[3072,256]{1,0:T(8,128)(2,1)}, bf16[3072,256]{1,0:T(8,128)(2,1)}, bf16[256,3072]{1,0:T(8,128)(2,1)}) custom-call(bf16[16,3200]{1,0:T(8,128)(2,1)S(1)} %get-tuple-element.23.refs_0_, bf16[16,3200]{1,0:T(8,128)(2,1)S(1)} %collective-permute-done.refs_1_, bf16[16,3200]{1,0:T(8,128)(2,1)S(1)} %collective-permute-done.1.refs_2_, ...), custom_call_target="tpu_custom_call" | custom-call | flops 603979776 | bytes 4718592 | tf_op jit(solution)/shard_map/weight_grads/pallas_call | solution.py:301
  27.0 1.3 %collective-permute-start.11 = (f32[16,1]{1,0:T(8,128)S(1)}, f32[16,1]{1,0:T(8,128)S(1)}, u32[]{:S(2)}, u32[]{:S(2)}) collective-permute-start(f32[16,1]{1,0:T(8,128)S(1)} %concatenate.3), channel_id=1, source_target_pairs={{0,4},{1,5},{2,6},{3,7},{4,0},{5,1},{6,2},{7,3},{8,12},{9,13},{10,... | collective-permute-start | bytes 200 | tf_op jit(solution)/shard_map/ppermute | solution.py:31
  28.3 1.6 %collective-permute-done.9.refs_1_ = bf16[16,3200]{1,0:T(8,128)(2,1)S(1)} collective-permute-done((bf16[16,3200]{1,0:T(8,128)(2,1)S(1)}, bf16[16,3200]{1,0:T(8,128)(2,1)S(1)}, u32[]{:S(2)}, u32[]{:S(2)}) %collective-permute-start.9) | collective-permute-done | bytes 102432 | tf_op jit(solution)/shard_map/ppermute | solution.py:45
  30.0 0.6 %collective-permute-start.10 = (bf16[8,3200]{1,0:T(8,128)(2,1)S(1)}, bf16[8,3200]{1,0:T(8,128)(2,1)S(1)}, u32[]{:S(2)}, u32[]{:S(2)}) collective-permute-start(bf16[8,3200]{1,0:T(8,128)(2,1)S(1)} %get-tuple-element.33), channel_id=1, source_target_pairs={{0,2},{1,3},{2,0},{3,1},{4,6},{5,7},{6,4},{7,5},{8,10},{9,11},{10,... | collective-permute-start | bytes 153608 | tf_op jit(solution)/shard_map/ppermute | solution.py:31
  30.6 0.2 collective-permute-done.11
  30.8 1.9 %collective-permute-start.12 = (f32[8,1]{1,0:T(8,128)S(1)}, f32[8,1]{1,0:T(8,128)S(1)}, u32[]{:S(2)}, u32[]{:S(2)}) collective-permute-start(f32[8,1]{1,0:T(8,128)S(1)} %get-tuple-element.41), channel_id=1, source_target_pairs={{0,1},{1,0},{2,3},{3,2},{4,5},{5,4},{6,7},{7,6},{8,9},{9,8},{10,11... | collective-permute-start | bytes 104 | tf_op jit(solution)/shard_map/ppermute | solution.py:31
  32.6 1.7 %collective-permute-done.12.refs_1_ = f32[8,1]{1,0:T(8,128)S(1)} collective-permute-done((f32[8,1]{1,0:T(8,128)S(1)}, f32[8,1]{1,0:T(8,128)S(1)}, u32[]{:S(2)}, u32[]{:S(2)}) %collective-permute-start.12) | collective-permute-done | bytes 64 | tf_op jit(solution)/shard_map/ppermute | solution.py:31
  34.4 0.7 %score_grads.1 = f32[6,1,128]{2,1,0:T(1,128)} custom-call(s32[1]{0:T(128)} %bitcast.1.own_ref, s32[6,1,128]{2,1,0:T(1,128)S(1)} %bitcast.15, f32[6,1,128]{2,1,0:T(1,128)S(1)} %bitcast.17, bf16[16,128]{1,0:T(8,128)(2,1)S(1)} %get-tuple-element.34.select_ref, f32[8,1]{1,0:T(8,128)S(1)} %get-tuple-element.42.refs_0_, f32[8,1]{1,0:T(8,128)S(1)} %collective-permute-done.12.refs_1_), custom_call_target="tpu_custom_call" | custom-call | flops 1000 | bytes 1000 | tf_op jit(solution)/shard_map/score_grads/pallas_call | solution.py:337
  35.0 1.5 %spread_rows.1 = bf16[128,3072]{1,0:T(8,128)(2,1)} custom-call(bf16[8,3200]{1,0:T(8,128)(2,1)S(1)} %get-tuple-element.32.own_ref, bf16[8,3200]{1,0:T(8,128)(2,1)S(1)} %collective-permute-done.10.other_ref), custom_call_target="tpu_custom_call" | custom-call | flops 12582912 | bytes 786432 | tf_op jit(solution)/shard_map/spread_rows/pallas_call | solution.py:397
  (16 shorter events, 0.1 us)
Async XLA Ops:
  2.3 6.2 %collective-permute-start.1 = (bf16[16,3200]{1,0:T(8,128)(2,1)S(1)}, bf16[16,3200]{1,0:T(8,128)(2,1)S(1)}, u32[]{:S(2)}, u32[]{:S(2)}) collective-permute-start(bf16[16,3200]{1,0:T(8,128)(2,1)S(1)} %get-tuple-element.23.refs_0_), channel_id=1, source_target_pairs={{0,4},{1,5},{2,6},{3,7},{4,0},{5,1},{6,2},{7,3},{8,12},{9,13},{10,... | collective-permute-start | bytes 307208 | tf_op jit(solution)/shard_map/ppermute | solution.py:31
  5.3 5.8 %collective-permute-start = (bf16[16,3200]{1,0:T(8,128)(2,1)S(1)}, bf16[16,3200]{1,0:T(8,128)(2,1)S(1)}, u32[]{:S(2)}, u32[]{:S(2)}) collective-permute-start(bf16[16,3200]{1,0:T(8,128)(2,1)S(1)} %get-tuple-element.24), channel_id=1, source_target_pairs={{0,1},{1,0},{2,3},{3,2},{4,5},{5,4},{6,7},{7,6},{8,9},{9,8},{10,11... | collective-permute-start | bytes 307208 | tf_op jit(solution)/shard_map/ppermute | solution.py:31
  6.9 5.6 %collective-permute-start.2 = (bf16[16,3200]{1,0:T(8,128)(2,1)S(1)}, bf16[16,3200]{1,0:T(8,128)(2,1)S(1)}, u32[]{:S(2)}, u32[]{:S(2)}) collective-permute-start(bf16[16,3200]{1,0:T(8,128)(2,1)S(1)} %get-tuple-element.24), channel_id=1, source_target_pairs={{0,5},{1,4},{2,7},{3,6},{4,1},{5,0},{6,3},{7,2},{8,13},{9,12},{10,... | collective-permute-start | bytes 307208 | tf_op jit(solution)/shard_map/ppermute | solution.py:31
  6.9 7.2 %collective-permute-start.3 = (bf16[16,3200]{1,0:T(8,128)(2,1)S(1)}, bf16[16,3200]{1,0:T(8,128)(2,1)S(1)}, u32[]{:S(2)}, u32[]{:S(2)}) collective-permute-start(bf16[16,3200]{1,0:T(8,128)(2,1)S(1)} %get-tuple-element.23.refs_0_), channel_id=1, source_target_pairs={{0,2},{1,3},{2,0},{3,1},{4,6},{5,7},{6,4},{7,5},{8,10},{9,11},{10,... | collective-permute-start | bytes 307208 | tf_op jit(solution)/shard_map/ppermute | solution.py:31
  8.5 5.6 %collective-permute-start.5 = (bf16[16,3200]{1,0:T(8,128)(2,1)S(1)}, bf16[16,3200]{1,0:T(8,128)(2,1)S(1)}, u32[]{:S(2)}, u32[]{:S(2)}) collective-permute-start(bf16[16,3200]{1,0:T(8,128)(2,1)S(1)} %collective-permute-done.1.refs_2_), channel_id=1, source_target_pairs={{0,2},{1,3},{2,0},{3,1},{4,6},{5,7},{6,4},{7,5},{8,10},{9,11},{10,... | collective-permute-start | bytes 307208 | tf_op jit(solution)/shard_map/ppermute | solution.py:31
  11.1 3.0 %collective-permute-start.4 = (bf16[16,3200]{1,0:T(8,128)(2,1)S(1)}, bf16[16,3200]{1,0:T(8,128)(2,1)S(1)}, u32[]{:S(2)}, u32[]{:S(2)}) collective-permute-start(bf16[16,3200]{1,0:T(8,128)(2,1)S(1)} %collective-permute-done.refs_1_), channel_id=1, source_target_pairs={{0,2},{1,3},{2,0},{3,1},{4,6},{5,7},{6,4},{7,5},{8,10},{9,11},{10,... | collective-permute-start | bytes 307208 | tf_op jit(solution)/shard_map/ppermute | solution.py:31
  12.4 1.7 %collective-permute-start.6 = (bf16[16,3200]{1,0:T(8,128)(2,1)S(1)}, bf16[16,3200]{1,0:T(8,128)(2,1)S(1)}, u32[]{:S(2)}, u32[]{:S(2)}) collective-permute-start(bf16[16,3200]{1,0:T(8,128)(2,1)S(1)} %collective-permute-done.2.refs_3_), channel_id=1, source_target_pairs={{0,2},{1,3},{2,0},{3,1},{4,6},{5,7},{6,4},{7,5},{8,10},{9,11},{10,... | collective-permute-start | bytes 307208 | tf_op jit(solution)/shard_map/ppermute | solution.py:31
  18.2 16.2 %copy-start = (s32[1,128,6]{1,0,2:T(1,128)S(1)}, s32[1,128,6]{1,0,2:T(1,128)}, u32[]{:S(2)}) copy-start(s32[1,128,6]{1,0,2:T(1,128)} %param.9) | copy-start | bytes 9220
  18.2 16.2 %copy-start.1 = (f32[1,128,6]{1,0,2:T(1,128)S(1)}, f32[1,128,6]{1,0,2:T(1,128)}, u32[]{:S(2)}) copy-start(f32[1,128,6]{1,0,2:T(1,128)} %param.10) | copy-start | bytes 9220
  18.2 1.7 %collective-permute-start.7 = (bf16[32,3200]{1,0:T(8,128)(2,1)S(1)}, bf16[32,3200]{1,0:T(8,128)(2,1)S(1)}, u32[]{:S(2)}, u32[]{:S(2)}) collective-permute-start(bf16[32,3200]{1,0:T(8,128)(2,1)S(1)} %get-tuple-element.29), channel_id=1, source_target_pairs={{0,2},{1,3},{2,0},{3,1},{4,6},{5,7},{6,4},{7,5},{8,10},{9,11},{10,... | collective-permute-start | bytes 614408 | tf_op jit(solution)/shard_map/ppermute | solution.py:31
  20.0 8.4 %collective-permute-start.8 = (bf16[16,3200]{1,0:T(8,128)(2,1)S(1)}, bf16[16,3200]{1,0:T(8,128)(2,1)S(1)}, u32[]{:S(2)}, u32[]{:S(2)}) collective-permute-start(bf16[16,3200]{1,0:T(8,128)(2,1)S(1)} %get-tuple-element.30), channel_id=1, source_target_pairs={{0,24},{1,26},{2,25},{3,27},{4,28},{5,30},{6,29},{7,31},{8,0},{9,2... | collective-permute-start | bytes 307208 | tf_op jit(solution)/shard_map/ppermute | solution.py:45
  23.6 6.4 %collective-permute-start.9 = (bf16[16,3200]{1,0:T(8,128)(2,1)S(1)}, bf16[16,3200]{1,0:T(8,128)(2,1)S(1)}, u32[]{:S(2)}, u32[]{:S(2)}) collective-permute-start(bf16[16,3200]{1,0:T(8,128)(2,1)S(1)} %get-tuple-element.31), channel_id=1, source_target_pairs={{0,28},{1,30},{2,29},{3,31},{4,24},{5,26},{6,25},{7,27},{8,4},{9,6... | collective-permute-start | bytes 307208 | tf_op jit(solution)/shard_map/ppermute | solution.py:45
  27.0 3.7 %collective-permute-start.11 = (f32[16,1]{1,0:T(8,128)S(1)}, f32[16,1]{1,0:T(8,128)S(1)}, u32[]{:S(2)}, u32[]{:S(2)}) collective-permute-start(f32[16,1]{1,0:T(8,128)S(1)} %concatenate.3), channel_id=1, source_target_pairs={{0,4},{1,5},{2,6},{3,7},{4,0},{5,1},{6,2},{7,3},{8,12},{9,13},{10,... | collective-permute-start | bytes 200 | tf_op jit(solution)/shard_map/ppermute | solution.py:31
  30.0 5.1 %collective-permute-start.10 = (bf16[8,3200]{1,0:T(8,128)(2,1)S(1)}, bf16[8,3200]{1,0:T(8,128)(2,1)S(1)}, u32[]{:S(2)}, u32[]{:S(2)}) collective-permute-start(bf16[8,3200]{1,0:T(8,128)(2,1)S(1)} %get-tuple-element.33), channel_id=1, source_target_pairs={{0,2},{1,3},{2,0},{3,1},{4,6},{5,7},{6,4},{7,5},{8,10},{9,11},{10,... | collective-permute-start | bytes 153608 | tf_op jit(solution)/shard_map/ppermute | solution.py:31
  30.8 3.6 %collective-permute-start.12 = (f32[8,1]{1,0:T(8,128)S(1)}, f32[8,1]{1,0:T(8,128)S(1)}, u32[]{:S(2)}, u32[]{:S(2)}) collective-permute-start(f32[8,1]{1,0:T(8,128)S(1)} %get-tuple-element.41), channel_id=1, source_target_pairs={{0,1},{1,0},{2,3},{3,2},{4,5},{5,4},{6,7},{7,6},{8,9},{9,8},{10,11... | collective-permute-start | bytes 104 | tf_op jit(solution)/shard_map/ppermute | solution.py:31

commit v3 on v2

--- a/solution.py
+++ b/solution.py
@@ -146,32 +146,47 @@
     return jnp.concatenate(parts, axis=0)
 
 
+def chain(steps):
+    count = [0, 0]
+    staged = []
+    for unit, weights, turned, left, total in steps:
+        staged.append((unit, count[unit] % 2))
+        count[unit] += 1
+    ahead = 2
+    for i in range(len(steps) + ahead):
+        if i < len(steps):
+            unit, weights, turned, _, _ = steps[i]
+            pltpu.matmul_push_rhs(weights(), staging_register=staged[i][1], mxu_index=unit, transpose=turned)
+        if i >= ahead:
+            _, _, _, left, total = steps[i - ahead]
+            pltpu.matmul_acc_lhs(total, left(), load_staged_rhs=staged[i - ahead][1])
+
+
 def hidden_kernel(capacity, offsets, swapped_ref, *refs):
     pieces = len(offsets)
     piece_refs = refs[:pieces]
     gate_ref, head_ref, upper_hbm, lower_hbm = refs[pieces : pieces + 4]
-    keep_ref, send_ref, score_ref, delta_ref, hidden_ref, tail_ref, lower_ref, sems = refs[pieces + 4 :]
+    keep_ref, send_ref, score_ref, delta_ref, hidden_ref = refs[pieces + 4 : pieces + 9]
+    tail_ref, lower_ref, sems = refs[pieces + 9 :]
     width, units = gate_ref.shape
     middle_row = head_ref.shape[0]
+    rows = pieces * capacity
+    half = rows // 2
+    tile = units
     tail_copy = pltpu.make_async_copy(upper_hbm.at[middle_row:], tail_ref, sems.at[0])
-    lower_copy = pltpu.make_async_copy(lower_hbm, lower_ref, sems.at[1])
+    lower_copies = [
+        pltpu.make_async_copy(lower_hbm.at[:, part], lower_ref.at[:, part], sems.at[1 + i])
+        for i, part in enumerate((slice(0, middle_row), slice(middle_row, width)))
+    ]
     tail_copy.start()
-    lower_copy.start()
-    half = keep_ref.shape[0]
-    across = (((1,), (1,)), ((), ()))
-
-    def rows(start, stop):
-        return jnp.concatenate([ref[:, start:stop] for ref in piece_refs], axis=0)
-
-    def upper_rows(value):
-        return jnp.concatenate(
-            [value[2 * p * capacity : (2 * p + 1) * capacity] for p in range(pieces)], axis=0
-        )
-
-    def lower_rows(value):
-        return jnp.concatenate(
-            [value[(2 * p + 1) * capacity : (2 * p + 2) * capacity] for p in range(pieces)], axis=0
-        )
+    for copy in lower_copies:
+        copy.start()
+
+    def acts(start):
+        return jnp.concatenate([ref[:capacity, start : start + tile] for ref in piece_refs], axis=0)
+
+    def grads(start):
+        return jnp.concatenate([ref[capacity:, start : start + tile] for ref in piece_refs], axis=0)
 
     def order(value, wanted):
         lists = [
@@ -185,31 +200,80 @@
     chips = [4 * x for x in range(pieces // 4)]
     kept = ([x | c for x in chips for c in (0, 2)], [x | c | 1 for x in chips for c in (2, 0)])
     sent = ([x | c | 1 for x in chips for c in (0, 2)], [x | c for x in chips for c in (2, 0)])
-    gate_pre = upper_rows(jnp.dot(rows(0, width), gate_ref[...], preferred_element_type=jnp.float32))
-    up_value = jnp.dot(rows(0, middle_row), head_ref[...], preferred_element_type=jnp.float32)
-    tail_copy.wait()
-    up_value = upper_rows(
-        up_value + jnp.dot(rows(middle_row, width), tail_ref[...], preferred_element_type=jnp.float32)
-    )
-    lower_copy.wait()
-    grad_hidden = lower_rows(lax.dot_general(rows(0, width), lower_ref[...], across, preferred_element_type=jnp.float32))
+
+    def at(ref, start):
+        return lambda: ref[start : start + tile]
+
+    def at_column(ref, start):
+        return lambda: ref[:, start : start + tile]
+
+    def forward(first, second):
+        def steps(starts, upper_ref, base):
+            result = []
+            for start in starts:
+                left = functools.partial(acts, start)
+                result.append((0, at(gate_ref, start), False, left, first))
+                result.append((1, at(upper_ref, start - base), False, left, second))
+            return result
+
+        chain(steps(range(0, middle_row, tile), head_ref, 0))
+        tail_copy.wait()
+        chain(steps(range(middle_row, width, tile), tail_ref, middle_row))
+        return pltpu.matmul_pop(first), pltpu.matmul_pop(second)
+
+    def backward(first, second):
+        totals = (first, second)
+
+        def steps(starts):
+            return [
+                (i % 2, at_column(lower_ref, start), True, functools.partial(grads, start), totals[i % 2])
+                for i, start in enumerate(starts)
+            ]
+
+        lower_copies[0].wait()
+        chain(steps(range(0, middle_row, tile)))
+        lower_copies[1].wait()
+        chain(steps(range(middle_row, width, tile)))
+        return pltpu.matmul_pop(first) + pltpu.matmul_pop(second)
+
+    totals = [pltpu.ACC(unit)((rows, tile), jnp.float32) for unit in range(2)]
+    gate_pre, up_value = pl.run_scoped(forward, *totals)
+    grad_hidden = pl.run_scoped(backward, *totals)
     sigma_gate = jax.nn.sigmoid(gate_pre)
     swish = gate_pre * sigma_gate
     hidden = swish * up_value
     scores = jnp.sum(hidden * grad_hidden, axis=1, keepdims=True)
     delta_gate = grad_hidden * up_value * sigma_gate * (1.0 + gate_pre * (1.0 - sigma_gate))
     delta_up = grad_hidden * swish
-
     marks = jnp.concatenate([ref[:, width:].astype(jnp.float32)[:capacity] for ref in piece_refs], axis=0)
-    gate_rows = jnp.concatenate([order(delta_gate, kept), order(delta_gate, sent)]).astype(jnp.bfloat16)
+    gate_part = jnp.concatenate([order(delta_gate, kept), order(delta_gate, sent)]).astype(jnp.bfloat16)
     upper_part = jnp.concatenate([order(delta_up, kept), order(delta_up, sent)]).astype(jnp.bfloat16)
-    for part, ref in ((slice(0, middle_row), head_ref), (slice(middle_row, width), tail_ref)):
-        partial_rows = lax.dot_general(
-            gate_rows, gate_ref[part], across, preferred_element_type=jnp.float32
-        ) + lax.dot_general(upper_part, ref[...], across, preferred_element_type=jnp.float32)
-        keep_ref[:, part] = partial_rows[:half]
-        send_ref[:, part] = partial_rows[half:].astype(jnp.bfloat16)
     keep_ref[:, width:] = order(marks, kept)
+
+    def back(*accs):
+        starts = list(range(0, width, tile))
+        for group in range(0, len(starts), 4):
+            steps = []
+            for source in range(2):
+                for i, start in enumerate(starts[group : group + 4]):
+                    unit = i % 2
+                    if source == 0:
+                        weights, left = at(gate_ref, start), gate_part
+                    elif start < middle_row:
+                        weights, left = at(head_ref, start), upper_part
+                    else:
+                        weights, left = at(tail_ref, start - middle_row), upper_part
+                    total = accs[2 * ((group // 4 * 2 + i // 2) % 2) + unit]
+                    steps.append((unit, weights, True, lambda left=left: left, total))
+            ordered = [steps[i] for i in (0, 1, 4, 5, 2, 3, 6, 7) if i < len(steps)] if len(steps) == 8 else steps
+            chain(ordered)
+            for i, start in enumerate(starts[group : group + 4]):
+                total = accs[2 * ((group // 4 * 2 + i // 2) % 2) + i % 2]
+                block = pltpu.matmul_pop(total)
+                keep_ref[:, start : start + tile] = block[:half]
+                send_ref[:, start : start + tile] = block[half:].astype(jnp.bfloat16)
+
+    pl.run_scoped(back, *totals, *totals)
     score_ref[...] = jnp.broadcast_to(scores[:half], (half, LANES))
     rest = scores[half:]
     high = rest.astype(jnp.bfloat16).astype(jnp.float32)
@@ -242,7 +306,7 @@
         scratch_shapes=[
             pltpu.VMEM((width - head.shape[0], units), jnp.bfloat16),
             pltpu.VMEM((units, width), jnp.bfloat16),
-            pltpu.SemaphoreType.DMA((2,)),
+            pltpu.SemaphoreType.DMA((3,)),
         ],
         cost_estimate=cost(10 * rows * width * units, 6 * width * units),
         compiler_params=pltpu.CompilerParams(vmem_limit_bytes=24 * 2**20),
@@ -372,34 +436,36 @@
     )(*arrays)
 
 
-def spread_kernel(step, own_ref, other_ref, out_ref):
-    tokens = out_ref.shape[0]
-    capacity, wide = own_ref.shape
-    width = wide - LANES
-    start = pl.multiple_of(pl.program_id(0) * step, step)
+def spread_kernel(chunks, own_ref, other_ref, out_hbm, out_ref, sems):
+    tokens, width = out_ref.shape
+    capacity = own_ref.shape[0]
     marks = jnp.concatenate([ref[:, width:].astype(jnp.float32) for ref in (own_ref, other_ref)], axis=0)
     lane = lax.broadcasted_iota(jnp.int32, marks.shape, 1)
     number = jnp.sum(jnp.where(lane == 0, marks * 256.0, jnp.where(lane == 1, marks, 0.0)), axis=1, keepdims=True)
     token = lax.broadcasted_iota(jnp.int32, (2 * capacity, tokens), 1).astype(jnp.float32)
     select = jnp.where(token + 1.0 == number, 1.0, 0.0).astype(jnp.bfloat16)
-    rows = jnp.concatenate(
-        [ref[:, pl.ds(start, step)].astype(jnp.float32) for ref in (own_ref, other_ref)], axis=0
-    ).astype(jnp.bfloat16)
-    out_ref[...] = lax.dot_general(
-        select, rows, (((0,), (0,)), ((), ())), preferred_element_type=jnp.float32
-    ).astype(jnp.bfloat16)
-
-
-def spread_rows(own_rows, other_rows, tokens, step):
+    copies = []
+    for i in range(chunks):
+        part = slice(i * width // chunks, (i + 1) * width // chunks)
+        rows = jnp.concatenate([ref[:, part] for ref in (own_ref, other_ref)], axis=0)
+        out_ref[:, part] = lax.dot_general(
+            select, rows, (((0,), (0,)), ((), ())), preferred_element_type=jnp.float32
+        ).astype(jnp.bfloat16)
+        copies.append(pltpu.make_async_copy(out_ref.at[:, part], out_hbm.at[:, part], sems.at[i]))
+        copies[-1].start()
+    for copy in copies:
+        copy.wait()
+
+
+def spread_rows(own_rows, other_rows, tokens, chunks):
     capacity, wide = own_rows.shape
     width = wide - LANES
-    whole = pl.BlockSpec(own_rows.shape, lambda i: (0, 0))
-    return pl.pallas_call(
-        functools.partial(spread_kernel, step),
-        grid=(width // step,),
+    return pl.pallas_call(
+        functools.partial(spread_kernel, chunks),
         out_shape=shape_of((tokens, width), jnp.bfloat16),
-        in_specs=[whole, whole],
-        out_specs=pl.BlockSpec((tokens, step), lambda i: (0, i)),
+        in_specs=[VMEM, VMEM],
+        out_specs=HBM,
+        scratch_shapes=[pltpu.VMEM((tokens, width), jnp.bfloat16), pltpu.SemaphoreType.DMA((chunks,))],
         cost_estimate=cost(4 * capacity * tokens * width, 2 * tokens * width),
         compiler_params=pltpu.CompilerParams(vmem_limit_bytes=16 * 2**20),
         name="spread_rows",
@@ -451,7 +517,7 @@
     score_list = [score_rows[0], swap(score_rows[1], 1)]
     weight_grad = score_grads(own, ids, weights, select, score_list, capacity)
     own_rows, other_rows = total_rows(messages)
-    received = spread_rows(own_rows, swap(other_rows, 2), tokens, width // 2)
+    received = spread_rows(own_rows, swap(other_rows, 2), tokens, 3)
     return (
         received[None],
         jnp.transpose(weight_grad, (1, 2, 0)),

time: 36.7 us -> 35.5 us (0.967)
  Pallas kernels: 12.5 us -> 11.3 us
    pallas_call x1, Pallas kernels: 4.08 us -> 3.15 us  [hidden_pass(): pl.pallas_call(functools.partial(hidden_kernel, capacity, offsets), out_s...]
  transfers between devices with their start and end apart: 13 -> 13, of which waited for: 7 -> 7; matrix products, arithmetic and copies ran while one was open for 0% -> 0% of each run, Pallas kernels for 14% -> 15%
where the time goes in v3:
time: 35.5 us; the launch traced here: 35.3 us
  starting transfers between devices  13.1 us (37%)
  Pallas kernels  11.3 us (32%)
  waiting for transfers between devices  10.1 us (28%)
  between operations  0.73 us (2%)
    ppermute x11, starting transfers between devices, swap(): lax.ppermute(value, ('dp', 'expert'), [(i, i ^ offset) for i in range(cou...  8.93 us
    ppermute x11, waiting for transfers between devices, swap(): lax.ppermute(value, ('dp', 'expert'), [(i, i ^ offset) for i in range(cou...  8.53 us
    ppermute x2, starting transfers between devices, send_back(): return lax.ppermute(value, ('pipe', 'dp', 'expert'), pairs)  4.21 us
    pallas_call x1, Pallas kernels, hidden_pass(): pl.pallas_call(functools.partial(hidden_kernel, capacity, offsets), out_s...  3.15 us
    pallas_call x1, Pallas kernels, weight_grads(): pl.pallas_call(functools.partial(weights_kernel, count, step), grid=(widt...  2.83 us
    pallas_call x1, Pallas kernels, pick_rows(): pl.pallas_call(functools.partial(pick_kernel, capacity), out_shape=[group...  1.66 us
    pallas_call x1, Pallas kernels, load_weights(): pl.pallas_call(load_kernel, out_shape=[shape_of((width, units), gate.dtyp...  1.62 us
    ppermute x2, waiting for transfers between devices, send_back(): return lax.ppermute(value, ('pipe', 'dp', 'expert'), pairs)  1.61 us
  transfers between devices with their start and end apart: 13, of which 7 were waited for; matrix products, arithmetic and copies ran while one was open for 0% of the time, Pallas kernels for 15%

profile of v3, /device:TPU:0, one launch (start us, length us, event | category | flops | bytes accessed | tf_op | source)
XLA Modules:
  0.0 35.3 jit_solution(1038271766892229007)
XLA Ops:
  0.6 1.7 %pick_rows.1 = (bf16[16,3200]{1,0:T(8,128)(2,1)S(1)}, bf16[16,3200]{1,0:T(8,128)(2,1)S(1)}, bf16[16,128]{1,0:T(8,128)(2,1)S(1)}) custom-call(s32[1]{0:T(128)} %bitcast.1.own_ref, s32[6,1,128]{2,1,0:T(1,128)} %bitcast.14, f32[6,1,128]{2,1,0:T(1,128)} %bitcast.16, bf16[128,3072]{1,0:T(8,128)(2,1)} %bitcast.22, bf16[128,3072]{1,0:T(8,128)(2,1)} %bitcast.23), custom_call_target="tpu_custom_call" | custom-call | flops 25165824 | bytes 1572864 | tf_op jit(solution)/shard_map/pick_rows/pallas_call | solution.py:99
  2.3 3.0 %collective-permute-start.1 = (bf16[16,3200]{1,0:T(8,128)(2,1)S(1)}, bf16[16,3200]{1,0:T(8,128)(2,1)S(1)}, u32[]{:S(2)}, u32[]{:S(2)}) collective-permute-start(bf16[16,3200]{1,0:T(8,128)(2,1)S(1)} %get-tuple-element.23.refs_0_), channel_id=1, source_target_pairs={{0,4},{1,5},{2,6},{3,7},{4,0},{5,1},{6,2},{7,3},{8,12},{9,13},{10,... | collective-permute-start | bytes 307208 | tf_op jit(solution)/shard_map/ppermute | solution.py:31
  5.3 1.5 %collective-permute-start = (bf16[16,3200]{1,0:T(8,128)(2,1)S(1)}, bf16[16,3200]{1,0:T(8,128)(2,1)S(1)}, u32[]{:S(2)}, u32[]{:S(2)}) collective-permute-start(bf16[16,3200]{1,0:T(8,128)(2,1)S(1)} %get-tuple-element.24), channel_id=1, source_target_pairs={{0,1},{1,0},{2,3},{3,2},{4,5},{5,4},{6,7},{7,6},{8,9},{9,8},{10,11... | collective-permute-start | bytes 307208 | tf_op jit(solution)/shard_map/ppermute | solution.py:31
  6.9 0.0 collective-permute-start.2
  6.9 1.6 %collective-permute-done.1.refs_2_ = bf16[16,3200]{1,0:T(8,128)(2,1)S(1)} collective-permute-done((bf16[16,3200]{1,0:T(8,128)(2,1)S(1)}, bf16[16,3200]{1,0:T(8,128)(2,1)S(1)}, u32[]{:S(2)}, u32[]{:S(2)}) %collective-permute-start.1) | collective-permute-done | bytes 102432 | tf_op jit(solution)/shard_map/ppermute | solution.py:31
  8.5 2.6 %collective-permute-done.refs_1_ = bf16[16,3200]{1,0:T(8,128)(2,1)S(1)} collective-permute-done((bf16[16,3200]{1,0:T(8,128)(2,1)S(1)}, bf16[16,3200]{1,0:T(8,128)(2,1)S(1)}, u32[]{:S(2)}, u32[]{:S(2)}) %collective-permute-start) | collective-permute-done | bytes 102432 | tf_op jit(solution)/shard_map/ppermute | solution.py:31
  11.1 1.3 %collective-permute-done.2.refs_3_ = bf16[16,3200]{1,0:T(8,128)(2,1)S(1)} collective-permute-done((bf16[16,3200]{1,0:T(8,128)(2,1)S(1)}, bf16[16,3200]{1,0:T(8,128)(2,1)S(1)}, u32[]{:S(2)}, u32[]{:S(2)}) %collective-permute-start.2) | collective-permute-done | bytes 102432 | tf_op jit(solution)/shard_map/ppermute | solution.py:31
  12.4 1.6 %load_weights.1 = (bf16[3072,256]{1,0:T(8,128)(2,1)S(1)}, bf16[1536,256]{1,0:T(8,128)(2,1)S(1)}) custom-call(bf16[3072,256]{1,0:T(8,128)(2,1)} %bitcast.20, bf16[3072,256]{1,0:T(8,128)(2,1)} %bitcast.18), custom_call_target="tpu_custom_call" | custom-call | bytes 2359296 | tf_op jit(solution)/shard_map/load_weights/pallas_call | solution.py:128
  14.1 3.1 %hidden_pass.1 = (f32[32,3200]{1,0:T(8,128)S(1)}, bf16[32,3200]{1,0:T(8,128)(2,1)S(1)}, f32[32,128]{1,0:T(8,128)S(1)}, bf16[128,512]{1,0:T(8,128)(2,1)S(1)}, bf16[128,256]{1,0:T(8,128)(2,1)S(1)}) custom-call(s32[1]{0:T(128)} %bitcast.swapped_ref, bf16[16,3200]{1,0:T(8,128)(2,1)S(1)} %get-tuple-element.23.refs_0_, ...), custom_call_target="tpu_custom_call" | custom-call | flops 1006632960 | bytes 4718592 | tf_op jit(solution)/shard_map/hidden_pass/pallas_call | solution.py:295
  17.3 0.0 copy-start
  17.3 0.6 %collective-permute-start.7 = (bf16[32,3200]{1,0:T(8,128)(2,1)S(1)}, bf16[32,3200]{1,0:T(8,128)(2,1)S(1)}, u32[]{:S(2)}, u32[]{:S(2)}) collective-permute-start(bf16[32,3200]{1,0:T(8,128)(2,1)S(1)} %get-tuple-element.29), channel_id=1, source_target_pairs={{0,2},{1,3},{2,0},{3,1},{4,6},{5,7},{6,4},{7,5},{8,10},{9,11},{10,... | collective-permute-start | bytes 614408 | tf_op jit(solution)/shard_map/ppermute | solution.py:31
  17.9 1.1 %collective-permute-done.7.recv_ref = bf16[32,3200]{1,0:T(8,128)(2,1)S(1)} collective-permute-done((bf16[32,3200]{1,0:T(8,128)(2,1)S(1)}, bf16[32,3200]{1,0:T(8,128)(2,1)S(1)}, u32[]{:S(2)}, u32[]{:S(2)}) %collective-permute-start.7) | collective-permute-done | bytes 204832 | tf_op jit(solution)/shard_map/ppermute | solution.py:31
  18.9 0.1 join_cores.1
  19.1 3.6 %collective-permute-start.8 = (bf16[16,3200]{1,0:T(8,128)(2,1)S(1)}, bf16[16,3200]{1,0:T(8,128)(2,1)S(1)}, u32[]{:S(2)}, u32[]{:S(2)}) collective-permute-start(bf16[16,3200]{1,0:T(8,128)(2,1)S(1)} %get-tuple-element.30), channel_id=1, source_target_pairs={{0,24},{1,26},{2,25},{3,27},{4,28},{5,30},{6,29},{7,31},{8,0},{9,2... | collective-permute-start | bytes 307208 | tf_op jit(solution)/shard_map/ppermute | solution.py:45
  22.7 0.6 %collective-permute-start.9 = (bf16[16,3200]{1,0:T(8,128)(2,1)S(1)}, bf16[16,3200]{1,0:T(8,128)(2,1)S(1)}, u32[]{:S(2)}, u32[]{:S(2)}) collective-permute-start(bf16[16,3200]{1,0:T(8,128)(2,1)S(1)} %get-tuple-element.31), channel_id=1, source_target_pairs={{0,28},{1,30},{2,29},{3,31},{4,24},{5,26},{6,25},{7,27},{8,4},{9,6... | collective-permute-start | bytes 307208 | tf_op jit(solution)/shard_map/ppermute | solution.py:45
  23.3 2.8 %weight_grads.1 = (bf16[3072,256]{1,0:T(8,128)(2,1)}, bf16[3072,256]{1,0:T(8,128)(2,1)}, bf16[256,3072]{1,0:T(8,128)(2,1)}) custom-call(bf16[16,3200]{1,0:T(8,128)(2,1)S(1)} %get-tuple-element.23.refs_0_, bf16[16,3200]{1,0:T(8,128)(2,1)S(1)} %collective-permute-done.refs_1_, bf16[16,3200]{1,0:T(8,128)(2,1)S(1)} %collective-permute-done.1.refs_2_, ...), custom_call_target="tpu_custom_call" | custom-call | flops 603979776 | bytes 4718592 | tf_op jit(solution)/shard_map/weight_grads/pallas_call | solution.py:365
  26.1 1.3 %collective-permute-start.11 = (f32[16,1]{1,0:T(8,128)S(1)}, f32[16,1]{1,0:T(8,128)S(1)}, u32[]{:S(2)}, u32[]{:S(2)}) collective-permute-start(f32[16,1]{1,0:T(8,128)S(1)} %concatenate.3), channel_id=1, source_target_pairs={{0,4},{1,5},{2,6},{3,7},{4,0},{5,1},{6,2},{7,3},{8,12},{9,13},{10,... | collective-permute-start | bytes 200 | tf_op jit(solution)/shard_map/ppermute | solution.py:31
  27.4 1.6 %collective-permute-done.9.refs_1_ = bf16[16,3200]{1,0:T(8,128)(2,1)S(1)} collective-permute-done((bf16[16,3200]{1,0:T(8,128)(2,1)S(1)}, bf16[16,3200]{1,0:T(8,128)(2,1)S(1)}, u32[]{:S(2)}, u32[]{:S(2)}) %collective-permute-start.9) | collective-permute-done | bytes 102432 | tf_op jit(solution)/shard_map/ppermute | solution.py:45
  29.0 0.6 %collective-permute-start.10 = (bf16[8,3200]{1,0:T(8,128)(2,1)S(1)}, bf16[8,3200]{1,0:T(8,128)(2,1)S(1)}, u32[]{:S(2)}, u32[]{:S(2)}) collective-permute-start(bf16[8,3200]{1,0:T(8,128)(2,1)S(1)} %get-tuple-element.33), channel_id=1, source_target_pairs={{0,2},{1,3},{2,0},{3,1},{4,6},{5,7},{6,4},{7,5},{8,10},{9,11},{10,... | collective-permute-start | bytes 153608 | tf_op jit(solution)/shard_map/ppermute | solution.py:31
  29.6 0.2 collective-permute-done.11
  29.8 1.9 %collective-permute-start.12 = (f32[8,1]{1,0:T(8,128)S(1)}, f32[8,1]{1,0:T(8,128)S(1)}, u32[]{:S(2)}, u32[]{:S(2)}) collective-permute-start(f32[8,1]{1,0:T(8,128)S(1)} %get-tuple-element.41), channel_id=1, source_target_pairs={{0,1},{1,0},{2,3},{3,2},{4,5},{5,4},{6,7},{7,6},{8,9},{9,8},{10,11... | collective-permute-start | bytes 104 | tf_op jit(solution)/shard_map/ppermute | solution.py:31
  31.7 1.7 %collective-permute-done.12.refs_1_ = f32[8,1]{1,0:T(8,128)S(1)} collective-permute-done((f32[8,1]{1,0:T(8,128)S(1)}, f32[8,1]{1,0:T(8,128)S(1)}, u32[]{:S(2)}, u32[]{:S(2)}) %collective-permute-start.12) | collective-permute-done | bytes 64 | tf_op jit(solution)/shard_map/ppermute | solution.py:31
  33.4 0.7 %score_grads.1 = f32[6,1,128]{2,1,0:T(1,128)} custom-call(s32[1]{0:T(128)} %bitcast.1.own_ref, s32[6,1,128]{2,1,0:T(1,128)S(1)} %bitcast.15, f32[6,1,128]{2,1,0:T(1,128)S(1)} %bitcast.17, bf16[16,128]{1,0:T(8,128)(2,1)S(1)} %get-tuple-element.34.select_ref, f32[8,1]{1,0:T(8,128)S(1)} %get-tuple-element.42.refs_0_, f32[8,1]{1,0:T(8,128)S(1)} %collective-permute-done.12.refs_1_), custom_call_target="tpu_custom_call" | custom-call | flops 1000 | bytes 1000 | tf_op jit(solution)/shard_map/score_grads/pallas_call | solution.py:401
  34.1 1.2 %spread_rows.1 = bf16[128,3072]{1,0:T(8,128)(2,1)} custom-call(bf16[8,3200]{1,0:T(8,128)(2,1)S(1)} %get-tuple-element.32.own_ref, bf16[8,3200]{1,0:T(8,128)(2,1)S(1)} %collective-permute-done.10.other_ref), custom_call_target="tpu_custom_call" | custom-call | flops 12582912 | bytes 786432 | tf_op jit(solution)/shard_map/spread_rows/pallas_call | solution.py:463
  (16 shorter events, 0.1 us)
Async XLA Ops:
  2.3 6.2 %collective-permute-start.1 = (bf16[16,3200]{1,0:T(8,128)(2,1)S(1)}, bf16[16,3200]{1,0:T(8,128)(2,1)S(1)}, u32[]{:S(2)}, u32[]{:S(2)}) collective-permute-start(bf16[16,3200]{1,0:T(8,128)(2,1)S(1)} %get-tuple-element.23.refs_0_), channel_id=1, source_target_pairs={{0,4},{1,5},{2,6},{3,7},{4,0},{5,1},{6,2},{7,3},{8,12},{9,13},{10,... | collective-permute-start | bytes 307208 | tf_op jit(solution)/shard_map/ppermute | solution.py:31
  5.3 5.8 %collective-permute-start = (bf16[16,3200]{1,0:T(8,128)(2,1)S(1)}, bf16[16,3200]{1,0:T(8,128)(2,1)S(1)}, u32[]{:S(2)}, u32[]{:S(2)}) collective-permute-start(bf16[16,3200]{1,0:T(8,128)(2,1)S(1)} %get-tuple-element.24), channel_id=1, source_target_pairs={{0,1},{1,0},{2,3},{3,2},{4,5},{5,4},{6,7},{7,6},{8,9},{9,8},{10,11... | collective-permute-start | bytes 307208 | tf_op jit(solution)/shard_map/ppermute | solution.py:31
  6.9 5.6 %collective-permute-start.2 = (bf16[16,3200]{1,0:T(8,128)(2,1)S(1)}, bf16[16,3200]{1,0:T(8,128)(2,1)S(1)}, u32[]{:S(2)}, u32[]{:S(2)}) collective-permute-start(bf16[16,3200]{1,0:T(8,128)(2,1)S(1)} %get-tuple-element.24), channel_id=1, source_target_pairs={{0,5},{1,4},{2,7},{3,6},{4,1},{5,0},{6,3},{7,2},{8,13},{9,12},{10,... | collective-permute-start | bytes 307208 | tf_op jit(solution)/shard_map/ppermute | solution.py:31
  6.9 7.2 %collective-permute-start.3 = (bf16[16,3200]{1,0:T(8,128)(2,1)S(1)}, bf16[16,3200]{1,0:T(8,128)(2,1)S(1)}, u32[]{:S(2)}, u32[]{:S(2)}) collective-permute-start(bf16[16,3200]{1,0:T(8,128)(2,1)S(1)} %get-tuple-element.23.refs_0_), channel_id=1, source_target_pairs={{0,2},{1,3},{2,0},{3,1},{4,6},{5,7},{6,4},{7,5},{8,10},{9,11},{10,... | collective-permute-start | bytes 307208 | tf_op jit(solution)/shard_map/ppermute | solution.py:31
  8.5 5.6 %collective-permute-start.5 = (bf16[16,3200]{1,0:T(8,128)(2,1)S(1)}, bf16[16,3200]{1,0:T(8,128)(2,1)S(1)}, u32[]{:S(2)}, u32[]{:S(2)}) collective-permute-start(bf16[16,3200]{1,0:T(8,128)(2,1)S(1)} %collective-permute-done.1.refs_2_), channel_id=1, source_target_pairs={{0,2},{1,3},{2,0},{3,1},{4,6},{5,7},{6,4},{7,5},{8,10},{9,11},{10,... | collective-permute-start | bytes 307208 | tf_op jit(solution)/shard_map/ppermute | solution.py:31
  11.1 3.0 %collective-permute-start.4 = (bf16[16,3200]{1,0:T(8,128)(2,1)S(1)}, bf16[16,3200]{1,0:T(8,128)(2,1)S(1)}, u32[]{:S(2)}, u32[]{:S(2)}) collective-permute-start(bf16[16,3200]{1,0:T(8,128)(2,1)S(1)} %collective-permute-done.refs_1_), channel_id=1, source_target_pairs={{0,2},{1,3},{2,0},{3,1},{4,6},{5,7},{6,4},{7,5},{8,10},{9,11},{10,... | collective-permute-start | bytes 307208 | tf_op jit(solution)/shard_map/ppermute | solution.py:31
  12.4 1.7 %collective-permute-start.6 = (bf16[16,3200]{1,0:T(8,128)(2,1)S(1)}, bf16[16,3200]{1,0:T(8,128)(2,1)S(1)}, u32[]{:S(2)}, u32[]{:S(2)}) collective-permute-start(bf16[16,3200]{1,0:T(8,128)(2,1)S(1)} %collective-permute-done.2.refs_3_), channel_id=1, source_target_pairs={{0,2},{1,3},{2,0},{3,1},{4,6},{5,7},{6,4},{7,5},{8,10},{9,11},{10,... | collective-permute-start | bytes 307208 | tf_op jit(solution)/shard_map/ppermute | solution.py:31
  17.3 16.2 %copy-start = (s32[1,128,6]{1,0,2:T(1,128)S(1)}, s32[1,128,6]{1,0,2:T(1,128)}, u32[]{:S(2)}) copy-start(s32[1,128,6]{1,0,2:T(1,128)} %param.9) | copy-start | bytes 9220
  17.3 16.2 %copy-start.1 = (f32[1,128,6]{1,0,2:T(1,128)S(1)}, f32[1,128,6]{1,0,2:T(1,128)}, u32[]{:S(2)}) copy-start(f32[1,128,6]{1,0,2:T(1,128)} %param.10) | copy-start | bytes 9220
  17.3 1.7 %collective-permute-start.7 = (bf16[32,3200]{1,0:T(8,128)(2,1)S(1)}, bf16[32,3200]{1,0:T(8,128)(2,1)S(1)}, u32[]{:S(2)}, u32[]{:S(2)}) collective-permute-start(bf16[32,3200]{1,0:T(8,128)(2,1)S(1)} %get-tuple-element.29), channel_id=1, source_target_pairs={{0,2},{1,3},{2,0},{3,1},{4,6},{5,7},{6,4},{7,5},{8,10},{9,11},{10,... | collective-permute-start | bytes 614408 | tf_op jit(solution)/shard_map/ppermute | solution.py:31
  19.1 8.4 %collective-permute-start.8 = (bf16[16,3200]{1,0:T(8,128)(2,1)S(1)}, bf16[16,3200]{1,0:T(8,128)(2,1)S(1)}, u32[]{:S(2)}, u32[]{:S(2)}) collective-permute-start(bf16[16,3200]{1,0:T(8,128)(2,1)S(1)} %get-tuple-element.30), channel_id=1, source_target_pairs={{0,24},{1,26},{2,25},{3,27},{4,28},{5,30},{6,29},{7,31},{8,0},{9,2... | collective-permute-start | bytes 307208 | tf_op jit(solution)/shard_map/ppermute | solution.py:45
  22.7 6.4 %collective-permute-start.9 = (bf16[16,3200]{1,0:T(8,128)(2,1)S(1)}, bf16[16,3200]{1,0:T(8,128)(2,1)S(1)}, u32[]{:S(2)}, u32[]{:S(2)}) collective-permute-start(bf16[16,3200]{1,0:T(8,128)(2,1)S(1)} %get-tuple-element.31), channel_id=1, source_target_pairs={{0,28},{1,30},{2,29},{3,31},{4,24},{5,26},{6,25},{7,27},{8,4},{9,6... | collective-permute-start | bytes 307208 | tf_op jit(solution)/shard_map/ppermute | solution.py:45
  26.1 3.7 %collective-permute-start.11 = (f32[16,1]{1,0:T(8,128)S(1)}, f32[16,1]{1,0:T(8,128)S(1)}, u32[]{:S(2)}, u32[]{:S(2)}) collective-permute-start(f32[16,1]{1,0:T(8,128)S(1)} %concatenate.3), channel_id=1, source_target_pairs={{0,4},{1,5},{2,6},{3,7},{4,0},{5,1},{6,2},{7,3},{8,12},{9,13},{10,... | collective-permute-start | bytes 200 | tf_op jit(solution)/shard_map/ppermute | solution.py:31
  29.0 5.0 %collective-permute-start.10 = (bf16[8,3200]{1,0:T(8,128)(2,1)S(1)}, bf16[8,3200]{1,0:T(8,128)(2,1)S(1)}, u32[]{:S(2)}, u32[]{:S(2)}) collective-permute-start(bf16[8,3200]{1,0:T(8,128)(2,1)S(1)} %get-tuple-element.33), channel_id=1, source_target_pairs={{0,2},{1,3},{2,0},{3,1},{4,6},{5,7},{6,4},{7,5},{8,10},{9,11},{10,... | collective-permute-start | bytes 153608 | tf_op jit(solution)/shard_map/ppermute | solution.py:31
  29.8 3.6 %collective-permute-start.12 = (f32[8,1]{1,0:T(8,128)S(1)}, f32[8,1]{1,0:T(8,128)S(1)}, u32[]{:S(2)}, u32[]{:S(2)}) collective-permute-start(f32[8,1]{1,0:T(8,128)S(1)} %get-tuple-element.41), channel_id=1, source_target_pairs={{0,1},{1,0},{2,3},{3,2},{4,5},{5,4},{6,7},{7,6},{8,9},{9,8},{10,11... | collective-permute-start | bytes 104 | tf_op jit(solution)/shard_map/ppermute | solution.py:31

commit v4 on v3

--- a/solution.py
+++ b/solution.py
@@ -45,7 +45,7 @@
     return lax.ppermute(value, ("pipe", "dp", "expert"), pairs)
 
 
-def pick_kernel(capacity, own_ref, ids_hbm, weight_hbm, acts_hbm, grad_hbm, *refs):
+def pick_kernel(capacity, index_ref, ids_hbm, weight_hbm, acts_hbm, grad_hbm, *refs):
     outs = refs[:2]
     select_ref, ids_ref, weight_ref, acts_ref, grad_ref, sems = refs[2:]
     copies = [
@@ -60,7 +60,7 @@
     width = acts_ref.shape[1]
     rows = 2 * capacity
     row = lax.broadcasted_iota(jnp.int32, (rows, tokens), 0)
-    row_expert = (row // capacity) ^ own_ref[0]
+    row_expert = (row // capacity) ^ (index_ref[0] & 1)
     before = lax.broadcasted_iota(jnp.int32, (tokens, tokens), 0)
     after = lax.broadcasted_iota(jnp.int32, (tokens, tokens), 1)
     earlier = jnp.where(before < after, 1.0, 0.0).astype(jnp.bfloat16)
@@ -93,7 +93,7 @@
         outs[j][:, width:] = jnp.concatenate([marks[part]] * 2, axis=0).astype(jnp.bfloat16)
 
 
-def pick_rows(own, ids, weights, acts, grads, capacity):
+def pick_rows(index, ids, weights, acts, grads, capacity):
     tokens, width = acts.shape
     group = shape_of((2 * capacity, width + LANES), jnp.bfloat16)
     return pl.pallas_call(
@@ -111,30 +111,30 @@
         cost_estimate=cost(8 * capacity * tokens * width, 4 * tokens * width),
         compiler_params=pltpu.CompilerParams(vmem_limit_bytes=16 * 2**20),
         name="pick_rows",
-    )(own, ids, weights, acts, grads)
-
-
-def load_kernel(gate_hbm, upper_hbm, gate_ref, upper_ref, sems):
-    gate_copy = pltpu.make_async_copy(gate_hbm, gate_ref, sems.at[0])
-    upper_copy = pltpu.make_async_copy(upper_hbm.at[: upper_ref.shape[0]], upper_ref, sems.at[1])
-    gate_copy.start()
-    upper_copy.start()
-    gate_copy.wait()
-    upper_copy.wait()
-
-
-def load_weights(gate, upper):
-    width, units = gate.shape
+    )(index, ids, weights, acts, grads)
+
+
+def load_kernel(*refs):
+    count = len(refs) // 2
+    sems = refs[-1]
+    copies = [pltpu.make_async_copy(refs[i], refs[count + i], sems.at[i]) for i in range(count)]
+    for copy in copies:
+        copy.start()
+    for copy in copies:
+        copy.wait()
+
+
+def load_weights(*arrays):
     return pl.pallas_call(
         load_kernel,
-        out_shape=[shape_of((width, units), gate.dtype), shape_of((width // 2, units), upper.dtype)],
-        in_specs=[HBM] * 2,
-        out_specs=[VMEM] * 2,
-        scratch_shapes=[pltpu.SemaphoreType.DMA((2,))],
-        cost_estimate=cost(0, 3 * width * units),
-        compiler_params=pltpu.CompilerParams(vmem_limit_bytes=24 * 2**20),
+        out_shape=[shape_of(array.shape, array.dtype) for array in arrays],
+        in_specs=[HBM] * len(arrays),
+        out_specs=[VMEM] * len(arrays),
+        scratch_shapes=[pltpu.SemaphoreType.DMA((len(arrays),))],
+        cost_estimate=cost(0, 2 * sum(array.size for array in arrays)),
+        compiler_params=pltpu.CompilerParams(vmem_limit_bytes=16 * 2**20),
         name="load_weights",
-    )(gate, upper)
+    )(*arrays)
 
 
 def weave(value, capacity, upper):
@@ -162,25 +162,17 @@
             pltpu.matmul_acc_lhs(total, left(), load_staged_rhs=staged[i - ahead][1])
 
 
-def hidden_kernel(capacity, offsets, swapped_ref, *refs):
+def hidden_kernel(capacity, offsets, index_ref, *refs):
     pieces = len(offsets)
+    swapped = (index_ref[0] ^ (index_ref[0] >> 1)) & 1
     piece_refs = refs[:pieces]
-    gate_ref, head_ref, upper_hbm, lower_hbm = refs[pieces : pieces + 4]
-    keep_ref, send_ref, score_ref, delta_ref, hidden_ref = refs[pieces + 4 : pieces + 9]
-    tail_ref, lower_ref, sems = refs[pieces + 9 :]
+    gate_ref, upper_ref, lower_ref = refs[pieces : pieces + 3]
+    keep_ref, send_ref, delta_ref, hidden_ref = refs[pieces + 3 : pieces + 7]
+    score_refs = refs[pieces + 7 :]
     width, units = gate_ref.shape
-    middle_row = head_ref.shape[0]
     rows = pieces * capacity
     half = rows // 2
     tile = units
-    tail_copy = pltpu.make_async_copy(upper_hbm.at[middle_row:], tail_ref, sems.at[0])
-    lower_copies = [
-        pltpu.make_async_copy(lower_hbm.at[:, part], lower_ref.at[:, part], sems.at[1 + i])
-        for i, part in enumerate((slice(0, middle_row), slice(middle_row, width)))
-    ]
-    tail_copy.start()
-    for copy in lower_copies:
-        copy.start()
 
     def acts(start):
         return jnp.concatenate([ref[:capacity, start : start + tile] for ref in piece_refs], axis=0)
@@ -195,7 +187,7 @@
             )
             for chosen in wanted
         ]
-        return jnp.where(swapped_ref[0] == 1, lists[1], lists[0])
+        return jnp.where(swapped == 1, lists[1], lists[0])
 
     chips = [4 * x for x in range(pieces // 4)]
     kept = ([x | c for x in chips for c in (0, 2)], [x | c | 1 for x in chips for c in (2, 0)])
@@ -208,32 +200,22 @@
         return lambda: ref[:, start : start + tile]
 
     def forward(first, second):
-        def steps(starts, upper_ref, base):
-            result = []
-            for start in starts:
-                left = functools.partial(acts, start)
-                result.append((0, at(gate_ref, start), False, left, first))
-                result.append((1, at(upper_ref, start - base), False, left, second))
-            return result
-
-        chain(steps(range(0, middle_row, tile), head_ref, 0))
-        tail_copy.wait()
-        chain(steps(range(middle_row, width, tile), tail_ref, middle_row))
+        steps = []
+        for start in range(0, width, tile):
+            left = functools.partial(acts, start)
+            steps.append((0, at(gate_ref, start), False, left, first))
+            steps.append((1, at(upper_ref, start), False, left, second))
+        chain(steps)
         return pltpu.matmul_pop(first), pltpu.matmul_pop(second)
 
     def backward(first, second):
         totals = (first, second)
-
-        def steps(starts):
-            return [
+        chain(
+            [
                 (i % 2, at_column(lower_ref, start), True, functools.partial(grads, start), totals[i % 2])
-                for i, start in enumerate(starts)
+                for i, start in enumerate(range(0, width, tile))
             ]
-
-        lower_copies[0].wait()
-        chain(steps(range(0, middle_row, tile)))
-        lower_copies[1].wait()
-        chain(steps(range(middle_row, width, tile)))
+        )
         return pltpu.matmul_pop(first) + pltpu.matmul_pop(second)
 
     totals = [pltpu.ACC(unit)((rows, tile), jnp.float32) for unit in range(2)]
@@ -257,12 +239,8 @@
             for source in range(2):
                 for i, start in enumerate(starts[group : group + 4]):
                     unit = i % 2
-                    if source == 0:
-                        weights, left = at(gate_ref, start), gate_part
-                    elif start < middle_row:
-                        weights, left = at(head_ref, start), upper_part
-                    else:
-                        weights, left = at(tail_ref, start - middle_row), upper_part
+                    weights = at((gate_ref, upper_ref)[source], start)
+                    left = (gate_part, upper_part)[source]
                     total = accs[2 * ((group // 4 * 2 + i // 2) % 2) + unit]
                     steps.append((unit, weights, True, lambda left=left: left, total))
             ordered = [steps[i] for i in (0, 1, 4, 5, 2, 3, 6, 7) if i < len(steps)] if len(steps) == 8 else steps
@@ -274,20 +252,16 @@
                 send_ref[:, start : start + tile] = block[half:].astype(jnp.bfloat16)
 
     pl.run_scoped(back, *totals, *totals)
-    score_ref[...] = jnp.broadcast_to(scores[:half], (half, LANES))
-    rest = scores[half:]
-    high = rest.astype(jnp.bfloat16).astype(jnp.float32)
-    middle = (rest - high).astype(jnp.bfloat16).astype(jnp.float32)
-    low = rest - high - middle
-    lane = lax.broadcasted_iota(jnp.int32, (half, LANES), 1)
-    parts = jnp.where(lane == 0, high, jnp.where(lane == 1, middle, jnp.where(lane == 2, low, 0.0)))
-    send_ref[:, width:] = parts.astype(jnp.bfloat16)
+    lane = lax.broadcasted_iota(jnp.int32, (capacity, LANES), 1)
+    for x, ref in enumerate(score_refs):
+        spots = [offsets.index(4 * x + j) * capacity for j in range(4)]
+        ref[...] = sum(jnp.where(lane == j, scores[spot : spot + capacity], 0.0) for j, spot in enumerate(spots))
     delta_ref[:, :units] = weave(delta_gate, capacity, True).astype(jnp.bfloat16)
     delta_ref[:, units:] = weave(delta_up, capacity, True).astype(jnp.bfloat16)
     hidden_ref[...] = weave(hidden, capacity, False).astype(jnp.bfloat16)
 
 
-def hidden_pass(swapped, pieces, offsets, gate, head, upper, lower, capacity):
+def hidden_pass(index, pieces, offsets, gate, upper, lower, capacity):
     width, units = gate.shape
     count = len(pieces)
     half = count * capacity // 2
@@ -296,117 +270,123 @@
         functools.partial(hidden_kernel, capacity, offsets),
         out_shape=[
             shape_of((half, width + LANES), jnp.float32),
-            shape_of((half, width + LANES), jnp.bfloat16),
-            shape_of((half, LANES), jnp.float32),
+            shape_of((half, width), jnp.bfloat16),
             shape_of((rows, 2 * units), jnp.bfloat16),
             shape_of((rows, units), jnp.bfloat16),
-        ],
-        in_specs=[pl.BlockSpec(memory_space=pltpu.SMEM)] + [VMEM] * (count + 2) + [HBM] * 2,
-        out_specs=[VMEM] * 5,
-        scratch_shapes=[
-            pltpu.VMEM((width - head.shape[0], units), jnp.bfloat16),
-            pltpu.VMEM((units, width), jnp.bfloat16),
-            pltpu.SemaphoreType.DMA((3,)),
-        ],
+        ]
+        + [shape_of((capacity, LANES), jnp.float32)] * (count // 4),
+        in_specs=[pl.BlockSpec(memory_space=pltpu.SMEM)] + [VMEM] * (count + 3),
+        out_specs=[VMEM] * (4 + count // 4),
         cost_estimate=cost(10 * rows * width * units, 6 * width * units),
         compiler_params=pltpu.CompilerParams(vmem_limit_bytes=24 * 2**20),
         name="hidden_pass",
-    )(swapped, *pieces, gate, head, upper, lower)
-
-
-def join_kernel(width, messages, keep_ref, score_ref, recv_ref, *out_refs):
-    for j in range(messages):
-        rows = out_refs[j].shape[0]
+    )(index, *pieces, gate, upper, lower)
+
+
+def join_kernel(keep_ref, recv_ref, *out_refs):
+    width = recv_ref.shape[1]
+    for j, ref in enumerate(out_refs):
+        rows = ref.shape[0]
         part = slice(j * rows, (j + 1) * rows)
-        other = recv_ref[part, :width].astype(jnp.float32)
-        out_refs[j][:, :width] = (keep_ref[part, :width] + other).astype(jnp.bfloat16)
-        out_refs[j][:, width:] = keep_ref[part, width:].astype(jnp.bfloat16)
-    extra = recv_ref[:, width:].astype(jnp.float32)
-    out_refs[messages][...] = score_ref[...] + jnp.sum(extra, axis=1, keepdims=True)
-
-
-def join_cores(keep, scores, recv, messages):
+        ref[:, :width] = (keep_ref[part, :width] + recv_ref[part].astype(jnp.float32)).astype(jnp.bfloat16)
+        ref[:, width:] = keep_ref[part, width:].astype(jnp.bfloat16)
+
+
+def join_cores(keep, recv, messages):
     half, wide = keep.shape
     return pl.pallas_call(
-        functools.partial(join_kernel, wide - LANES, messages),
-        out_shape=[shape_of((half // messages, wide), jnp.bfloat16)] * messages
-        + [shape_of((half, LANES), jnp.float32)],
-        in_specs=[VMEM] * 3,
-        out_specs=[VMEM] * (messages + 1),
+        join_kernel,
+        out_shape=[shape_of((half // messages, wide), jnp.bfloat16)] * messages,
+        in_specs=[VMEM] * 2,
+        out_specs=[VMEM] * messages,
         cost_estimate=cost(2 * half * wide, 8 * half * wide),
         compiler_params=pltpu.CompilerParams(vmem_limit_bytes=8 * 2**20),
         name="join_cores",
-    )(keep, scores, recv)
-
-
-def weights_kernel(pieces, step, *refs):
+    )(keep, recv)
+
+
+def weights_kernel(pieces, chunks, *refs):
     piece_refs = refs[:pieces]
-    delta_ref, hidden_ref, gate_out, upper_out, lower_out = refs[pieces:]
-    start = pl.multiple_of(pl.program_id(0) * step, step)
-    rows = jnp.concatenate([ref[:, pl.ds(start, step)] for ref in piece_refs], axis=0)
+    delta_ref, hidden_ref, *outs = refs[pieces:]
+    hbm_refs, buffers, sems = outs[:3], outs[3:6], outs[6]
+    width, units = buffers[0].shape
     down = (((0,), (0,)), ((), ()))
-    both = lax.dot_general(rows, delta_ref[...], down, preferred_element_type=jnp.float32)
-    units = gate_out.shape[1]
-    gate_out[...] = both[:, :units].astype(jnp.bfloat16)
-    upper_out[...] = both[:, units:].astype(jnp.bfloat16)
-    lower_out[...] = lax.dot_general(
-        hidden_ref[...], rows, down, preferred_element_type=jnp.float32
-    ).astype(jnp.bfloat16)
-
-
-def weight_grads(pieces, delta, hidden, step):
+    copies = []
+    for i in range(chunks):
+        part = slice(i * width // chunks, (i + 1) * width // chunks)
+        rows = jnp.concatenate([ref[:, part] for ref in piece_refs], axis=0)
+        both = lax.dot_general(rows, delta_ref[...], down, preferred_element_type=jnp.float32)
+        buffers[0][part] = both[:, :units].astype(jnp.bfloat16)
+        buffers[1][part] = both[:, units:].astype(jnp.bfloat16)
+        buffers[2][:, part] = lax.dot_general(
+            hidden_ref[...], rows, down, preferred_element_type=jnp.float32
+        ).astype(jnp.bfloat16)
+        for j, spot in enumerate(((part,), (part,), (slice(None), part))):
+            copy = pltpu.make_async_copy(buffers[j].at[spot], hbm_refs[j].at[spot], sems.at[j, i])
+            copy.start()
+            copies.append(copy)
+    for copy in copies:
+        copy.wait()
+
+
+def weight_grads(pieces, delta, hidden, chunks):
     width = pieces[0].shape[1] - LANES
     rows, units = hidden.shape
     count = len(pieces)
-
-    def whole(array):
-        return pl.BlockSpec(array.shape, lambda i: (0, 0))
-
-    return pl.pallas_call(
-        functools.partial(weights_kernel, count, step),
-        grid=(width // step,),
-        out_shape=[
-            shape_of((width, units), jnp.bfloat16),
-            shape_of((width, units), jnp.bfloat16),
-            shape_of((units, width), jnp.bfloat16),
-        ],
-        in_specs=[whole(array) for array in (*pieces, delta, hidden)],
-        out_specs=[
-            pl.BlockSpec((step, units), lambda i: (i, 0)),
-            pl.BlockSpec((step, units), lambda i: (i, 0)),
-            pl.BlockSpec((units, step), lambda i: (0, i)),
-        ],
+    shapes = [(width, units), (width, units), (units, width)]
+    return pl.pallas_call(
+        functools.partial(weights_kernel, count, chunks),
+        out_shape=[shape_of(shape, jnp.bfloat16) for shape in shapes],
+        in_specs=[VMEM] * (count + 2),
+        out_specs=[HBM] * 3,
+        scratch_shapes=[pltpu.VMEM(shape, jnp.bfloat16) for shape in shapes]
+        + [pltpu.SemaphoreType.DMA((3, chunks))],
         cost_estimate=cost(6 * rows * width * units, 6 * width * units),
         compiler_params=pltpu.CompilerParams(vmem_limit_bytes=24 * 2**20),
         name="weight_grads",
     )(*pieces, delta, hidden)
 
 
-def score_kernel(capacity, own_ref, ids_ref, weight_ref, select_ref, *refs):
-    out_ref = refs[-1]
+def add_kernel(left_ref, right_ref, out_ref):
+    out_ref[...] = left_ref[...] + right_ref[...]
+
+
+def add_scores(left, right):
+    return pl.pallas_call(
+        add_kernel,
+        out_shape=shape_of(left.shape, jnp.float32),
+        in_specs=[VMEM] * 2,
+        out_specs=VMEM,
+        cost_estimate=cost(left.size, 12 * left.size),
+        compiler_params=pltpu.CompilerParams(vmem_limit_bytes=2**20),
+        name="add_scores",
+    )(left, right)
+
+
+def score_kernel(capacity, index_ref, ids_ref, weight_ref, select_ref, near_ref, core_ref, other_ref, out_ref):
     chosen, _, tokens = ids_ref.shape
+    scores = (near_ref[:, 0:1] + core_ref[:, 2:3], other_ref[:, 1:2])
     sums = []
     for j in range(2):
-        part = slice(j * capacity, (j + 1) * capacity)
-        picked = select_ref[part].astype(jnp.float32) * refs[j][:, :1]
+        picked = select_ref[j * capacity : (j + 1) * capacity].astype(jnp.float32) * scores[j]
         sums.append(jnp.sum(picked, axis=0, keepdims=True))
     for k in range(chosen):
         value = jnp.zeros((1, tokens), jnp.float32)
         for j in range(2):
-            value = jnp.where(ids_ref[k] == (own_ref[0] ^ j), sums[j], value)
+            value = jnp.where(ids_ref[k] == ((index_ref[0] & 1) ^ j), sums[j], value)
         out_ref[k] = value / weight_ref[k]
 
 
-def score_grads(own, ids, weights, select, scores, capacity):
+def score_grads(index, ids, weights, select, near, core, other, capacity):
     return pl.pallas_call(
         functools.partial(score_kernel, capacity),
         out_shape=shape_of(weights.shape, jnp.float32),
-        in_specs=[pl.BlockSpec(memory_space=pltpu.SMEM)] + [VMEM] * 5,
+        in_specs=[pl.BlockSpec(memory_space=pltpu.SMEM)] + [VMEM] * 6,
         out_specs=VMEM,
         cost_estimate=cost(1000, 1000),
         compiler_params=pltpu.CompilerParams(vmem_limit_bytes=4 * 2**20),
         name="score_grads",
-    )(own, ids, weights, select, *scores)
+    )(index, ids, weights, select, near, core, other)
 
 
 def total_kernel(messages, *refs):
@@ -474,48 +454,35 @@
 
 def pairwise_shards(block_input, output_grad, expert_ids, gate_weights, gate_proj, up_proj, down_proj):
     tokens = block_input.shape[1]
-    width = block_input.shape[2]
     capacity = tokens // 16
     count = 2 * lax.axis_size("dp")
     plane = [offset for offset in range(count) if not offset & 2]
     offsets = plane + [offset | 2 for offset in plane]
-    expert_index = lax.axis_index("expert").astype(jnp.int32)
-    core_index = lax.axis_index("dp").astype(jnp.int32) & 1
-    own = expert_index.reshape(1)
-    swapped = (expert_index ^ core_index).reshape(1)
+    index = lax.axis_index(("dp", "expert")).astype(jnp.int32).reshape(1)
     ids = jnp.transpose(expert_ids, (2, 0, 1))
     weights = jnp.transpose(gate_weights, (2, 0, 1))
     stay = functools.partial(pltpu.with_memory_space_constraint, memory_space=pltpu.HBM)
-    *sends, select = pick_rows(
-        own, stay(ids), stay(weights), stay(block_input[0]), stay(output_grad[0]), capacity
-    )
-    upper, lower = stay(up_proj[0, 0]), stay(down_proj[0, 0])
-    gate, head = load_weights(stay(gate_proj[0, 0]), upper)
+    *sends, select = pick_rows(index, stay(ids), stay(weights), stay(block_input[0]), stay(output_grad[0]), capacity)
+    gate, upper, lower = load_weights(*[stay(array[0, 0]) for array in (gate_proj, up_proj, down_proj)])
     mine = {0: sends[0]}
     for offset in sorted(plane[1:], reverse=True):
         mine[offset] = swap(sends[offset % 2], offset)
     theirs = {offset: swap(mine[offset], 2) for offset in plane}
     pieces = [mine[offset] for offset in plane] + [theirs[offset] for offset in plane]
-    keep, send, scores, delta, hidden = hidden_pass(
-        swapped, pieces, offsets, gate, head, upper, lower, capacity
+    keep, send, delta, hidden, near, *far = hidden_pass(
+        index, pieces, offsets, gate, upper, lower, capacity
     )
     recv = swap(send, 2)
+    for scores in far:
+        moved = swap(scores, 4)
+        near = add_scores(near, moved)
     chips = count // 4
-    *joined, scores = join_cores(keep, scores, recv, chips)
+    joined = join_cores(keep, recv, chips)
     messages = [send_back(joined[x], x) for x in range(chips)]
-    gate_grad, upper_grad, lower_grad = weight_grads(pieces, delta, hidden, width // 2)
-    score_rows = {offset: scores[i * capacity : (i + 1) * capacity, :1] for i, offset in enumerate(plane)}
-    bit = count // 2
-    while bit > 2:
-        low = [offset for offset in score_rows if not offset & bit]
-        moved = swap(jnp.concatenate([score_rows[offset | bit] for offset in low]), bit)
-        score_rows = {
-            offset: score_rows[offset] + moved[i * capacity : (i + 1) * capacity]
-            for i, offset in enumerate(low)
-        }
-        bit //= 2
-    score_list = [score_rows[0], swap(score_rows[1], 1)]
-    weight_grad = score_grads(own, ids, weights, select, score_list, capacity)
+    gate_grad, upper_grad, lower_grad = weight_grads(pieces, delta, hidden, 6)
+    core = swap(near, 2)
+    other = swap(near[:, :2] + core[:, 2:4], 1)
+    weight_grad = score_grads(index, ids, weights, select, near, core, other, capacity)
     own_rows, other_rows = total_rows(messages)
     received = spread_rows(own_rows, swap(other_rows, 2), tokens, 3)
     return (

time: 35.5 us -> 36.3 us (1.023)
  waiting for transfers between devices: 10.1 us -> 12.3 us
  starting transfers between devices: 13.1 us -> 12.2 us
  Pallas kernels: 11.3 us -> 10.8 us
    ppermute x2, waiting for transfers between devices: 1.61 us -> 3.87 us  [send_back(): return lax.ppermute(value, ('pipe', 'dp', 'expert'), pairs)]
    pallas_call x1, Pallas kernels: 3.15 us -> 2.09 us  [hidden_pass(): pl.pallas_call(functools.partial(hidden_kernel, capacity, offsets), out_s...]
    ppermute x11 -> x12, starting transfers between devices: 8.93 us -> 7.9 us  [swap(): lax.ppermute(value, ('dp', 'expert'), [(i, i ^ offset) for i in range(cou...]
    pallas_call x3 -> x4, Pallas kernels: 4.57 us -> 5.07 us  [the longest x1 2.64 us: weight_grads(): pl.pallas_call(functools.partial(weights_kernel, count, chunks), out_shap...]
    ppermute x11 -> x12, waiting for transfers between devices: 8.53 us -> 8.42 us  [swap(): lax.ppermute(value, ('dp', 'expert'), [(i, i ^ offset) for i in range(cou...]
  transfers between devices with their start and end apart: 13 -> 14, of which waited for: 7 -> 6; matrix products, arithmetic and copies ran while one was open for 0% -> 0% of each run, Pallas kernels for 15% -> 16%
where the time goes in v4:
time: 36.3 us; the launch traced here: 36.1 us
  waiting for transfers between devices  12.3 us (34%)
  starting transfers between devices  12.2 us (34%)
  Pallas kernels  10.8 us (30%)
  between operations  0.76 us (2%)
    ppermute x12, waiting for transfers between devices, swap(): lax.ppermute(value, ('dp', 'expert'), [(i, i ^ offset) for i in range(cou...  8.42 us
    ppermute x12, starting transfers between devices, swap(): lax.ppermute(value, ('dp', 'expert'), [(i, i ^ offset) for i in range(cou...  7.9 us
    ppermute x2, starting transfers between devices, send_back(): return lax.ppermute(value, ('pipe', 'dp', 'expert'), pairs)  4.27 us
    ppermute x2, waiting for transfers between devices, send_back(): return lax.ppermute(value, ('pipe', 'dp', 'expert'), pairs)  3.87 us
    pallas_call x1, Pallas kernels, weight_grads(): pl.pallas_call(functools.partial(weights_kernel, count, chunks), out_shap...  2.64 us
    pallas_call x1, Pallas kernels, load_weights(): pl.pallas_call(load_kernel, out_shape=[shape_of(array.shape, array.dtype)...  2.38 us
    pallas_call x1, Pallas kernels, hidden_pass(): pl.pallas_call(functools.partial(hidden_kernel, capacity, offsets), out_s...  2.09 us
    pallas_call x1, Pallas kernels, pick_rows(): pl.pallas_call(functools.partial(pick_kernel, capacity), out_shape=[group...  1.66 us
  transfers between devices with their start and end apart: 14, of which 6 were waited for; matrix products, arithmetic and copies ran while one was open for 0% of the time, Pallas kernels for 16%

profile of v4, /device:TPU:0, one launch (start us, length us, event | category | flops | bytes accessed | tf_op | source)
XLA Modules:
  0.0 36.1 jit_solution(2903004559850430590)
XLA Ops:
  0.6 1.7 %pick_rows.1 = (bf16[16,3200]{1,0:T(8,128)(2,1)S(1)}, bf16[16,3200]{1,0:T(8,128)(2,1)S(1)}, bf16[16,128]{1,0:T(8,128)(2,1)S(1)}) custom-call(s32[1]{0:T(128)} %bitcast.index_ref, s32[6,1,128]{2,1,0:T(1,128)} %bitcast.13, f32[6,1,128]{2,1,0:T(1,128)} %bitcast.15, bf16[128,3072]{1,0:T(8,128)(2,1)} %bitcast.20, bf16[128,3072]{1,0:T(8,128)(2,1)} %bitcast.21), custom_call_target="tpu_custom_call" | custom-call | flops 25165824 | bytes 1572864 | tf_op jit(solution)/shard_map/pick_rows/pallas_call | solution.py:99
  2.3 3.0 %collective-permute-start.1 = (bf16[16,3200]{1,0:T(8,128)(2,1)S(1)}, bf16[16,3200]{1,0:T(8,128)(2,1)S(1)}, u32[]{:S(2)}, u32[]{:S(2)}) collective-permute-start(bf16[16,3200]{1,0:T(8,128)(2,1)S(1)} %get-tuple-element.24.refs_0_), channel_id=1, source_target_pairs={{0,4},{1,5},{2,6},{3,7},{4,0},{5,1},{6,2},{7,3},{8,12},{9,13},{10,... | collective-permute-start | bytes 307208 | tf_op jit(solution)/shard_map/ppermute | solution.py:31
  5.3 1.5 %collective-permute-start = (bf16[16,3200]{1,0:T(8,128)(2,1)S(1)}, bf16[16,3200]{1,0:T(8,128)(2,1)S(1)}, u32[]{:S(2)}, u32[]{:S(2)}) collective-permute-start(bf16[16,3200]{1,0:T(8,128)(2,1)S(1)} %get-tuple-element.25), channel_id=1, source_target_pairs={{0,1},{1,0},{2,3},{3,2},{4,5},{5,4},{6,7},{7,6},{8,9},{9,8},{10,11... | collective-permute-start | bytes 307208 | tf_op jit(solution)/shard_map/ppermute | solution.py:31
  6.9 0.0 collective-permute-start.2
  6.9 1.6 %collective-permute-done.1.refs_2_ = bf16[16,3200]{1,0:T(8,128)(2,1)S(1)} collective-permute-done((bf16[16,3200]{1,0:T(8,128)(2,1)S(1)}, bf16[16,3200]{1,0:T(8,128)(2,1)S(1)}, u32[]{:S(2)}, u32[]{:S(2)}) %collective-permute-start.1) | collective-permute-done | bytes 102432 | tf_op jit(solution)/shard_map/ppermute | solution.py:31
  8.5 2.6 %collective-permute-done.refs_1_ = bf16[16,3200]{1,0:T(8,128)(2,1)S(1)} collective-permute-done((bf16[16,3200]{1,0:T(8,128)(2,1)S(1)}, bf16[16,3200]{1,0:T(8,128)(2,1)S(1)}, u32[]{:S(2)}, u32[]{:S(2)}) %collective-permute-start) | collective-permute-done | bytes 102432 | tf_op jit(solution)/shard_map/ppermute | solution.py:31
  11.1 1.3 %collective-permute-done.2.refs_3_ = bf16[16,3200]{1,0:T(8,128)(2,1)S(1)} collective-permute-done((bf16[16,3200]{1,0:T(8,128)(2,1)S(1)}, bf16[16,3200]{1,0:T(8,128)(2,1)S(1)}, u32[]{:S(2)}, u32[]{:S(2)}) %collective-permute-start.2) | collective-permute-done | bytes 102432 | tf_op jit(solution)/shard_map/ppermute | solution.py:31
  12.4 2.4 %load_weights.1 = (bf16[3072,256]{1,0:T(8,128)(2,1)S(1)}, bf16[3072,256]{1,0:T(8,128)(2,1)S(1)}, bf16[256,3072]{1,0:T(8,128)(2,1)S(1)}) custom-call(bf16[3072,256]{1,0:T(8,128)(2,1)} %bitcast.17, bf16[3072,256]{1,0:T(8,128)(2,1)} %bitcast.18, bf16[256,3072]{1,0:T(8,128)(2,1)} %bitcast.19), custom_call_target="tpu_custom_call" | custom-call | bytes 4718592 | tf_op jit(solution)/shard_map/load_weights/pallas_call | solution.py:128
  14.9 2.1 %hidden_pass.1 = (f32[32,3200]{1,0:T(8,128)S(1)}, bf16[32,3072]{1,0:T(8,128)(2,1)S(1)}, bf16[128,512]{1,0:T(8,128)(2,1)S(1)}, bf16[128,256]{1,0:T(8,128)(2,1)S(1...) custom-call(s32[1]{0:T(128)} %bitcast.index_ref, bf16[16,3200]{1,0:T(8,128)(2,1)S(1)} %get-tuple-element.24.refs_0_, ...), custom_call_target="tpu_custom_call" | custom-call | flops 1006632960 | bytes 4718592 | tf_op jit(solution)/shard_map/hidden_pass/pallas_call | solution.py:269
  16.9 0.0 copy-start
  17.0 0.0 copy-start.1
  17.0 0.6 %collective-permute-start.7 = (bf16[32,3072]{1,0:T(8,128)(2,1)S(1)}, bf16[32,3072]{1,0:T(8,128)(2,1)S(1)}, u32[]{:S(2)}, u32[]{:S(2)}) collective-permute-start(bf16[32,3072]{1,0:T(8,128)(2,1)S(1)} %get-tuple-element.30), channel_id=1, source_target_pairs={{0,2},{1,3},{2,0},{3,1},{4,6},{5,7},{6,4},{7,5},{8,10},{9,11},{10,... | collective-permute-start | bytes 589832 | tf_op jit(solution)/shard_map/ppermute | solution.py:31
  17.5 0.7 %collective-permute-start.11 = (f32[8,128]{1,0:T(8,128)S(1)}, f32[8,128]{1,0:T(8,128)S(1)}, u32[]{:S(2)}, u32[]{:S(2)}) collective-permute-start(f32[8,128]{1,0:T(8,128)S(1)} %get-tuple-element.37), channel_id=1, source_target_pairs={{0,4},{1,5},{2,6},{3,7},{4,0},{5,1},{6,2},{7,3},{8,12},{9,13},{10,... | collective-permute-start | bytes 12296 | tf_op jit(solution)/shard_map/ppermute | solution.py:31
  18.3 2.9 %collective-permute-done.11.right_ref = f32[8,128]{1,0:T(8,128)S(1)} collective-permute-done((f32[8,128]{1,0:T(8,128)S(1)}, f32[8,128]{1,0:T(8,128)S(1)}, u32[]{:S(2)}, u32[]{:S(2)}) %collective-permute-start.11) | collective-permute-done | bytes 4128 | tf_op jit(solution)/shard_map/ppermute | solution.py:31
  21.2 3.7 %collective-permute-start.8 = (bf16[16,3200]{1,0:T(8,128)(2,1)S(1)}, bf16[16,3200]{1,0:T(8,128)(2,1)S(1)}, u32[]{:S(2)}, u32[]{:S(2)}) collective-permute-start(bf16[16,3200]{1,0:T(8,128)(2,1)S(1)} %get-tuple-element.31), channel_id=1, source_target_pairs={{0,24},{1,26},{2,25},{3,27},{4,28},{5,30},{6,29},{7,31},{8,0},{9,2... | collective-permute-start | bytes 307208 | tf_op jit(solution)/shard_map/ppermute | solution.py:45
  24.9 0.6 %collective-permute-start.9 = (bf16[16,3200]{1,0:T(8,128)(2,1)S(1)}, bf16[16,3200]{1,0:T(8,128)(2,1)S(1)}, u32[]{:S(2)}, u32[]{:S(2)}) collective-permute-start(bf16[16,3200]{1,0:T(8,128)(2,1)S(1)} %get-tuple-element.32), channel_id=1, source_target_pairs={{0,28},{1,30},{2,29},{3,31},{4,24},{5,26},{6,25},{7,27},{8,4},{9,6... | collective-permute-start | bytes 307208 | tf_op jit(solution)/shard_map/ppermute | solution.py:45
  25.5 0.1 slice_add_fusion
  25.6 1.7 %collective-permute-start.13 = (f32[8,2]{1,0:T(8,128)S(1)}, f32[8,2]{1,0:T(8,128)S(1)}, u32[]{:S(2)}, u32[]{:S(2)}) collective-permute-start(f32[8,2]{1,0:T(8,128)S(1)} %slice_add_fusion), channel_id=1, source_target_pairs={{0,1},{1,0},{2,3},{3,2},{4,5},{5,4},{6,7},{7,6},{8,9},{9,8},{10,11... | collective-permute-start | bytes 200 | tf_op jit(solution)/shard_map/ppermute | solution.py:31
  27.2 0.9 %collective-permute-done.8.refs_0_ = bf16[16,3200]{1,0:T(8,128)(2,1)S(1)} collective-permute-done((bf16[16,3200]{1,0:T(8,128)(2,1)S(1)}, bf16[16,3200]{1,0:T(8,128)(2,1)S(1)}, u32[]{:S(2)}, u32[]{:S(2)}) %collective-permute-start.8) | collective-permute-done | bytes 102432 | tf_op jit(solution)/shard_map/ppermute | solution.py:45
  28.1 2.9 %collective-permute-done.9.refs_1_ = bf16[16,3200]{1,0:T(8,128)(2,1)S(1)} collective-permute-done((bf16[16,3200]{1,0:T(8,128)(2,1)S(1)}, bf16[16,3200]{1,0:T(8,128)(2,1)S(1)}, u32[]{:S(2)}, u32[]{:S(2)}) %collective-permute-start.9) | collective-permute-done | bytes 102432 | tf_op jit(solution)/shard_map/ppermute | solution.py:45
  31.1 0.4 %collective-permute-start.10 = (bf16[8,3200]{1,0:T(8,128)(2,1)S(1)}, bf16[8,3200]{1,0:T(8,128)(2,1)S(1)}, u32[]{:S(2)}, u32[]{:S(2)}) collective-permute-start(bf16[8,3200]{1,0:T(8,128)(2,1)S(1)} %get-tuple-element.34), channel_id=1, source_target_pairs={{0,2},{1,3},{2,0},{3,1},{4,6},{5,7},{6,4},{7,5},{8,10},{9,11},{10,... | collective-permute-start | bytes 153608 | tf_op jit(solution)/shard_map/ppermute | solution.py:31
  31.5 2.6 %weight_grads.1 = (bf16[3072,256]{1,0:T(8,128)(2,1)}, bf16[3072,256]{1,0:T(8,128)(2,1)}, bf16[256,3072]{1,0:T(8,128)(2,1)}) custom-call(bf16[16,3200]{1,0:T(8,128)(2,1)S(1)} %get-tuple-element.24.refs_0_, bf16[16,3200]{1,0:T(8,128)(2,1)S(1)} %collective-permute-done.refs_1_, bf16[16,3200]{1,0:T(8,128)(2,1)S(1)} %collective-permute-done.1.refs_2_, ...), custom_call_target="tpu_custom_call" | custom-call | flops 603979776 | bytes 4718592 | tf_op jit(solution)/shard_map/weight_grads/pallas_call | solution.py:337
  34.2 0.7 %score_grads.1 = f32[6,1,128]{2,1,0:T(1,128)} custom-call(s32[1]{0:T(128)} %bitcast.index_ref, s32[6,1,128]{2,1,0:T(1,128)S(1)} %bitcast.14, f32[6,1,128]{2,1,0:T(1,128)S(1)} %bitcast.16, bf16[16,128]{1,0:T(8,128)(2,1)S(1)} %get-tuple-element.35.select_ref, f32[8,128]{1,0:T(8,128)S(1)} %add_scores.1.near_ref, f32[8,128]{1,0:T(8,128)S(1)} %collective-permute-done.12.core_ref, ...), custom_call_target="tpu_custom_call" | custom-call | flops 1000 | bytes 1000 | tf_op jit(solution)/shard_map/score_grads/pallas_call | solution.py:381
  34.9 1.2 %spread_rows.1 = bf16[128,3072]{1,0:T(8,128)(2,1)} custom-call(bf16[8,3200]{1,0:T(8,128)(2,1)S(1)} %get-tuple-element.33.own_ref, bf16[8,3200]{1,0:T(8,128)(2,1)S(1)} %collective-permute-done.10.other_ref), custom_call_target="tpu_custom_call" | custom-call | flops 12582912 | bytes 786432 | tf_op jit(solution)/shard_map/spread_rows/pallas_call | solution.py:443
  (18 shorter events, 0.1 us)
Async XLA Ops:
  2.3 6.2 %collective-permute-start.1 = (bf16[16,3200]{1,0:T(8,128)(2,1)S(1)}, bf16[16,3200]{1,0:T(8,128)(2,1)S(1)}, u32[]{:S(2)}, u32[]{:S(2)}) collective-permute-start(bf16[16,3200]{1,0:T(8,128)(2,1)S(1)} %get-tuple-element.24.refs_0_), channel_id=1, source_target_pairs={{0,4},{1,5},{2,6},{3,7},{4,0},{5,1},{6,2},{7,3},{8,12},{9,13},{10,... | collective-permute-start | bytes 307208 | tf_op jit(solution)/shard_map/ppermute | solution.py:31
  5.3 5.8 %collective-permute-start = (bf16[16,3200]{1,0:T(8,128)(2,1)S(1)}, bf16[16,3200]{1,0:T(8,128)(2,1)S(1)}, u32[]{:S(2)}, u32[]{:S(2)}) collective-permute-start(bf16[16,3200]{1,0:T(8,128)(2,1)S(1)} %get-tuple-element.25), channel_id=1, source_target_pairs={{0,1},{1,0},{2,3},{3,2},{4,5},{5,4},{6,7},{7,6},{8,9},{9,8},{10,11... | collective-permute-start | bytes 307208 | tf_op jit(solution)/shard_map/ppermute | solution.py:31
  6.9 5.6 %collective-permute-start.2 = (bf16[16,3200]{1,0:T(8,128)(2,1)S(1)}, bf16[16,3200]{1,0:T(8,128)(2,1)S(1)}, u32[]{:S(2)}, u32[]{:S(2)}) collective-permute-start(bf16[16,3200]{1,0:T(8,128)(2,1)S(1)} %get-tuple-element.25), channel_id=1, source_target_pairs={{0,5},{1,4},{2,7},{3,6},{4,1},{5,0},{6,3},{7,2},{8,13},{9,12},{10,... | collective-permute-start | bytes 307208 | tf_op jit(solution)/shard_map/ppermute | solution.py:31
  6.9 7.9 %collective-permute-start.3 = (bf16[16,3200]{1,0:T(8,128)(2,1)S(1)}, bf16[16,3200]{1,0:T(8,128)(2,1)S(1)}, u32[]{:S(2)}, u32[]{:S(2)}) collective-permute-start(bf16[16,3200]{1,0:T(8,128)(2,1)S(1)} %get-tuple-element.24.refs_0_), channel_id=1, source_target_pairs={{0,2},{1,3},{2,0},{3,1},{4,6},{5,7},{6,4},{7,5},{8,10},{9,11},{10,... | collective-permute-start | bytes 307208 | tf_op jit(solution)/shard_map/ppermute | solution.py:31
  8.5 6.3 %collective-permute-start.5 = (bf16[16,3200]{1,0:T(8,128)(2,1)S(1)}, bf16[16,3200]{1,0:T(8,128)(2,1)S(1)}, u32[]{:S(2)}, u32[]{:S(2)}) collective-permute-start(bf16[16,3200]{1,0:T(8,128)(2,1)S(1)} %collective-permute-done.1.refs_2_), channel_id=1, source_target_pairs={{0,2},{1,3},{2,0},{3,1},{4,6},{5,7},{6,4},{7,5},{8,10},{9,11},{10,... | collective-permute-start | bytes 307208 | tf_op jit(solution)/shard_map/ppermute | solution.py:31
  11.1 3.7 %collective-permute-start.4 = (bf16[16,3200]{1,0:T(8,128)(2,1)S(1)}, bf16[16,3200]{1,0:T(8,128)(2,1)S(1)}, u32[]{:S(2)}, u32[]{:S(2)}) collective-permute-start(bf16[16,3200]{1,0:T(8,128)(2,1)S(1)} %collective-permute-done.refs_1_), channel_id=1, source_target_pairs={{0,2},{1,3},{2,0},{3,1},{4,6},{5,7},{6,4},{7,5},{8,10},{9,11},{10,... | collective-permute-start | bytes 307208 | tf_op jit(solution)/shard_map/ppermute | solution.py:31
  12.4 2.4 %collective-permute-start.6 = (bf16[16,3200]{1,0:T(8,128)(2,1)S(1)}, bf16[16,3200]{1,0:T(8,128)(2,1)S(1)}, u32[]{:S(2)}, u32[]{:S(2)}) collective-permute-start(bf16[16,3200]{1,0:T(8,128)(2,1)S(1)} %collective-permute-done.2.refs_3_), channel_id=1, source_target_pairs={{0,2},{1,3},{2,0},{3,1},{4,6},{5,7},{6,4},{7,5},{8,10},{9,11},{10,... | collective-permute-start | bytes 307208 | tf_op jit(solution)/shard_map/ppermute | solution.py:31
  16.9 17.2 %copy-start = (s32[1,128,6]{1,0,2:T(1,128)S(1)}, s32[1,128,6]{1,0,2:T(1,128)}, u32[]{:S(2)}) copy-start(s32[1,128,6]{1,0,2:T(1,128)} %param.9) | copy-start | bytes 9220
  17.0 17.2 %copy-start.1 = (f32[1,128,6]{1,0,2:T(1,128)S(1)}, f32[1,128,6]{1,0,2:T(1,128)}, u32[]{:S(2)}) copy-start(f32[1,128,6]{1,0,2:T(1,128)} %param.10) | copy-start | bytes 9220
  17.0 4.2 %collective-permute-start.7 = (bf16[32,3072]{1,0:T(8,128)(2,1)S(1)}, bf16[32,3072]{1,0:T(8,128)(2,1)S(1)}, u32[]{:S(2)}, u32[]{:S(2)}) collective-permute-start(bf16[32,3072]{1,0:T(8,128)(2,1)S(1)} %get-tuple-element.30), channel_id=1, source_target_pairs={{0,2},{1,3},{2,0},{3,1},{4,6},{5,7},{6,4},{7,5},{8,10},{9,11},{10,... | collective-permute-start | bytes 589832 | tf_op jit(solution)/shard_map/ppermute | solution.py:31
  17.5 3.6 %collective-permute-start.11 = (f32[8,128]{1,0:T(8,128)S(1)}, f32[8,128]{1,0:T(8,128)S(1)}, u32[]{:S(2)}, u32[]{:S(2)}) collective-permute-start(f32[8,128]{1,0:T(8,128)S(1)} %get-tuple-element.37), channel_id=1, source_target_pairs={{0,4},{1,5},{2,6},{3,7},{4,0},{5,1},{6,2},{7,3},{8,12},{9,13},{10,... | collective-permute-start | bytes 12296 | tf_op jit(solution)/shard_map/ppermute | solution.py:31
  21.1 4.3 %collective-permute-start.12 = (f32[8,128]{1,0:T(8,128)S(1)}, f32[8,128]{1,0:T(8,128)S(1)}, u32[]{:S(2)}, u32[]{:S(2)}) collective-permute-start(f32[8,128]{1,0:T(8,128)S(1)} %add_scores.1.near_ref), channel_id=1, source_target_pairs={{0,2},{1,3},{2,0},{3,1},{4,6},{5,7},{6,4},{7,5},{8,10},{9,11},{10,... | collective-permute-start | bytes 12296 | tf_op jit(solution)/shard_map/ppermute | solution.py:31
  21.2 6.9 %collective-permute-start.8 = (bf16[16,3200]{1,0:T(8,128)(2,1)S(1)}, bf16[16,3200]{1,0:T(8,128)(2,1)S(1)}, u32[]{:S(2)}, u32[]{:S(2)}) collective-permute-start(bf16[16,3200]{1,0:T(8,128)(2,1)S(1)} %get-tuple-element.31), channel_id=1, source_target_pairs={{0,24},{1,26},{2,25},{3,27},{4,28},{5,30},{6,29},{7,31},{8,0},{9,2... | collective-permute-start | bytes 307208 | tf_op jit(solution)/shard_map/ppermute | solution.py:45
  24.9 6.2 %collective-permute-start.9 = (bf16[16,3200]{1,0:T(8,128)(2,1)S(1)}, bf16[16,3200]{1,0:T(8,128)(2,1)S(1)}, u32[]{:S(2)}, u32[]{:S(2)}) collective-permute-start(bf16[16,3200]{1,0:T(8,128)(2,1)S(1)} %get-tuple-element.32), channel_id=1, source_target_pairs={{0,28},{1,30},{2,29},{3,31},{4,24},{5,26},{6,25},{7,27},{8,4},{9,6... | collective-permute-start | bytes 307208 | tf_op jit(solution)/shard_map/ppermute | solution.py:45
  25.6 8.6 %collective-permute-start.13 = (f32[8,2]{1,0:T(8,128)S(1)}, f32[8,2]{1,0:T(8,128)S(1)}, u32[]{:S(2)}, u32[]{:S(2)}) collective-permute-start(f32[8,2]{1,0:T(8,128)S(1)} %slice_add_fusion), channel_id=1, source_target_pairs={{0,1},{1,0},{2,3},{3,2},{4,5},{5,4},{6,7},{7,6},{8,9},{9,8},{10,11... | collective-permute-start | bytes 200 | tf_op jit(solution)/shard_map/ppermute | solution.py:31
  31.1 3.8 %collective-permute-start.10 = (bf16[8,3200]{1,0:T(8,128)(2,1)S(1)}, bf16[8,3200]{1,0:T(8,128)(2,1)S(1)}, u32[]{:S(2)}, u32[]{:S(2)}) collective-permute-start(bf16[8,3200]{1,0:T(8,128)(2,1)S(1)} %get-tuple-element.34), channel_id=1, source_target_pairs={{0,2},{1,3},{2,0},{3,1},{4,6},{5,7},{6,4},{7,5},{8,10},{9,11},{10,... | collective-permute-start | bytes 153608 | tf_op jit(solution)/shard_map/ppermute | solution.py:31

commit v5 on v4

--- a/solution.py
+++ b/solution.py
@@ -31,7 +31,7 @@
     return lax.ppermute(value, ("dp", "expert"), [(i, i ^ offset) for i in range(count)])
 
 
-def send_back(value, across):
+def send_back(value, across, flip):
     sections = lax.axis_size("pipe")
     chips = lax.axis_size("dp") // 2
     pairs = []
@@ -40,7 +40,7 @@
             for core in range(2):
                 for expert in range(2):
                     source = (s * chips + x) * 4 + 2 * core + expert
-                    target = (((s - 1) % sections) * chips + (x ^ across)) * 4 + 2 * expert + core
+                    target = (((s - 1) % sections) * chips + (x ^ across)) * 4 + 2 * (expert ^ flip) + core
                     pairs.append((source, target))
     return lax.ppermute(value, ("pipe", "dp", "expert"), pairs)
 
@@ -98,12 +98,16 @@
     group = shape_of((2 * capacity, width + LANES), jnp.bfloat16)
     return pl.pallas_call(
         functools.partial(pick_kernel, capacity),
-        out_shape=[group, group, shape_of((2 * capacity, tokens), jnp.bfloat16)],
+        out_shape=[
+            group,
+            group,
+            shape_of((2 * capacity, tokens), jnp.bfloat16),
+            shape_of(ids.shape, jnp.int32),
+            shape_of(weights.shape, jnp.float32),
+        ],
         in_specs=[pl.BlockSpec(memory_space=pltpu.SMEM)] + [HBM] * 4,
-        out_specs=[VMEM] * 3,
+        out_specs=[VMEM] * 5,
         scratch_shapes=[
-            pltpu.VMEM(ids.shape, jnp.int32),
-            pltpu.VMEM(weights.shape, jnp.float32),
             pltpu.VMEM((tokens, width), jnp.bfloat16),
             pltpu.VMEM((tokens, width), jnp.bfloat16),
             pltpu.SemaphoreType.DMA((4,)),
@@ -149,17 +153,19 @@
 def chain(steps):
     count = [0, 0]
     staged = []
-    for unit, weights, turned, left, total in steps:
-        staged.append((unit, count[unit] % 2))
+    for unit, *_ in steps:
+        staged.append(count[unit] % 2)
         count[unit] += 1
     ahead = 2
     for i in range(len(steps) + ahead):
         if i < len(steps):
-            unit, weights, turned, _, _ = steps[i]
-            pltpu.matmul_push_rhs(weights(), staging_register=staged[i][1], mxu_index=unit, transpose=turned)
+            unit, weights, turned = steps[i][:3]
+            pltpu.matmul_push_rhs(weights(), staging_register=staged[i], mxu_index=unit, transpose=turned)
         if i >= ahead:
-            _, _, _, left, total = steps[i - ahead]
-            pltpu.matmul_acc_lhs(total, left(), load_staged_rhs=staged[i - ahead][1])
+            left, total, after = steps[i - ahead][3:]
+            pltpu.matmul_acc_lhs(total, left(), load_staged_rhs=staged[i - ahead])
+            if after is not None:
+                after()
 
 
 def hidden_kernel(capacity, offsets, index_ref, *refs):
@@ -199,28 +205,26 @@
     def at_column(ref, start):
         return lambda: ref[:, start : start + tile]
 
-    def forward(first, second):
+    def forward(first, second, third, fourth):
+        taken = []
+
+        def take():
+            taken.extend((pltpu.matmul_pop(first), pltpu.matmul_pop(second)))
+
         steps = []
         for start in range(0, width, tile):
             left = functools.partial(acts, start)
-            steps.append((0, at(gate_ref, start), False, left, first))
-            steps.append((1, at(upper_ref, start), False, left, second))
+            steps.append((0, at(gate_ref, start), False, left, first, None))
+            steps.append((1, at(upper_ref, start), False, left, second, None))
+        for i, start in enumerate(range(0, width, tile)):
+            left = functools.partial(grads, start)
+            total = (third, fourth)[i % 2]
+            steps.append((i % 2, at_column(lower_ref, start), True, left, total, take if i == 1 else None))
         chain(steps)
-        return pltpu.matmul_pop(first), pltpu.matmul_pop(second)
-
-    def backward(first, second):
-        totals = (first, second)
-        chain(
-            [
-                (i % 2, at_column(lower_ref, start), True, functools.partial(grads, start), totals[i % 2])
-                for i, start in enumerate(range(0, width, tile))
-            ]
-        )
-        return pltpu.matmul_pop(first) + pltpu.matmul_pop(second)
+        return (*taken, pltpu.matmul_pop(third) + pltpu.matmul_pop(fourth))
 
     totals = [pltpu.ACC(unit)((rows, tile), jnp.float32) for unit in range(2)]
-    gate_pre, up_value = pl.run_scoped(forward, *totals)
-    grad_hidden = pl.run_scoped(backward, *totals)
+    gate_pre, up_value, grad_hidden = pl.run_scoped(forward, *totals, *totals)
     sigma_gate = jax.nn.sigmoid(gate_pre)
     swish = gate_pre * sigma_gate
     hidden = swish * up_value
@@ -234,22 +238,23 @@
 
     def back(*accs):
         starts = list(range(0, width, tile))
-        for group in range(0, len(starts), 4):
-            steps = []
+
+        def store(i):
+            block = pltpu.matmul_pop(accs[i % len(accs)])
+            keep_ref[:, starts[i] : starts[i] + tile] = block[:half]
+            send_ref[:, starts[i] : starts[i] + tile] = block[half:].astype(jnp.bfloat16)
+
+        steps = []
+        for pair in range(0, len(starts), 2):
             for source in range(2):
-                for i, start in enumerate(starts[group : group + 4]):
-                    unit = i % 2
-                    weights = at((gate_ref, upper_ref)[source], start)
+                for i in range(pair, min(pair + 2, len(starts))):
+                    weights = at((gate_ref, upper_ref)[source], starts[i])
                     left = (gate_part, upper_part)[source]
-                    total = accs[2 * ((group // 4 * 2 + i // 2) % 2) + unit]
-                    steps.append((unit, weights, True, lambda left=left: left, total))
-            ordered = [steps[i] for i in (0, 1, 4, 5, 2, 3, 6, 7) if i < len(steps)] if len(steps) == 8 else steps
-            chain(ordered)
-            for i, start in enumerate(starts[group : group + 4]):
-                total = accs[2 * ((group // 4 * 2 + i // 2) % 2) + i % 2]
-                block = pltpu.matmul_pop(total)
-                keep_ref[:, start : start + tile] = block[:half]
-                send_ref[:, start : start + tile] = block[half:].astype(jnp.bfloat16)
+                    after = functools.partial(store, i - 2) if source == 0 and i >= 2 else None
+                    steps.append((i % 2, weights, True, lambda left=left: left, accs[i % len(accs)], after))
+        chain(steps)
+        for i in range(max(0, len(starts) - 2), len(starts)):
+            store(i)
 
     pl.run_scoped(back, *totals, *totals)
     lane = lax.broadcasted_iota(jnp.int32, (capacity, LANES), 1)
@@ -285,66 +290,101 @@
 
 def join_kernel(keep_ref, recv_ref, *out_refs):
     width = recv_ref.shape[1]
-    for j, ref in enumerate(out_refs):
-        rows = ref.shape[0]
-        part = slice(j * rows, (j + 1) * rows)
+    start = 0
+    for ref in out_refs:
+        part = slice(start, start + ref.shape[0])
         ref[:, :width] = (keep_ref[part, :width] + recv_ref[part].astype(jnp.float32)).astype(jnp.bfloat16)
         ref[:, width:] = keep_ref[part, width:].astype(jnp.bfloat16)
-
-
-def join_cores(keep, recv, messages):
+        start += ref.shape[0]
+
+
+def join_cores(keep, recv, capacity):
     half, wide = keep.shape
+    sizes = [capacity, capacity] + [half - 2 * capacity] * (half > 2 * capacity)
     return pl.pallas_call(
         join_kernel,
-        out_shape=[shape_of((half // messages, wide), jnp.bfloat16)] * messages,
+        out_shape=[shape_of((size, wide), jnp.bfloat16) for size in sizes],
         in_specs=[VMEM] * 2,
-        out_specs=[VMEM] * messages,
+        out_specs=[VMEM] * len(sizes),
         cost_estimate=cost(2 * half * wide, 8 * half * wide),
         compiler_params=pltpu.CompilerParams(vmem_limit_bytes=8 * 2**20),
         name="join_cores",
     )(keep, recv)
 
 
-def weights_kernel(pieces, chunks, *refs):
+def weights_kernel(pieces, chunks, chosen, *refs):
     piece_refs = refs[:pieces]
-    delta_ref, hidden_ref, *outs = refs[pieces:]
-    hbm_refs, buffers, sems = outs[:3], outs[3:6], outs[6]
+    delta_ref, hidden_ref = refs[pieces : pieces + 2]
+    hbm_refs, buffers, sems = refs[-7:-4], refs[-4:-1], refs[-1]
     width, units = buffers[0].shape
     down = (((0,), (0,)), ((), ()))
-    copies = []
-    for i in range(chunks):
-        part = slice(i * width // chunks, (i + 1) * width // chunks)
-        rows = jnp.concatenate([ref[:, part] for ref in piece_refs], axis=0)
-        both = lax.dot_general(rows, delta_ref[...], down, preferred_element_type=jnp.float32)
-        buffers[0][part] = both[:, :units].astype(jnp.bfloat16)
-        buffers[1][part] = both[:, units:].astype(jnp.bfloat16)
-        buffers[2][:, part] = lax.dot_general(
-            hidden_ref[...], rows, down, preferred_element_type=jnp.float32
-        ).astype(jnp.bfloat16)
-        for j, spot in enumerate(((part,), (part,), (slice(None), part))):
-            copy = pltpu.make_async_copy(buffers[j].at[spot], hbm_refs[j].at[spot], sems.at[j, i])
-            copy.start()
-            copies.append(copy)
-    for copy in copies:
-        copy.wait()
-
-
-def weight_grads(pieces, delta, hidden, chunks):
+
+    @pl.when(chosen(lax.axis_index("pipe"), lax.axis_size("pipe")))
+    def _():
+        copies = []
+        for i in range(chunks):
+            part = slice(i * width // chunks, (i + 1) * width // chunks)
+            rows = jnp.concatenate([ref[:, part] for ref in piece_refs], axis=0)
+            both = lax.dot_general(rows, delta_ref[...], down, preferred_element_type=jnp.float32)
+            buffers[0][part] = both[:, :units].astype(jnp.bfloat16)
+            buffers[1][part] = both[:, units:].astype(jnp.bfloat16)
+            buffers[2][:, part] = lax.dot_general(
+                hidden_ref[...], rows, down, preferred_element_type=jnp.float32
+            ).astype(jnp.bfloat16)
+            for j, spot in enumerate(((part,), (part,), (slice(None), part))):
+                copy = pltpu.make_async_copy(buffers[j].at[spot], hbm_refs[j].at[spot], sems.at[j, i])
+                copy.start()
+                copies.append(copy)
+        for copy in copies:
+            copy.wait()
+
+
+def weight_grads(chosen, pieces, delta, hidden, earlier, chunks):
     width = pieces[0].shape[1] - LANES
     rows, units = hidden.shape
     count = len(pieces)
     shapes = [(width, units), (width, units), (units, width)]
     return pl.pallas_call(
-        functools.partial(weights_kernel, count, chunks),
+        functools.partial(weights_kernel, count, chunks, chosen),
         out_shape=[shape_of(shape, jnp.bfloat16) for shape in shapes],
-        in_specs=[VMEM] * (count + 2),
+        in_specs=[VMEM] * (count + 2) + [HBM] * len(earlier),
         out_specs=[HBM] * 3,
+        input_output_aliases={2 + count + j: j for j in range(len(earlier))},
         scratch_shapes=[pltpu.VMEM(shape, jnp.bfloat16) for shape in shapes]
         + [pltpu.SemaphoreType.DMA((3, chunks))],
         cost_estimate=cost(6 * rows * width * units, 6 * width * units),
         compiler_params=pltpu.CompilerParams(vmem_limit_bytes=24 * 2**20),
         name="weight_grads",
-    )(*pieces, delta, hidden)
+    )(*pieces, delta, hidden, *earlier)
+
+
+def is_first(section, sections):
+    return section == 0
+
+
+def is_last(section, sections):
+    return (section == sections - 1) & (section != 0)
+
+
+def is_between(section, sections):
+    return (section != sections - 1) & (section != 0)
+
+
+def cut_kernel(rows_ref, out_ref):
+    out_ref[...] = rows_ref[out_ref.shape[0] :]
+
+
+def lower_half(rows):
+    count, wide = rows.shape
+    return pl.pallas_call(
+        cut_kernel,
+        out_shape=shape_of((count // 2, wide), rows.dtype),
+        in_specs=[VMEM],
+        out_specs=VMEM,
+        cost_estimate=cost(0, 4 * rows.size),
+        compiler_params=pltpu.CompilerParams(vmem_limit_bytes=2 * 2**20),
+        name="lower_half",
+    )(rows)
 
 
 def add_kernel(left_ref, right_ref, out_ref):
@@ -363,63 +403,15 @@
     )(left, right)
 
 
-def score_kernel(capacity, index_ref, ids_ref, weight_ref, select_ref, near_ref, core_ref, other_ref, out_ref):
-    chosen, _, tokens = ids_ref.shape
-    scores = (near_ref[:, 0:1] + core_ref[:, 2:3], other_ref[:, 1:2])
-    sums = []
-    for j in range(2):
-        picked = select_ref[j * capacity : (j + 1) * capacity].astype(jnp.float32) * scores[j]
-        sums.append(jnp.sum(picked, axis=0, keepdims=True))
-    for k in range(chosen):
-        value = jnp.zeros((1, tokens), jnp.float32)
-        for j in range(2):
-            value = jnp.where(ids_ref[k] == ((index_ref[0] & 1) ^ j), sums[j], value)
-        out_ref[k] = value / weight_ref[k]
-
-
-def score_grads(index, ids, weights, select, near, core, other, capacity):
-    return pl.pallas_call(
-        functools.partial(score_kernel, capacity),
-        out_shape=shape_of(weights.shape, jnp.float32),
-        in_specs=[pl.BlockSpec(memory_space=pltpu.SMEM)] + [VMEM] * 6,
-        out_specs=VMEM,
-        cost_estimate=cost(1000, 1000),
-        compiler_params=pltpu.CompilerParams(vmem_limit_bytes=4 * 2**20),
-        name="score_grads",
-    )(index, ids, weights, select, near, core, other)
-
-
-def total_kernel(messages, *refs):
-    own_ref, other_ref = refs[messages:]
-    capacity, wide = own_ref.shape
-    width = wide - LANES
-    total = refs[0][:, :width].astype(jnp.float32)
-    for ref in refs[1:messages]:
-        total = total + ref[:, :width].astype(jnp.float32)
-    marks = refs[0][:, width:].astype(jnp.float32)
-    own_ref[:, :width] = total[:capacity].astype(jnp.bfloat16)
-    own_ref[:, width:] = marks[:capacity].astype(jnp.bfloat16)
-    other_ref[:, :width] = total[capacity:].astype(jnp.bfloat16)
-    other_ref[:, width:] = marks[capacity:].astype(jnp.bfloat16)
-
-
-def total_rows(arrays):
-    rows, wide = arrays[0].shape
-    return pl.pallas_call(
-        functools.partial(total_kernel, len(arrays)),
-        out_shape=[shape_of((rows // 2, wide), jnp.bfloat16)] * 2,
-        in_specs=[VMEM] * len(arrays),
-        out_specs=[VMEM] * 2,
-        cost_estimate=cost(rows * wide, 4 * rows * wide),
-        compiler_params=pltpu.CompilerParams(vmem_limit_bytes=4 * 2**20),
-        name="total_rows",
-    )(*arrays)
-
-
-def spread_kernel(chunks, own_ref, other_ref, out_hbm, out_ref, sems):
+def spread_kernel(chunks, terms, *refs):
+    own_refs, other_refs = refs[:terms], refs[terms : 2 * terms]
+    ids_ref, weight_ref, select_ref, near_ref, core_ref, side_ref, corner_ref = refs[2 * terms : 2 * terms + 7]
+    out_hbm, score_hbm, out_ref, score_ref, sems = refs[2 * terms + 7 :]
     tokens, width = out_ref.shape
-    capacity = own_ref.shape[0]
-    marks = jnp.concatenate([ref[:, width:].astype(jnp.float32) for ref in (own_ref, other_ref)], axis=0)
+    capacity = other_refs[0].shape[0]
+    marks = jnp.concatenate(
+        [group[0][:capacity, width:].astype(jnp.float32) for group in (own_refs, other_refs)], axis=0
+    )
     lane = lax.broadcasted_iota(jnp.int32, marks.shape, 1)
     number = jnp.sum(jnp.where(lane == 0, marks * 256.0, jnp.where(lane == 1, marks, 0.0)), axis=1, keepdims=True)
     token = lax.broadcasted_iota(jnp.int32, (2 * capacity, tokens), 1).astype(jnp.float32)
@@ -427,29 +419,54 @@
     copies = []
     for i in range(chunks):
         part = slice(i * width // chunks, (i + 1) * width // chunks)
-        rows = jnp.concatenate([ref[:, part] for ref in (own_ref, other_ref)], axis=0)
+        rows = jnp.concatenate(
+            [
+                sum(ref[:capacity, part].astype(jnp.float32) for ref in group)
+                for group in (own_refs, other_refs)
+            ],
+            axis=0,
+        )
         out_ref[:, part] = lax.dot_general(
-            select, rows, (((0,), (0,)), ((), ())), preferred_element_type=jnp.float32
+            select, rows.astype(jnp.bfloat16), (((0,), (0,)), ((), ())), preferred_element_type=jnp.float32
         ).astype(jnp.bfloat16)
         copies.append(pltpu.make_async_copy(out_ref.at[:, part], out_hbm.at[:, part], sems.at[i]))
         copies[-1].start()
+    own = lax.axis_index("expert")
+    scores = (near_ref[:, 0:1] + core_ref[:, 2:3], side_ref[:, 1:2] + corner_ref[:, 3:4])
+    sums = []
+    for j in range(2):
+        picked = select_ref[j * capacity : (j + 1) * capacity].astype(jnp.float32) * scores[j]
+        sums.append(jnp.sum(picked, axis=0, keepdims=True))
+    for k in range(ids_ref.shape[0]):
+        value = jnp.zeros((1, tokens), jnp.float32)
+        for j in range(2):
+            value = jnp.where(ids_ref[k] == (own ^ j), sums[j], value)
+        score_ref[k] = value / weight_ref[k]
+    copies.append(pltpu.make_async_copy(score_ref, score_hbm, sems.at[chunks]))
+    copies[-1].start()
     for copy in copies:
         copy.wait()
 
 
-def spread_rows(own_rows, other_rows, tokens, chunks):
-    capacity, wide = own_rows.shape
+def spread_rows(own_terms, other_terms, ids, weights, select, scores, chunks):
+    wide = own_terms[0].shape[1]
     width = wide - LANES
-    return pl.pallas_call(
-        functools.partial(spread_kernel, chunks),
-        out_shape=shape_of((tokens, width), jnp.bfloat16),
-        in_specs=[VMEM, VMEM],
-        out_specs=HBM,
-        scratch_shapes=[pltpu.VMEM((tokens, width), jnp.bfloat16), pltpu.SemaphoreType.DMA((chunks,))],
-        cost_estimate=cost(4 * capacity * tokens * width, 2 * tokens * width),
+    tokens = select.shape[1]
+    terms = len(own_terms)
+    return pl.pallas_call(
+        functools.partial(spread_kernel, chunks, terms),
+        out_shape=[shape_of((tokens, width), jnp.bfloat16), shape_of(weights.shape, jnp.float32)],
+        in_specs=[VMEM] * (2 * terms + 7),
+        out_specs=[HBM, HBM],
+        scratch_shapes=[
+            pltpu.VMEM((tokens, width), jnp.bfloat16),
+            pltpu.VMEM(weights.shape, jnp.float32),
+            pltpu.SemaphoreType.DMA((chunks + 1,)),
+        ],
+        cost_estimate=cost(64 * tokens * width, 2 * tokens * width),
         compiler_params=pltpu.CompilerParams(vmem_limit_bytes=16 * 2**20),
         name="spread_rows",
-    )(own_rows, other_rows)
+    )(*own_terms, *other_terms, ids, weights, select, *scores)
 
 
 def pairwise_shards(block_input, output_grad, expert_ids, gate_weights, gate_proj, up_proj, down_proj):
@@ -462,7 +479,9 @@
     ids = jnp.transpose(expert_ids, (2, 0, 1))
     weights = jnp.transpose(gate_weights, (2, 0, 1))
     stay = functools.partial(pltpu.with_memory_space_constraint, memory_space=pltpu.HBM)
-    *sends, select = pick_rows(index, stay(ids), stay(weights), stay(block_input[0]), stay(output_grad[0]), capacity)
+    *sends, select, ids, weights = pick_rows(
+        index, stay(ids), stay(weights), stay(block_input[0]), stay(output_grad[0]), capacity
+    )
     gate, upper, lower = load_weights(*[stay(array[0, 0]) for array in (gate_proj, up_proj, down_proj)])
     mine = {0: sends[0]}
     for offset in sorted(plane[1:], reverse=True):
@@ -476,15 +495,20 @@
     for scores in far:
         moved = swap(scores, 4)
         near = add_scores(near, moved)
-    chips = count // 4
-    joined = join_cores(keep, recv, chips)
-    messages = [send_back(joined[x], x) for x in range(chips)]
-    gate_grad, upper_grad, lower_grad = weight_grads(pieces, delta, hidden, 6)
-    core = swap(near, 2)
-    other = swap(near[:, :2] + core[:, 2:4], 1)
-    weight_grad = score_grads(index, ids, weights, select, near, core, other, capacity)
-    own_rows, other_rows = total_rows(messages)
-    received = spread_rows(own_rows, swap(other_rows, 2), tokens, 3)
+    straight, crossed, *beyond = join_cores(keep, recv, capacity)
+    own_terms, other_terms, grads = [], [], ()
+    grads = weight_grads(is_first, pieces, delta, hidden, grads, 6)
+    grads = weight_grads(is_last, pieces, delta, hidden, grads, 6)
+    for rows in beyond:
+        rows = send_back(rows, 1, 0)
+        own_terms.append(rows)
+        rows = lower_half(rows)
+        other_terms.append(swap(rows, 2))
+    own_terms.append(send_back(straight, 0, 0))
+    other_terms.append(send_back(crossed, 0, 1))
+    gate_grad, upper_grad, lower_grad = weight_grads(is_between, pieces, delta, hidden, grads, 6)
+    scores = [near] + [swap(near, offset) for offset in (2, 1, 3)]
+    received, weight_grad = spread_rows(own_terms, other_terms, ids, weights, select, scores, 3)
     return (
         received[None],
         jnp.transpose(weight_grad, (1, 2, 0)),

time: 36.3 us -> 35.2 us (0.970)
  waiting for transfers between devices: 12.3 us -> 7.29 us
  starting transfers between devices: 12.2 us -> 16.2 us
  Pallas kernels: 10.8 us -> 10.4 us
    ppermute x2 -> x3, starting transfers between devices: 4.27 us -> 6.86 us  [send_back(): return lax.ppermute(value, ('pipe', 'dp', 'expert'), pairs)]
    ppermute x12 -> x13, waiting for transfers between devices: 8.42 us -> 5.89 us  [swap(): lax.ppermute(value, ('dp', 'expert'), [(i, i ^ offset) for i in range(cou...]
    ppermute x2 -> x3, waiting for transfers between devices: 3.87 us -> 1.4 us  [send_back(): return lax.ppermute(value, ('pipe', 'dp', 'expert'), pairs)]
    ppermute x12 -> x13, starting transfers between devices: 7.9 us -> 9.38 us  [swap(): lax.ppermute(value, ('dp', 'expert'), [(i, i ^ offset) for i in range(cou...]
    pallas_call x5 -> x6, Pallas kernels: 4.68 us -> 4.27 us  [the longest x3 2.96 us: weight_grads(): pl.pallas_call(functools.partial(weights_kernel, count, chunks, chosen),...]
  transfers between devices with their start and end apart: 14 -> 16, of which waited for: 6 -> 6; matrix products, arithmetic and copies ran while one was open for 0% -> 0% of each run, Pallas kernels for 16% -> 16%
where the time goes in v5:
time: 35.2 us; the launch traced here: 34.7 us
  starting transfers between devices  16.2 us (46%)
  Pallas kernels  10.4 us (30%)
  waiting for transfers between devices  7.29 us (21%)
  between operations  0.76 us (2%)
    ppermute x13, starting transfers between devices, swap(): lax.ppermute(value, ('dp', 'expert'), [(i, i ^ offset) for i in range(cou...  9.38 us
    ppermute x3, starting transfers between devices, send_back(): return lax.ppermute(value, ('pipe', 'dp', 'expert'), pairs)  6.86 us
    ppermute x13, waiting for transfers between devices, swap(): lax.ppermute(value, ('dp', 'expert'), [(i, i ^ offset) for i in range(cou...  5.89 us
    pallas_call x3, Pallas kernels, weight_grads(): pl.pallas_call(functools.partial(weights_kernel, count, chunks, chosen),...  2.96 us
    pallas_call x1, Pallas kernels, load_weights(): pl.pallas_call(load_kernel, out_shape=[shape_of(array.shape, array.dtype)...  2.38 us
    pallas_call x1, Pallas kernels, hidden_pass(): pl.pallas_call(functools.partial(hidden_kernel, capacity, offsets), out_s...  2.07 us
    pallas_call x1, Pallas kernels, pick_rows(): pl.pallas_call(functools.partial(pick_kernel, capacity), out_shape=[group...  1.66 us
    ppermute x3, waiting for transfers between devices, send_back(): return lax.ppermute(value, ('pipe', 'dp', 'expert'), pairs)  1.4 us
  transfers between devices with their start and end apart: 16, of which 6 were waited for; matrix products, arithmetic and copies ran while one was open for 0% of the time, Pallas kernels for 16%

profile of v5, /device:TPU:0, one launch (start us, length us, event | category | flops | bytes accessed | tf_op | source)
XLA Modules:
  0.0 34.7 jit_solution(1828371650664744546)
XLA Ops:
  0.6 1.7 %pick_rows.1 = (bf16[16,3200]{1,0:T(8,128)(2,1)S(1)}, bf16[16,3200]{1,0:T(8,128)(2,1)S(1)}, bf16[16,128]{1,0:T(8,128)(2,1)S(1)}, s32[6,1,128]{2,1,0:T(1,128)S(1)}, f32[6,1,128]{2,1,0:T(1,128)S(1)}) custom-call(s32[1]{0:T(128)} %bitcast.index_ref, s32[6,1,128]{2,1,0:T(1,128)} %bitcast.21, f32[6,1,128]{2,1,0:T(1,128)} %bitcast.22, bf16[128,3072]{1,0:T(8,128)(2,1)} %bitcast.19, ...), custom_call_target="tpu_custom_call" | custom-call | flops 25165824 | bytes 1572864 | tf_op jit(solution)/shard_map/pick_rows/pallas_call | solution.py:99
  2.3 3.0 %collective-permute-start.1 = (bf16[16,3200]{1,0:T(8,128)(2,1)S(1)}, bf16[16,3200]{1,0:T(8,128)(2,1)S(1)}, u32[]{:S(2)}, u32[]{:S(2)}) collective-permute-start(bf16[16,3200]{1,0:T(8,128)(2,1)S(1)} %get-tuple-element.33.refs_0_), channel_id=1, source_target_pairs={{0,4},{1,5},{2,6},{3,7},{4,0},{5,1},{6,2},{7,3},{8,12},{9,13},{10,... | collective-permute-start | bytes 307208 | tf_op jit(solution)/shard_map/ppermute | solution.py:31
  5.3 1.5 %collective-permute-start = (bf16[16,3200]{1,0:T(8,128)(2,1)S(1)}, bf16[16,3200]{1,0:T(8,128)(2,1)S(1)}, u32[]{:S(2)}, u32[]{:S(2)}) collective-permute-start(bf16[16,3200]{1,0:T(8,128)(2,1)S(1)} %get-tuple-element.34), channel_id=1, source_target_pairs={{0,1},{1,0},{2,3},{3,2},{4,5},{5,4},{6,7},{7,6},{8,9},{9,8},{10,11... | collective-permute-start | bytes 307208 | tf_op jit(solution)/shard_map/ppermute | solution.py:31
  6.9 1.6 %collective-permute-done.1.refs_2_ = bf16[16,3200]{1,0:T(8,128)(2,1)S(1)} collective-permute-done((bf16[16,3200]{1,0:T(8,128)(2,1)S(1)}, bf16[16,3200]{1,0:T(8,128)(2,1)S(1)}, u32[]{:S(2)}, u32[]{:S(2)}) %collective-permute-start.1) | collective-permute-done | bytes 102432 | tf_op jit(solution)/shard_map/ppermute | solution.py:31
  8.5 2.6 %collective-permute-done.refs_1_ = bf16[16,3200]{1,0:T(8,128)(2,1)S(1)} collective-permute-done((bf16[16,3200]{1,0:T(8,128)(2,1)S(1)}, bf16[16,3200]{1,0:T(8,128)(2,1)S(1)}, u32[]{:S(2)}, u32[]{:S(2)}) %collective-permute-start) | collective-permute-done | bytes 102432 | tf_op jit(solution)/shard_map/ppermute | solution.py:31
  11.1 1.3 %collective-permute-done.2.refs_3_ = bf16[16,3200]{1,0:T(8,128)(2,1)S(1)} collective-permute-done((bf16[16,3200]{1,0:T(8,128)(2,1)S(1)}, bf16[16,3200]{1,0:T(8,128)(2,1)S(1)}, u32[]{:S(2)}, u32[]{:S(2)}) %collective-permute-start.2) | collective-permute-done | bytes 102432 | tf_op jit(solution)/shard_map/ppermute | solution.py:31
  12.4 2.4 %load_weights.1 = (bf16[3072,256]{1,0:T(8,128)(2,1)S(1)}, bf16[3072,256]{1,0:T(8,128)(2,1)S(1)}, bf16[256,3072]{1,0:T(8,128)(2,1)S(1)}) custom-call(bf16[3072,256]{1,0:T(8,128)(2,1)} %bitcast.16, bf16[3072,256]{1,0:T(8,128)(2,1)} %bitcast.17, bf16[256,3072]{1,0:T(8,128)(2,1)} %bitcast.18), custom_call_target="tpu_custom_call" | custom-call | bytes 4718592 | tf_op jit(solution)/shard_map/load_weights/pallas_call | solution.py:132
  14.9 2.1 %hidden_pass.1 = (f32[32,3200]{1,0:T(8,128)S(1)}, bf16[32,3072]{1,0:T(8,128)(2,1)S(1)}, bf16[128,512]{1,0:T(8,128)(2,1)S(1)}, bf16[128,256]{1,0:T(8,128)(2,1)S(1...) custom-call(s32[1]{0:T(128)} %bitcast.index_ref, bf16[16,3200]{1,0:T(8,128)(2,1)S(1)} %get-tuple-element.33.refs_0_, ...), custom_call_target="tpu_custom_call" | custom-call | flops 1006632960 | bytes 4718592 | tf_op jit(solution)/shard_map/hidden_pass/pallas_call | solution.py:274
  16.9 0.6 %collective-permute-start.7 = (bf16[32,3072]{1,0:T(8,128)(2,1)S(1)}, bf16[32,3072]{1,0:T(8,128)(2,1)S(1)}, u32[]{:S(2)}, u32[]{:S(2)}) collective-permute-start(bf16[32,3072]{1,0:T(8,128)(2,1)S(1)} %get-tuple-element.39), channel_id=1, source_target_pairs={{0,2},{1,3},{2,0},{3,1},{4,6},{5,7},{6,4},{7,5},{8,10},{9,11},{10,... | collective-permute-start | bytes 589832 | tf_op jit(solution)/shard_map/ppermute | solution.py:31
  17.5 0.7 %collective-permute-start.12 = (f32[8,128]{1,0:T(8,128)S(1)}, f32[8,128]{1,0:T(8,128)S(1)}, u32[]{:S(2)}, u32[]{:S(2)}) collective-permute-start(f32[8,128]{1,0:T(8,128)S(1)} %get-tuple-element.47), channel_id=1, source_target_pairs={{0,4},{1,5},{2,6},{3,7},{4,0},{5,1},{6,2},{7,3},{8,12},{9,13},{10,... | collective-permute-start | bytes 12296 | tf_op jit(solution)/shard_map/ppermute | solution.py:31
  18.2 0.3 collective-permute-done.7.recv_ref
  18.6 4.1 %collective-permute-start.8 = (bf16[16,3200]{1,0:T(8,128)(2,1)S(1)}, bf16[16,3200]{1,0:T(8,128)(2,1)S(1)}, u32[]{:S(2)}, u32[]{:S(2)}) collective-permute-start(bf16[16,3200]{1,0:T(8,128)(2,1)S(1)} %get-tuple-element.40), channel_id=1, source_target_pairs={{0,28},{1,30},{2,29},{3,31},{4,24},{5,26},{6,25},{7,27},{8,4},{9,6... | collective-permute-start | bytes 307208 | tf_op jit(solution)/shard_map/ppermute | solution.py:45
  22.7 2.6 %weight_grads.3 = (bf16[3072,256]{1,0:T(8,128)(2,1)}, bf16[3072,256]{1,0:T(8,128)(2,1)}, bf16[256,3072]{1,0:T(8,128)(2,1)}) custom-call(bf16[16,3200]{1,0:T(8,128)(2,1)S(1)} %get-tuple-element.33.refs_0_, bf16[16,3200]{1,0:T(8,128)(2,1)S(1)} %collective-permute-done.refs_1_, bf16[16,3200]{1,0:T(8,128)(2,1)S(1)} %collective-permute-done.1.refs_2_, ...), custom_call_target="tpu_custom_call" | custom-call | flops 603979776 | bytes 4718592 | tf_op jit(solution)/shard_map/weight_grads/pallas_call | solution.py:347
  25.3 0.7 %collective-permute-start.13 = (f32[8,128]{1,0:T(8,128)S(1)}, f32[8,128]{1,0:T(8,128)S(1)}, u32[]{:S(2)}, u32[]{:S(2)}) collective-permute-start(f32[8,128]{1,0:T(8,128)S(1)} %add_scores.1.refs_7_), channel_id=1, source_target_pairs={{0,2},{1,3},{2,0},{3,1},{4,6},{5,7},{6,4},{7,5},{8,10},{9,11},{10,... | collective-permute-start | bytes 12296 | tf_op jit(solution)/shard_map/ppermute | solution.py:31
  26.0 0.2 weight_grads.4
  26.2 0.7 %collective-permute-start.14 = (f32[8,128]{1,0:T(8,128)S(1)}, f32[8,128]{1,0:T(8,128)S(1)}, u32[]{:S(2)}, u32[]{:S(2)}) collective-permute-start(f32[8,128]{1,0:T(8,128)S(1)} %add_scores.1.refs_7_), channel_id=1, source_target_pairs={{0,1},{1,0},{2,3},{3,2},{4,5},{5,4},{6,7},{7,6},{8,9},{9,8},{10,11... | collective-permute-start | bytes 12296 | tf_op jit(solution)/shard_map/ppermute | solution.py:31
  26.9 0.8 %collective-permute-start.15 = (f32[8,128]{1,0:T(8,128)S(1)}, f32[8,128]{1,0:T(8,128)S(1)}, u32[]{:S(2)}, u32[]{:S(2)}) collective-permute-start(f32[8,128]{1,0:T(8,128)S(1)} %add_scores.1.refs_7_), channel_id=1, source_target_pairs={{0,3},{1,2},{2,1},{3,0},{4,7},{5,6},{6,5},{7,4},{8,11},{9,10},{10,... | collective-permute-start | bytes 12296 | tf_op jit(solution)/shard_map/ppermute | solution.py:31
  27.7 1.5 %collective-permute-start.11 = (bf16[8,3200]{1,0:T(8,128)(2,1)S(1)}, bf16[8,3200]{1,0:T(8,128)(2,1)S(1)}, u32[]{:S(2)}, u32[]{:S(2)}) collective-permute-start(bf16[8,3200]{1,0:T(8,128)(2,1)S(1)} %get-tuple-element.42), channel_id=1, source_target_pairs={{0,26},{1,24},{2,27},{3,25},{4,30},{5,28},{6,31},{7,29},{8,2},{9,0... | collective-permute-start | bytes 153608 | tf_op jit(solution)/shard_map/ppermute | solution.py:45
  29.2 1.3 %collective-permute-start.9 = (bf16[8,3200]{1,0:T(8,128)(2,1)S(1)}, bf16[8,3200]{1,0:T(8,128)(2,1)S(1)}, u32[]{:S(2)}, u32[]{:S(2)}) collective-permute-start(bf16[8,3200]{1,0:T(8,128)(2,1)S(1)} %get-tuple-element.41), channel_id=1, source_target_pairs={{0,24},{1,26},{2,25},{3,27},{4,28},{5,30},{6,29},{7,31},{8,0},{9,2... | collective-permute-start | bytes 153608 | tf_op jit(solution)/shard_map/ppermute | solution.py:45
  30.5 1.3 %collective-permute-start.10 = (bf16[8,3200]{1,0:T(8,128)(2,1)S(1)}, bf16[8,3200]{1,0:T(8,128)(2,1)S(1)}, u32[]{:S(2)}, u32[]{:S(2)}) collective-permute-start(bf16[8,3200]{1,0:T(8,128)(2,1)S(1)} %lower_half.1), channel_id=1, source_target_pairs={{0,2},{1,3},{2,0},{3,1},{4,6},{5,7},{6,4},{7,5},{8,10},{9,11},{10,... | collective-permute-start | bytes 153608 | tf_op jit(solution)/shard_map/ppermute | solution.py:31
  31.8 0.2 weight_grads.5
  32.0 0.8 %collective-permute-done.11.refs_3_ = bf16[8,3200]{1,0:T(8,128)(2,1)S(1)} collective-permute-done((bf16[8,3200]{1,0:T(8,128)(2,1)S(1)}, bf16[8,3200]{1,0:T(8,128)(2,1)S(1)}, u32[]{:S(2)}, u32[]{:S(2)}) %collective-permute-start.11) | collective-permute-done | bytes 51232 | tf_op jit(solution)/shard_map/ppermute | solution.py:45
  32.8 0.6 %collective-permute-done.9.refs_1_ = bf16[8,3200]{1,0:T(8,128)(2,1)S(1)} collective-permute-done((bf16[8,3200]{1,0:T(8,128)(2,1)S(1)}, bf16[8,3200]{1,0:T(8,128)(2,1)S(1)}, u32[]{:S(2)}, u32[]{:S(2)}) %collective-permute-start.9) | collective-permute-done | bytes 51232 | tf_op jit(solution)/shard_map/ppermute | solution.py:45
  33.4 1.3 %spread_rows.1 = (bf16[128,3072]{1,0:T(8,128)(2,1)}, f32[6,1,128]{2,1,0:T(1,128)}) custom-call(bf16[16,3200]{1,0:T(8,128)(2,1)S(1)} %collective-permute-done.8.rows_ref.refs_0_, bf16[8,3200]{1,0:T(8,128)(2,1)S(1)} %collective-permute-done.9.refs_1_, bf16[8,3200]{1,0:T(8,128)(2,1)S(1)} %collective-permute-done.10.refs_2_, ...), custom_call_target="tpu_custom_call" | custom-call | flops 25165824 | bytes 786432 | tf_op jit(solution)/shard_map/spread_rows/pallas_call | solution.py:456
  (18 shorter events, 0.1 us)
Async XLA Ops:
  2.3 6.2 %collective-permute-start.1 = (bf16[16,3200]{1,0:T(8,128)(2,1)S(1)}, bf16[16,3200]{1,0:T(8,128)(2,1)S(1)}, u32[]{:S(2)}, u32[]{:S(2)}) collective-permute-start(bf16[16,3200]{1,0:T(8,128)(2,1)S(1)} %get-tuple-element.33.refs_0_), channel_id=1, source_target_pairs={{0,4},{1,5},{2,6},{3,7},{4,0},{5,1},{6,2},{7,3},{8,12},{9,13},{10,... | collective-permute-start | bytes 307208 | tf_op jit(solution)/shard_map/ppermute | solution.py:31
  5.3 5.8 %collective-permute-start = (bf16[16,3200]{1,0:T(8,128)(2,1)S(1)}, bf16[16,3200]{1,0:T(8,128)(2,1)S(1)}, u32[]{:S(2)}, u32[]{:S(2)}) collective-permute-start(bf16[16,3200]{1,0:T(8,128)(2,1)S(1)} %get-tuple-element.34), channel_id=1, source_target_pairs={{0,1},{1,0},{2,3},{3,2},{4,5},{5,4},{6,7},{7,6},{8,9},{9,8},{10,11... | collective-permute-start | bytes 307208 | tf_op jit(solution)/shard_map/ppermute | solution.py:31
  6.9 5.6 %collective-permute-start.2 = (bf16[16,3200]{1,0:T(8,128)(2,1)S(1)}, bf16[16,3200]{1,0:T(8,128)(2,1)S(1)}, u32[]{:S(2)}, u32[]{:S(2)}) collective-permute-start(bf16[16,3200]{1,0:T(8,128)(2,1)S(1)} %get-tuple-element.34), channel_id=1, source_target_pairs={{0,5},{1,4},{2,7},{3,6},{4,1},{5,0},{6,3},{7,2},{8,13},{9,12},{10,... | collective-permute-start | bytes 307208 | tf_op jit(solution)/shard_map/ppermute | solution.py:31
  6.9 7.9 %collective-permute-start.3 = (bf16[16,3200]{1,0:T(8,128)(2,1)S(1)}, bf16[16,3200]{1,0:T(8,128)(2,1)S(1)}, u32[]{:S(2)}, u32[]{:S(2)}) collective-permute-start(bf16[16,3200]{1,0:T(8,128)(2,1)S(1)} %get-tuple-element.33.refs_0_), channel_id=1, source_target_pairs={{0,2},{1,3},{2,0},{3,1},{4,6},{5,7},{6,4},{7,5},{8,10},{9,11},{10,... | collective-permute-start | bytes 307208 | tf_op jit(solution)/shard_map/ppermute | solution.py:31
  8.5 6.3 %collective-permute-start.5 = (bf16[16,3200]{1,0:T(8,128)(2,1)S(1)}, bf16[16,3200]{1,0:T(8,128)(2,1)S(1)}, u32[]{:S(2)}, u32[]{:S(2)}) collective-permute-start(bf16[16,3200]{1,0:T(8,128)(2,1)S(1)} %collective-permute-done.1.refs_2_), channel_id=1, source_target_pairs={{0,2},{1,3},{2,0},{3,1},{4,6},{5,7},{6,4},{7,5},{8,10},{9,11},{10,... | collective-permute-start | bytes 307208 | tf_op jit(solution)/shard_map/ppermute | solution.py:31
  11.1 3.7 %collective-permute-start.4 = (bf16[16,3200]{1,0:T(8,128)(2,1)S(1)}, bf16[16,3200]{1,0:T(8,128)(2,1)S(1)}, u32[]{:S(2)}, u32[]{:S(2)}) collective-permute-start(bf16[16,3200]{1,0:T(8,128)(2,1)S(1)} %collective-permute-done.refs_1_), channel_id=1, source_target_pairs={{0,2},{1,3},{2,0},{3,1},{4,6},{5,7},{6,4},{7,5},{8,10},{9,11},{10,... | collective-permute-start | bytes 307208 | tf_op jit(solution)/shard_map/ppermute | solution.py:31
  12.4 2.4 %collective-permute-start.6 = (bf16[16,3200]{1,0:T(8,128)(2,1)S(1)}, bf16[16,3200]{1,0:T(8,128)(2,1)S(1)}, u32[]{:S(2)}, u32[]{:S(2)}) collective-permute-start(bf16[16,3200]{1,0:T(8,128)(2,1)S(1)} %collective-permute-done.2.refs_3_), channel_id=1, source_target_pairs={{0,2},{1,3},{2,0},{3,1},{4,6},{5,7},{6,4},{7,5},{8,10},{9,11},{10,... | collective-permute-start | bytes 307208 | tf_op jit(solution)/shard_map/ppermute | solution.py:31
  16.9 1.6 %collective-permute-start.7 = (bf16[32,3072]{1,0:T(8,128)(2,1)S(1)}, bf16[32,3072]{1,0:T(8,128)(2,1)S(1)}, u32[]{:S(2)}, u32[]{:S(2)}) collective-permute-start(bf16[32,3072]{1,0:T(8,128)(2,1)S(1)} %get-tuple-element.39), channel_id=1, source_target_pairs={{0,2},{1,3},{2,0},{3,1},{4,6},{5,7},{6,4},{7,5},{8,10},{9,11},{10,... | collective-permute-start | bytes 589832 | tf_op jit(solution)/shard_map/ppermute | solution.py:31
  17.5 7.8 %collective-permute-start.12 = (f32[8,128]{1,0:T(8,128)S(1)}, f32[8,128]{1,0:T(8,128)S(1)}, u32[]{:S(2)}, u32[]{:S(2)}) collective-permute-start(f32[8,128]{1,0:T(8,128)S(1)} %get-tuple-element.47), channel_id=1, source_target_pairs={{0,4},{1,5},{2,6},{3,7},{4,0},{5,1},{6,2},{7,3},{8,12},{9,13},{10,... | collective-permute-start | bytes 12296 | tf_op jit(solution)/shard_map/ppermute | solution.py:31
  18.6 10.6 %collective-permute-start.8 = (bf16[16,3200]{1,0:T(8,128)(2,1)S(1)}, bf16[16,3200]{1,0:T(8,128)(2,1)S(1)}, u32[]{:S(2)}, u32[]{:S(2)}) collective-permute-start(bf16[16,3200]{1,0:T(8,128)(2,1)S(1)} %get-tuple-element.40), channel_id=1, source_target_pairs={{0,28},{1,30},{2,29},{3,31},{4,24},{5,26},{6,25},{7,27},{8,4},{9,6... | collective-permute-start | bytes 307208 | tf_op jit(solution)/shard_map/ppermute | solution.py:45
  25.3 5.2 %collective-permute-start.13 = (f32[8,128]{1,0:T(8,128)S(1)}, f32[8,128]{1,0:T(8,128)S(1)}, u32[]{:S(2)}, u32[]{:S(2)}) collective-permute-start(f32[8,128]{1,0:T(8,128)S(1)} %add_scores.1.refs_7_), channel_id=1, source_target_pairs={{0,2},{1,3},{2,0},{3,1},{4,6},{5,7},{6,4},{7,5},{8,10},{9,11},{10,... | collective-permute-start | bytes 12296 | tf_op jit(solution)/shard_map/ppermute | solution.py:31
  26.2 5.8 %collective-permute-start.14 = (f32[8,128]{1,0:T(8,128)S(1)}, f32[8,128]{1,0:T(8,128)S(1)}, u32[]{:S(2)}, u32[]{:S(2)}) collective-permute-start(f32[8,128]{1,0:T(8,128)S(1)} %add_scores.1.refs_7_), channel_id=1, source_target_pairs={{0,1},{1,0},{2,3},{3,2},{4,5},{5,4},{6,7},{7,6},{8,9},{9,8},{10,11... | collective-permute-start | bytes 12296 | tf_op jit(solution)/shard_map/ppermute | solution.py:31
  26.9 5.1 %collective-permute-start.15 = (f32[8,128]{1,0:T(8,128)S(1)}, f32[8,128]{1,0:T(8,128)S(1)}, u32[]{:S(2)}, u32[]{:S(2)}) collective-permute-start(f32[8,128]{1,0:T(8,128)S(1)} %add_scores.1.refs_7_), channel_id=1, source_target_pairs={{0,3},{1,2},{2,1},{3,0},{4,7},{5,6},{6,5},{7,4},{8,11},{9,10},{10,... | collective-permute-start | bytes 12296 | tf_op jit(solution)/shard_map/ppermute | solution.py:31
  27.7 5.2 %collective-permute-start.11 = (bf16[8,3200]{1,0:T(8,128)(2,1)S(1)}, bf16[8,3200]{1,0:T(8,128)(2,1)S(1)}, u32[]{:S(2)}, u32[]{:S(2)}) collective-permute-start(bf16[8,3200]{1,0:T(8,128)(2,1)S(1)} %get-tuple-element.42), channel_id=1, source_target_pairs={{0,26},{1,24},{2,27},{3,25},{4,30},{5,28},{6,31},{7,29},{8,2},{9,0... | collective-permute-start | bytes 153608 | tf_op jit(solution)/shard_map/ppermute | solution.py:45
  29.2 4.2 %collective-permute-start.9 = (bf16[8,3200]{1,0:T(8,128)(2,1)S(1)}, bf16[8,3200]{1,0:T(8,128)(2,1)S(1)}, u32[]{:S(2)}, u32[]{:S(2)}) collective-permute-start(bf16[8,3200]{1,0:T(8,128)(2,1)S(1)} %get-tuple-element.41), channel_id=1, source_target_pairs={{0,24},{1,26},{2,25},{3,27},{4,28},{5,30},{6,29},{7,31},{8,0},{9,2... | collective-permute-start | bytes 153608 | tf_op jit(solution)/shard_map/ppermute | solution.py:45
  30.5 2.9 %collective-permute-start.10 = (bf16[8,3200]{1,0:T(8,128)(2,1)S(1)}, bf16[8,3200]{1,0:T(8,128)(2,1)S(1)}, u32[]{:S(2)}, u32[]{:S(2)}) collective-permute-start(bf16[8,3200]{1,0:T(8,128)(2,1)S(1)} %lower_half.1), channel_id=1, source_target_pairs={{0,2},{1,3},{2,0},{3,1},{4,6},{5,7},{6,4},{7,5},{8,10},{9,11},{10,... | collective-permute-start | bytes 153608 | tf_op jit(solution)/shard_map/ppermute | solution.py:31

commit v6 on v5

--- a/solution.py
+++ b/solution.py
@@ -9,6 +9,7 @@
 
 
 PAIRWISE_MAX = 8
+EARLY = 3
 LANES = 128
 VMEM = pl.BlockSpec(memory_space=pltpu.VMEM)
 HBM = pl.BlockSpec(memory_space=pltpu.HBM)
@@ -294,18 +295,20 @@
     for ref in out_refs:
         part = slice(start, start + ref.shape[0])
         ref[:, :width] = (keep_ref[part, :width] + recv_ref[part].astype(jnp.float32)).astype(jnp.bfloat16)
-        ref[:, width:] = keep_ref[part, width:].astype(jnp.bfloat16)
+        if ref.shape[1] > width:
+            ref[:, width:] = keep_ref[part, width:].astype(jnp.bfloat16)
         start += ref.shape[0]
 
 
 def join_cores(keep, recv, capacity):
     half, wide = keep.shape
-    sizes = [capacity, capacity] + [half - 2 * capacity] * (half > 2 * capacity)
+    far = half - 2 * capacity
+    shapes = [(capacity, recv.shape[1] if far else wide)] * 2 + [(far, wide)] * (far > 0)
     return pl.pallas_call(
         join_kernel,
-        out_shape=[shape_of((size, wide), jnp.bfloat16) for size in sizes],
+        out_shape=[shape_of(shape, jnp.bfloat16) for shape in shapes],
         in_specs=[VMEM] * 2,
-        out_specs=[VMEM] * len(sizes),
+        out_specs=[VMEM] * len(shapes),
         cost_estimate=cost(2 * half * wide, 8 * half * wide),
         compiler_params=pltpu.CompilerParams(vmem_limit_bytes=8 * 2**20),
         name="join_cores",
@@ -319,10 +322,9 @@
     width, units = buffers[0].shape
     down = (((0,), (0,)), ((), ()))
 
-    @pl.when(chosen(lax.axis_index("pipe"), lax.axis_size("pipe")))
-    def _():
+    def run(spots):
         copies = []
-        for i in range(chunks):
+        for i in spots:
             part = slice(i * width // chunks, (i + 1) * width // chunks)
             rows = jnp.concatenate([ref[:, part] for ref in piece_refs], axis=0)
             both = lax.dot_general(rows, delta_ref[...], down, preferred_element_type=jnp.float32)
@@ -338,6 +340,9 @@
         for copy in copies:
             copy.wait()
 
+    for predicate, spots in chosen:
+        pl.when(predicate(lax.axis_index("pipe"), lax.axis_size("pipe")))(functools.partial(run, spots))
+
 
 def weight_grads(chosen, pieces, delta, hidden, earlier, chunks):
     width = pieces[0].shape[1] - LANES
@@ -351,7 +356,7 @@
         out_specs=[HBM] * 3,
         input_output_aliases={2 + count + j: j for j in range(len(earlier))},
         scratch_shapes=[pltpu.VMEM(shape, jnp.bfloat16) for shape in shapes]
-        + [pltpu.SemaphoreType.DMA((3, chunks))],
+        + [pltpu.SemaphoreType.DMA((3, max(spots.stop for _, spots in chosen)))],
         cost_estimate=cost(6 * rows * width * units, 6 * width * units),
         compiler_params=pltpu.CompilerParams(vmem_limit_bytes=24 * 2**20),
         name="weight_grads",
@@ -497,8 +502,8 @@
         near = add_scores(near, moved)
     straight, crossed, *beyond = join_cores(keep, recv, capacity)
     own_terms, other_terms, grads = [], [], ()
-    grads = weight_grads(is_first, pieces, delta, hidden, grads, 6)
-    grads = weight_grads(is_last, pieces, delta, hidden, grads, 6)
+    grads = weight_grads([(is_first, range(EARLY))], pieces, delta, hidden, grads, 6)
+    grads = weight_grads([(is_last, range(3))], pieces, delta, hidden, grads, 3)
     for rows in beyond:
         rows = send_back(rows, 1, 0)
         own_terms.append(rows)
@@ -506,7 +511,9 @@
         other_terms.append(swap(rows, 2))
     own_terms.append(send_back(straight, 0, 0))
     other_terms.append(send_back(crossed, 0, 1))
-    gate_grad, upper_grad, lower_grad = weight_grads(is_between, pieces, delta, hidden, grads, 6)
+    gate_grad, upper_grad, lower_grad = weight_grads(
+        [(is_first, range(EARLY, 6)), (is_between, range(6))], pieces, delta, hidden, grads, 6
+    )
     scores = [near] + [swap(near, offset) for offset in (2, 1, 3)]
     received, weight_grad = spread_rows(own_terms, other_terms, ids, weights, select, scores, 3)
     return (

time: 35.2 us -> 35.3 us (level)
  waiting for transfers between devices: 7.29 us -> 5.9 us
  starting transfers between devices: 16.2 us -> 17.2 us
  Pallas kernels: 10.4 us -> 11.2 us
    ppermute x3, waiting for transfers between devices: 1.4 us -> 0.01 us  [send_back(): return lax.ppermute(value, ('pipe', 'dp', 'expert'), pairs)]
    ppermute x3, starting transfers between devices: 6.86 us -> 7.78 us  [send_back(): return lax.ppermute(value, ('pipe', 'dp', 'expert'), pairs)]
    pallas_call x3, Pallas kernels: 2.96 us -> 3.75 us  [weight_grads(): pl.pallas_call(functools.partial(weights_kernel, count, chunks, chosen),...]
  transfers between devices with their start and end apart: 16 -> 16, of which waited for: 6 -> 4; matrix products, arithmetic and copies ran while one was open for 0% -> 0% of each run, Pallas kernels for 16% -> 18%
where the time goes in v6:
time: 35.3 us; the launch traced here: 35 us
  starting transfers between devices  17.2 us (49%)
  Pallas kernels  11.2 us (32%)
  waiting for transfers between devices  5.9 us (17%)
  between operations  0.78 us (2%)
    ppermute x13, starting transfers between devices, swap(): lax.ppermute(value, ('dp', 'expert'), [(i, i ^ offset) for i in range(cou...  9.37 us
    ppermute x3, starting transfers between devices, send_back(): return lax.ppermute(value, ('pipe', 'dp', 'expert'), pairs)  7.78 us
    ppermute x13, waiting for transfers between devices, swap(): lax.ppermute(value, ('dp', 'expert'), [(i, i ^ offset) for i in range(cou...  5.89 us
    pallas_call x3, Pallas kernels, weight_grads(): pl.pallas_call(functools.partial(weights_kernel, count, chunks, chosen),...  3.75 us
    pallas_call x1, Pallas kernels, load_weights(): pl.pallas_call(load_kernel, out_shape=[shape_of(array.shape, array.dtype)...  2.38 us
    pallas_call x1, Pallas kernels, hidden_pass(): pl.pallas_call(functools.partial(hidden_kernel, capacity, offsets), out_s...  2.07 us
    pallas_call x1, Pallas kernels, pick_rows(): pl.pallas_call(functools.partial(pick_kernel, capacity), out_shape=[group...  1.66 us
    pallas_call x1, Pallas kernels, spread_rows(): pl.pallas_call(functools.partial(spread_kernel, chunks, terms), out_shape...  1.26 us
  transfers between devices with their start and end apart: 16, of which 4 were waited for; matrix products, arithmetic and copies ran while one was open for 0% of the time, Pallas kernels for 18%

profile of v6, /device:TPU:0, one launch (start us, length us, event | category | flops | bytes accessed | tf_op | source)
XLA Modules:
  0.0 35.0 jit_solution(9718856224646964266)
XLA Ops:
  0.6 1.7 %pick_rows.1 = (bf16[16,3200]{1,0:T(8,128)(2,1)S(1)}, bf16[16,3200]{1,0:T(8,128)(2,1)S(1)}, bf16[16,128]{1,0:T(8,128)(2,1)S(1)}, s32[6,1,128]{2,1,0:T(1,128)S(1)}, f32[6,1,128]{2,1,0:T(1,128)S(1)}) custom-call(s32[1]{0:T(128)} %bitcast.index_ref, s32[6,1,128]{2,1,0:T(1,128)} %bitcast.21, f32[6,1,128]{2,1,0:T(1,128)} %bitcast.22, bf16[128,3072]{1,0:T(8,128)(2,1)} %bitcast.19, ...), custom_call_target="tpu_custom_call" | custom-call | flops 25165824 | bytes 1572864 | tf_op jit(solution)/shard_map/pick_rows/pallas_call | solution.py:100
  2.3 3.0 %collective-permute-start.1 = (bf16[16,3200]{1,0:T(8,128)(2,1)S(1)}, bf16[16,3200]{1,0:T(8,128)(2,1)S(1)}, u32[]{:S(2)}, u32[]{:S(2)}) collective-permute-start(bf16[16,3200]{1,0:T(8,128)(2,1)S(1)} %get-tuple-element.33.refs_0_), channel_id=1, source_target_pairs={{0,4},{1,5},{2,6},{3,7},{4,0},{5,1},{6,2},{7,3},{8,12},{9,13},{10,... | collective-permute-start | bytes 307208 | tf_op jit(solution)/shard_map/ppermute | solution.py:32
  5.3 1.5 %collective-permute-start = (bf16[16,3200]{1,0:T(8,128)(2,1)S(1)}, bf16[16,3200]{1,0:T(8,128)(2,1)S(1)}, u32[]{:S(2)}, u32[]{:S(2)}) collective-permute-start(bf16[16,3200]{1,0:T(8,128)(2,1)S(1)} %get-tuple-element.34), channel_id=1, source_target_pairs={{0,1},{1,0},{2,3},{3,2},{4,5},{5,4},{6,7},{7,6},{8,9},{9,8},{10,11... | collective-permute-start | bytes 307208 | tf_op jit(solution)/shard_map/ppermute | solution.py:32
  6.9 0.0 collective-permute-start.2
  6.9 0.0 collective-permute-start.3
  6.9 1.6 %collective-permute-done.1.refs_2_ = bf16[16,3200]{1,0:T(8,128)(2,1)S(1)} collective-permute-done((bf16[16,3200]{1,0:T(8,128)(2,1)S(1)}, bf16[16,3200]{1,0:T(8,128)(2,1)S(1)}, u32[]{:S(2)}, u32[]{:S(2)}) %collective-permute-start.1) | collective-permute-done | bytes 102432 | tf_op jit(solution)/shard_map/ppermute | solution.py:32
  8.5 2.6 %collective-permute-done.refs_1_ = bf16[16,3200]{1,0:T(8,128)(2,1)S(1)} collective-permute-done((bf16[16,3200]{1,0:T(8,128)(2,1)S(1)}, bf16[16,3200]{1,0:T(8,128)(2,1)S(1)}, u32[]{:S(2)}, u32[]{:S(2)}) %collective-permute-start) | collective-permute-done | bytes 102432 | tf_op jit(solution)/shard_map/ppermute | solution.py:32
  11.1 1.3 %collective-permute-done.2.refs_3_ = bf16[16,3200]{1,0:T(8,128)(2,1)S(1)} collective-permute-done((bf16[16,3200]{1,0:T(8,128)(2,1)S(1)}, bf16[16,3200]{1,0:T(8,128)(2,1)S(1)}, u32[]{:S(2)}, u32[]{:S(2)}) %collective-permute-start.2) | collective-permute-done | bytes 102432 | tf_op jit(solution)/shard_map/ppermute | solution.py:32
  12.4 2.4 %load_weights.1 = (bf16[3072,256]{1,0:T(8,128)(2,1)S(1)}, bf16[3072,256]{1,0:T(8,128)(2,1)S(1)}, bf16[256,3072]{1,0:T(8,128)(2,1)S(1)}) custom-call(bf16[3072,256]{1,0:T(8,128)(2,1)} %bitcast.16, bf16[3072,256]{1,0:T(8,128)(2,1)} %bitcast.17, bf16[256,3072]{1,0:T(8,128)(2,1)} %bitcast.18), custom_call_target="tpu_custom_call" | custom-call | bytes 4718592 | tf_op jit(solution)/shard_map/load_weights/pallas_call | solution.py:133
  14.9 2.1 %hidden_pass.1 = (f32[32,3200]{1,0:T(8,128)S(1)}, bf16[32,3072]{1,0:T(8,128)(2,1)S(1)}, bf16[128,512]{1,0:T(8,128)(2,1)S(1)}, bf16[128,256]{1,0:T(8,128)(2,1)S(1...) custom-call(s32[1]{0:T(128)} %bitcast.index_ref, bf16[16,3200]{1,0:T(8,128)(2,1)S(1)} %get-tuple-element.33.refs_0_, ...), custom_call_target="tpu_custom_call" | custom-call | flops 1006632960 | bytes 4718592 | tf_op jit(solution)/shard_map/hidden_pass/pallas_call | solution.py:275
  16.9 0.6 %collective-permute-start.7 = (bf16[32,3072]{1,0:T(8,128)(2,1)S(1)}, bf16[32,3072]{1,0:T(8,128)(2,1)S(1)}, u32[]{:S(2)}, u32[]{:S(2)}) collective-permute-start(bf16[32,3072]{1,0:T(8,128)(2,1)S(1)} %get-tuple-element.39), channel_id=1, source_target_pairs={{0,2},{1,3},{2,0},{3,1},{4,6},{5,7},{6,4},{7,5},{8,10},{9,11},{10,... | collective-permute-start | bytes 589832 | tf_op jit(solution)/shard_map/ppermute | solution.py:32
  17.5 0.7 %collective-permute-start.12 = (f32[8,128]{1,0:T(8,128)S(1)}, f32[8,128]{1,0:T(8,128)S(1)}, u32[]{:S(2)}, u32[]{:S(2)}) collective-permute-start(f32[8,128]{1,0:T(8,128)S(1)} %get-tuple-element.47), channel_id=1, source_target_pairs={{0,4},{1,5},{2,6},{3,7},{4,0},{5,1},{6,2},{7,3},{8,12},{9,13},{10,... | collective-permute-start | bytes 12296 | tf_op jit(solution)/shard_map/ppermute | solution.py:32
  18.2 0.3 collective-permute-done.7.recv_ref
  18.6 4.1 %collective-permute-start.8 = (bf16[16,3200]{1,0:T(8,128)(2,1)S(1)}, bf16[16,3200]{1,0:T(8,128)(2,1)S(1)}, u32[]{:S(2)}, u32[]{:S(2)}) collective-permute-start(bf16[16,3200]{1,0:T(8,128)(2,1)S(1)} %get-tuple-element.40), channel_id=1, source_target_pairs={{0,28},{1,30},{2,29},{3,31},{4,24},{5,26},{6,25},{7,27},{8,4},{9,6... | collective-permute-start | bytes 307208 | tf_op jit(solution)/shard_map/ppermute | solution.py:46
  22.7 1.8 %weight_grads.3 = (bf16[3072,256]{1,0:T(8,128)(2,1)}, bf16[3072,256]{1,0:T(8,128)(2,1)}, bf16[256,3072]{1,0:T(8,128)(2,1)}) custom-call(bf16[16,3200]{1,0:T(8,128)(2,1)S(1)} %get-tuple-element.33.refs_0_, bf16[16,3200]{1,0:T(8,128)(2,1)S(1)} %collective-permute-done.refs_1_, bf16[16,3200]{1,0:T(8,128)(2,1)S(1)} %collective-permute-done.1.refs_2_, ...), custom_call_target="tpu_custom_call" | custom-call | flops 603979776 | bytes 4718592 | tf_op jit(solution)/shard_map/weight_grads/pallas_call | solution.py:352
  24.5 0.7 %collective-permute-start.13 = (f32[8,128]{1,0:T(8,128)S(1)}, f32[8,128]{1,0:T(8,128)S(1)}, u32[]{:S(2)}, u32[]{:S(2)}) collective-permute-start(f32[8,128]{1,0:T(8,128)S(1)} %add_scores.1.refs_7_), channel_id=1, source_target_pairs={{0,2},{1,3},{2,0},{3,1},{4,6},{5,7},{6,4},{7,5},{8,10},{9,11},{10,... | collective-permute-start | bytes 12296 | tf_op jit(solution)/shard_map/ppermute | solution.py:32
  25.2 0.1 weight_grads.4
  25.3 0.7 %collective-permute-start.14 = (f32[8,128]{1,0:T(8,128)S(1)}, f32[8,128]{1,0:T(8,128)S(1)}, u32[]{:S(2)}, u32[]{:S(2)}) collective-permute-start(f32[8,128]{1,0:T(8,128)S(1)} %add_scores.1.refs_7_), channel_id=1, source_target_pairs={{0,1},{1,0},{2,3},{3,2},{4,5},{5,4},{6,7},{7,6},{8,9},{9,8},{10,11... | collective-permute-start | bytes 12296 | tf_op jit(solution)/shard_map/ppermute | solution.py:32
  25.9 0.8 %collective-permute-start.15 = (f32[8,128]{1,0:T(8,128)S(1)}, f32[8,128]{1,0:T(8,128)S(1)}, u32[]{:S(2)}, u32[]{:S(2)}) collective-permute-start(f32[8,128]{1,0:T(8,128)S(1)} %add_scores.1.refs_7_), channel_id=1, source_target_pairs={{0,3},{1,2},{2,1},{3,0},{4,7},{5,6},{6,5},{7,4},{8,11},{9,10},{10,... | collective-permute-start | bytes 12296 | tf_op jit(solution)/shard_map/ppermute | solution.py:32
  26.7 2.5 %collective-permute-start.11 = (bf16[8,3072]{1,0:T(8,128)(2,1)S(1)}, bf16[8,3072]{1,0:T(8,128)(2,1)S(1)}, u32[]{:S(2)}, u32[]{:S(2)}) collective-permute-start(bf16[8,3072]{1,0:T(8,128)(2,1)S(1)} %get-tuple-element.42), channel_id=1, source_target_pairs={{0,26},{1,24},{2,27},{3,25},{4,30},{5,28},{6,31},{7,29},{8,2},{9,0... | collective-permute-start | bytes 147464 | tf_op jit(solution)/shard_map/ppermute | solution.py:46
  29.2 1.2 %collective-permute-start.9 = (bf16[8,3072]{1,0:T(8,128)(2,1)S(1)}, bf16[8,3072]{1,0:T(8,128)(2,1)S(1)}, u32[]{:S(2)}, u32[]{:S(2)}) collective-permute-start(bf16[8,3072]{1,0:T(8,128)(2,1)S(1)} %get-tuple-element.41), channel_id=1, source_target_pairs={{0,24},{1,26},{2,25},{3,27},{4,28},{5,30},{6,29},{7,31},{8,0},{9,2... | collective-permute-start | bytes 147464 | tf_op jit(solution)/shard_map/ppermute | solution.py:46
  30.5 1.3 %collective-permute-start.10 = (bf16[8,3200]{1,0:T(8,128)(2,1)S(1)}, bf16[8,3200]{1,0:T(8,128)(2,1)S(1)}, u32[]{:S(2)}, u32[]{:S(2)}) collective-permute-start(bf16[8,3200]{1,0:T(8,128)(2,1)S(1)} %lower_half.1), channel_id=1, source_target_pairs={{0,2},{1,3},{2,0},{3,1},{4,6},{5,7},{6,4},{7,5},{8,10},{9,11},{10,... | collective-permute-start | bytes 153608 | tf_op jit(solution)/shard_map/ppermute | solution.py:32
  31.8 1.9 %weight_grads.5 = (bf16[3072,256]{1,0:T(8,128)(2,1)}, bf16[3072,256]{1,0:T(8,128)(2,1)}, bf16[256,3072]{1,0:T(8,128)(2,1)}) custom-call(bf16[16,3200]{1,0:T(8,128)(2,1)S(1)} %get-tuple-element.33.refs_0_, bf16[16,3200]{1,0:T(8,128)(2,1)S(1)} %collective-permute-done.refs_1_, ...), custom_call_target="tpu_custom_call", output_to_operand_aliasing={{0}: (10, {}), {1}: (11, {}), {2}: (12, {})} | custom-call | flops 603979776 | bytes 4718592 | tf_op jit(solution)/shard_map/weight_grads/pallas_call | solution.py:352
  33.7 1.3 %spread_rows.1 = (bf16[128,3072]{1,0:T(8,128)(2,1)}, f32[6,1,128]{2,1,0:T(1,128)}) custom-call(bf16[16,3200]{1,0:T(8,128)(2,1)S(1)} %collective-permute-done.8.rows_ref.refs_0_, bf16[8,3072]{1,0:T(8,128)(2,1)S(1)} %collective-permute-done.9.refs_1_, bf16[8,3200]{1,0:T(8,128)(2,1)S(1)} %collective-permute-done.10.refs_2_, ...), custom_call_target="tpu_custom_call" | custom-call | flops 25165824 | bytes 786432 | tf_op jit(solution)/shard_map/spread_rows/pallas_call | solution.py:461
  (18 shorter events, 0.1 us)
Async XLA Ops:
  2.3 6.2 %collective-permute-start.1 = (bf16[16,3200]{1,0:T(8,128)(2,1)S(1)}, bf16[16,3200]{1,0:T(8,128)(2,1)S(1)}, u32[]{:S(2)}, u32[]{:S(2)}) collective-permute-start(bf16[16,3200]{1,0:T(8,128)(2,1)S(1)} %get-tuple-element.33.refs_0_), channel_id=1, source_target_pairs={{0,4},{1,5},{2,6},{3,7},{4,0},{5,1},{6,2},{7,3},{8,12},{9,13},{10,... | collective-permute-start | bytes 307208 | tf_op jit(solution)/shard_map/ppermute | solution.py:32
  5.3 5.8 %collective-permute-start = (bf16[16,3200]{1,0:T(8,128)(2,1)S(1)}, bf16[16,3200]{1,0:T(8,128)(2,1)S(1)}, u32[]{:S(2)}, u32[]{:S(2)}) collective-permute-start(bf16[16,3200]{1,0:T(8,128)(2,1)S(1)} %get-tuple-element.34), channel_id=1, source_target_pairs={{0,1},{1,0},{2,3},{3,2},{4,5},{5,4},{6,7},{7,6},{8,9},{9,8},{10,11... | collective-permute-start | bytes 307208 | tf_op jit(solution)/shard_map/ppermute | solution.py:32
  6.9 5.6 %collective-permute-start.2 = (bf16[16,3200]{1,0:T(8,128)(2,1)S(1)}, bf16[16,3200]{1,0:T(8,128)(2,1)S(1)}, u32[]{:S(2)}, u32[]{:S(2)}) collective-permute-start(bf16[16,3200]{1,0:T(8,128)(2,1)S(1)} %get-tuple-element.34), channel_id=1, source_target_pairs={{0,5},{1,4},{2,7},{3,6},{4,1},{5,0},{6,3},{7,2},{8,13},{9,12},{10,... | collective-permute-start | bytes 307208 | tf_op jit(solution)/shard_map/ppermute | solution.py:32
  6.9 7.9 %collective-permute-start.3 = (bf16[16,3200]{1,0:T(8,128)(2,1)S(1)}, bf16[16,3200]{1,0:T(8,128)(2,1)S(1)}, u32[]{:S(2)}, u32[]{:S(2)}) collective-permute-start(bf16[16,3200]{1,0:T(8,128)(2,1)S(1)} %get-tuple-element.33.refs_0_), channel_id=1, source_target_pairs={{0,2},{1,3},{2,0},{3,1},{4,6},{5,7},{6,4},{7,5},{8,10},{9,11},{10,... | collective-permute-start | bytes 307208 | tf_op jit(solution)/shard_map/ppermute | solution.py:32
  8.5 6.3 %collective-permute-start.5 = (bf16[16,3200]{1,0:T(8,128)(2,1)S(1)}, bf16[16,3200]{1,0:T(8,128)(2,1)S(1)}, u32[]{:S(2)}, u32[]{:S(2)}) collective-permute-start(bf16[16,3200]{1,0:T(8,128)(2,1)S(1)} %collective-permute-done.1.refs_2_), channel_id=1, source_target_pairs={{0,2},{1,3},{2,0},{3,1},{4,6},{5,7},{6,4},{7,5},{8,10},{9,11},{10,... | collective-permute-start | bytes 307208 | tf_op jit(solution)/shard_map/ppermute | solution.py:32
  11.1 3.7 %collective-permute-start.4 = (bf16[16,3200]{1,0:T(8,128)(2,1)S(1)}, bf16[16,3200]{1,0:T(8,128)(2,1)S(1)}, u32[]{:S(2)}, u32[]{:S(2)}) collective-permute-start(bf16[16,3200]{1,0:T(8,128)(2,1)S(1)} %collective-permute-done.refs_1_), channel_id=1, source_target_pairs={{0,2},{1,3},{2,0},{3,1},{4,6},{5,7},{6,4},{7,5},{8,10},{9,11},{10,... | collective-permute-start | bytes 307208 | tf_op jit(solution)/shard_map/ppermute | solution.py:32
  12.4 2.4 %collective-permute-start.6 = (bf16[16,3200]{1,0:T(8,128)(2,1)S(1)}, bf16[16,3200]{1,0:T(8,128)(2,1)S(1)}, u32[]{:S(2)}, u32[]{:S(2)}) collective-permute-start(bf16[16,3200]{1,0:T(8,128)(2,1)S(1)} %collective-permute-done.2.refs_3_), channel_id=1, source_target_pairs={{0,2},{1,3},{2,0},{3,1},{4,6},{5,7},{6,4},{7,5},{8,10},{9,11},{10,... | collective-permute-start | bytes 307208 | tf_op jit(solution)/shard_map/ppermute | solution.py:32
  16.9 1.6 %collective-permute-start.7 = (bf16[32,3072]{1,0:T(8,128)(2,1)S(1)}, bf16[32,3072]{1,0:T(8,128)(2,1)S(1)}, u32[]{:S(2)}, u32[]{:S(2)}) collective-permute-start(bf16[32,3072]{1,0:T(8,128)(2,1)S(1)} %get-tuple-element.39), channel_id=1, source_target_pairs={{0,2},{1,3},{2,0},{3,1},{4,6},{5,7},{6,4},{7,5},{8,10},{9,11},{10,... | collective-permute-start | bytes 589832 | tf_op jit(solution)/shard_map/ppermute | solution.py:32
  17.5 7.0 %collective-permute-start.12 = (f32[8,128]{1,0:T(8,128)S(1)}, f32[8,128]{1,0:T(8,128)S(1)}, u32[]{:S(2)}, u32[]{:S(2)}) collective-permute-start(f32[8,128]{1,0:T(8,128)S(1)} %get-tuple-element.47), channel_id=1, source_target_pairs={{0,4},{1,5},{2,6},{3,7},{4,0},{5,1},{6,2},{7,3},{8,12},{9,13},{10,... | collective-permute-start | bytes 12296 | tf_op jit(solution)/shard_map/ppermute | solution.py:32
  18.6 10.6 %collective-permute-start.8 = (bf16[16,3200]{1,0:T(8,128)(2,1)S(1)}, bf16[16,3200]{1,0:T(8,128)(2,1)S(1)}, u32[]{:S(2)}, u32[]{:S(2)}) collective-permute-start(bf16[16,3200]{1,0:T(8,128)(2,1)S(1)} %get-tuple-element.40), channel_id=1, source_target_pairs={{0,28},{1,30},{2,29},{3,31},{4,24},{5,26},{6,25},{7,27},{8,4},{9,6... | collective-permute-start | bytes 307208 | tf_op jit(solution)/shard_map/ppermute | solution.py:46
  24.5 6.0 %collective-permute-start.13 = (f32[8,128]{1,0:T(8,128)S(1)}, f32[8,128]{1,0:T(8,128)S(1)}, u32[]{:S(2)}, u32[]{:S(2)}) collective-permute-start(f32[8,128]{1,0:T(8,128)S(1)} %add_scores.1.refs_7_), channel_id=1, source_target_pairs={{0,2},{1,3},{2,0},{3,1},{4,6},{5,7},{6,4},{7,5},{8,10},{9,11},{10,... | collective-permute-start | bytes 12296 | tf_op jit(solution)/shard_map/ppermute | solution.py:32
  25.3 8.4 %collective-permute-start.14 = (f32[8,128]{1,0:T(8,128)S(1)}, f32[8,128]{1,0:T(8,128)S(1)}, u32[]{:S(2)}, u32[]{:S(2)}) collective-permute-start(f32[8,128]{1,0:T(8,128)S(1)} %add_scores.1.refs_7_), channel_id=1, source_target_pairs={{0,1},{1,0},{2,3},{3,2},{4,5},{5,4},{6,7},{7,6},{8,9},{9,8},{10,11... | collective-permute-start | bytes 12296 | tf_op jit(solution)/shard_map/ppermute | solution.py:32
  25.9 7.8 %collective-permute-start.15 = (f32[8,128]{1,0:T(8,128)S(1)}, f32[8,128]{1,0:T(8,128)S(1)}, u32[]{:S(2)}, u32[]{:S(2)}) collective-permute-start(f32[8,128]{1,0:T(8,128)S(1)} %add_scores.1.refs_7_), channel_id=1, source_target_pairs={{0,3},{1,2},{2,1},{3,0},{4,7},{5,6},{6,5},{7,4},{8,11},{9,10},{10,... | collective-permute-start | bytes 12296 | tf_op jit(solution)/shard_map/ppermute | solution.py:32
  26.7 7.0 %collective-permute-start.11 = (bf16[8,3072]{1,0:T(8,128)(2,1)S(1)}, bf16[8,3072]{1,0:T(8,128)(2,1)S(1)}, u32[]{:S(2)}, u32[]{:S(2)}) collective-permute-start(bf16[8,3072]{1,0:T(8,128)(2,1)S(1)} %get-tuple-element.42), channel_id=1, source_target_pairs={{0,26},{1,24},{2,27},{3,25},{4,30},{5,28},{6,31},{7,29},{8,2},{9,0... | collective-permute-start | bytes 147464 | tf_op jit(solution)/shard_map/ppermute | solution.py:46
  29.2 4.5 %collective-permute-start.9 = (bf16[8,3072]{1,0:T(8,128)(2,1)S(1)}, bf16[8,3072]{1,0:T(8,128)(2,1)S(1)}, u32[]{:S(2)}, u32[]{:S(2)}) collective-permute-start(bf16[8,3072]{1,0:T(8,128)(2,1)S(1)} %get-tuple-element.41), channel_id=1, source_target_pairs={{0,24},{1,26},{2,25},{3,27},{4,28},{5,30},{6,29},{7,31},{8,0},{9,2... | collective-permute-start | bytes 147464 | tf_op jit(solution)/shard_map/ppermute | solution.py:46
  30.5 3.2 %collective-permute-start.10 = (bf16[8,3200]{1,0:T(8,128)(2,1)S(1)}, bf16[8,3200]{1,0:T(8,128)(2,1)S(1)}, u32[]{:S(2)}, u32[]{:S(2)}) collective-permute-start(bf16[8,3200]{1,0:T(8,128)(2,1)S(1)} %lower_half.1), channel_id=1, source_target_pairs={{0,2},{1,3},{2,0},{3,1},{4,6},{5,7},{6,4},{7,5},{8,10},{9,11},{10,... | collective-permute-start | bytes 153608 | tf_op jit(solution)/shard_map/ppermute | solution.py:32
